TPU v7x, 32 devices: a whole 2x2x4 slice. The times are simulated.
32 devices in a mesh: ctx: 16 (over z, x, core), ch: 2 (over y).
Axes of the slice: x: 2, y: 2, z: 4, core: 2. Of those that a mesh axis runs over, the one named last changes fastest.
Arguments:
- query: bfloat16 [4096, 2048], P('ch', 'ctx'), may hold values from -6 to 6
- key_in: bfloat16 [4096, 2048], P('ch', 'ctx'), may hold values from -6 to 6
- value_in: bfloat16 [4096, 2048], P('ch', 'ctx'), may hold values from -6 to 6
- grad_out: bfloat16 [4096, 2048], P('ch', 'ctx'), may hold values from -6 to 6
- med_filter: bfloat16 [256, 512], P('ch'), may hold values from -0.25 to 0.25
- residues: float32 [16, 256], P(None, 'ch'), may hold values from -4 to 4
- pole_rate: float32 [16, 256], P(None, 'ch'), may hold values from 0.05 to 400
Outputs:
- grad_query: bfloat16 [4096, 2048], P('ch', 'ctx')
- grad_key: bfloat16 [4096, 2048], P('ch', 'ctx')
- grad_value: bfloat16 [4096, 2048], P('ch', 'ctx')
- grad_med: float32 [256, 512], P('ch')
- grad_res: float32 [16, 256], P(None, 'ch')
All inputs are finite; a program needn't handle non-finite values.
Results may differ from a plain program's by a relative error of at most 0.0055.
Values may be sent and summed in bfloat16 or wider, within the bound.
No kernel may reach another device: no remote copies, remote signals or barrier semaphores. Data moves between devices by JAX's collectives and lax.ppermute only.
A program may use at most 128 MiB of HBM per device.

v0:
```python
import functools
import math

import jax
import jax.numpy as jnp
from jax import lax
from jax.experimental import pallas as pl
from jax.experimental.pallas import tpu as pltpu
from jax.sharding import PartitionSpec as P

GROUP = 16
BLK = 128
SPAN = 4
STEP = 8
WIDE = (SPAN + 1) * BLK
F32 = jnp.float32
BF16 = jnp.bfloat16
NT = (((1,), (1,)), ((), ()))
TN = (((0,), (0,)), ((), ()))
NN = (((1,), (0,)), ((), ()))


def mm(left, right, dims=NN):
    return lax.dot_general(left, right, dims, preferred_element_type=F32)


def halves(value):
    high = value.astype(BF16)
    return high, (value - high.astype(F32)).astype(BF16)


def lanes_of(rows):
    return lax.broadcasted_iota(jnp.int32, (rows, BLK), 1)


def table_kernel(rate_ref, gain_ref, med_ref, table_ref):
    lane = lanes_of(GROUP).astype(F32)
    for g in range(STEP):
        rate = rate_ref[g]
        gain = gain_ref[g]
        pieces = [jnp.zeros((1, BLK), F32)]
        for o in range(SPAN + 1):
            tail = jnp.sum(gain * jnp.exp(-rate * (lane + float(o * BLK))), axis=0, keepdims=True)
            if o < SPAN:
                tail = tail + med_ref[g : g + 1, o * BLK : (o + 1) * BLK].astype(F32)
            pieces.append(tail)
        taps = jnp.broadcast_to(jnp.concatenate(pieces, axis=1), (GROUP, WIDE + BLK))
        skewed = pltpu.roll(taps, 0, 1, stride=1, stride_axis=0)
        for i in range(BLK // GROUP):
            moved = skewed if i == 0 else pltpu.roll(skewed, GROUP * i, 1)
            table_ref[g, GROUP * i : GROUP * (i + 1), :] = moved[:, BLK:].astype(BF16)


def state_kernel(q_ref, rate_ref, p0, p1, p2, p3, end_ref, head_ref, both):
    q = q_ref[0]
    lane = lanes_of(GROUP)
    tok = lane.astype(F32)
    for m, piece in enumerate((p0, p1, p2, p3)):
        both[q ^ m] = piece[...]
    ends = jnp.zeros((GROUP, BLK), F32)
    heads = jnp.zeros((GROUP, BLK), F32)
    for g in range(STEP):
        rate = rate_ref[g]
        rows = slice(GROUP * g, GROUP * (g + 1))
        own = jnp.concatenate(
            [both[s, 0, rows, :] for s in range(SPAN)] + [both[s, 1, rows, :] for s in range(SPAN)],
            axis=0,
        )
        fin = halves(jnp.exp(-rate * (BLK - 1.0 - tok)))
        ini = halves(jnp.exp(-rate * (tok + 1.0)))
        state = mm(jnp.concatenate(fin + ini, axis=0), own, NT)
        end = state[0:16] + state[16:32]
        head = state[32:48] + state[48:64]
        block = (lane // GROUP).astype(F32)
        end = jnp.where(lane < 64, end * jnp.exp(-rate * (BLK * (SPAN - 1.0 - block))), 0.0)
        head = jnp.where(lane >= 64, head * jnp.exp(-rate * (BLK * (block - SPAN))), 0.0)
        for value, is_end in ((end, True), (head, False)):
            value = value + pltpu.roll(value, 64, 1)
            value = value + pltpu.roll(value, 32, 1)
            value = value + pltpu.roll(value, 16, 1)
            if is_end:
                ends = jnp.where(lane // GROUP == g, value, ends)
            else:
                heads = jnp.where(lane // GROUP == g, value, heads)
    end_ref[0] = ends
    head_ref[0] = heads


def roll_left(value, amount):
    width = value.shape[1]
    return value if amount % width == 0 else pltpu.roll(value, width - amount, 1)


def main_kernel(
    q_ref, rate_ref, gain_ref, table_ref, before_ref, after_ref,
    p0, p1, p2, p3, xa, xb, ga, gb,
    o0, o1, o2, o3, lag_ref, res_ref, xs, gs, fs, bs,
):
    q = q_ref[0]
    lane = lanes_of(GROUP)
    tok = lane.astype(F32)
    block = lane // GROUP
    for m, piece in enumerate((p0, p1, p2, p3)):
        xs[SPAN + (q ^ m)] = piece[0]
        gs[q ^ m] = piece[1]
    for m, (x_part, g_part) in enumerate(((xa, ga), (xa, ga), (xb, gb), (xb, gb))):
        xs[q ^ m] = x_part[m % 2]
        gs[SPAN + (q ^ m)] = g_part[m % 2]
    row_at = lax.broadcasted_iota(jnp.int32, (BLK, BLK), 0)
    col_at = lax.broadcasted_iota(jnp.int32, (BLK, BLK), 1)
    causal = col_at >= row_at
    sub_at = lax.broadcasted_iota(jnp.int32, (8, WIDE), 0)
    lag_rows = []
    for g in range(STEP):
        rate = rate_ref[g]
        gain = gain_ref[g]
        rows = slice(GROUP * g, GROUP * (g + 1))
        x = [xs[j, rows, :] for j in range(2 * SPAN)]
        y = [gs[j, rows, :] for j in range(2 * SPAN)]
        fin = jnp.exp(-rate * (BLK - 1.0 - tok))
        ini = jnp.exp(-rate * (tok + 1.0))
        end = mm(jnp.concatenate(halves(fin), axis=0), jnp.concatenate(x, axis=0), NT)
        end = end[0:16] + end[16:32]
        head = mm(jnp.concatenate(halves(ini), axis=0), jnp.concatenate(y, axis=0), NT)
        head = head[0:16] + head[16:32]

        def spread(ref):
            start = jnp.where(lane < GROUP, roll_left(ref[0], GROUP * g), 0.0)
            start = start + pltpu.roll(start, 16, 1)
            return start + pltpu.roll(start, 32, 1)

        decay = [jnp.exp(-rate * float(BLK * k)) for k in range(SPAN)]
        near = block.astype(F32)
        carried = spread(before_ref) * jnp.exp(-rate * (BLK * near))
        returned = spread(after_ref) * jnp.exp(-rate * (BLK * (SPAN - 1.0 - near)))
        for k in range(SPAN - 1):
            moved = pltpu.roll(end, GROUP * (k + 1), 1)
            moved = jnp.where(lane >= GROUP * (k + 1), moved, 0.0)
            carried = carried + (moved if k == 0 else moved * decay[k])
            moved = pltpu.roll(head, GROUP * (SPAN - 1 - k), 1)
            moved = jnp.where(lane < GROUP * (SPAN - 1 - k), moved, 0.0)
            returned = returned + (moved if k == 0 else moved * decay[k])
        skip = jnp.exp(-rate * float(SPAN * BLK))
        cross = jnp.where(lane < 64, pltpu.roll(end, 64, 1) * returned * skip, 0.0)
        out_f = halves(gain * ini * skip)
        out_b = halves(gain * fin * skip)
        car = halves(carried[:, :64])
        ret = halves(returned[:, :64])
        far_f = mm(
            jnp.concatenate((car[0], car[1], car[0]), axis=0),
            jnp.concatenate((out_f[0], out_f[0], out_f[1]), axis=0),
            TN,
        )
        far_b = mm(
            jnp.concatenate((ret[0], ret[1], ret[0]), axis=0),
            jnp.concatenate((out_b[0], out_b[0], out_b[1]), axis=0),
            TN,
        )
        wide_x = jnp.concatenate(
            [jnp.concatenate(x[SPAN - o : 2 * SPAN - o], axis=0) for o in range(SPAN + 1)], axis=1
        )
        wide_y = jnp.concatenate(
            [jnp.concatenate(y[o : o + SPAN], axis=0) for o in range(SPAN + 1)], axis=1
        )
        table = table_ref[g]
        tall = jnp.concatenate(
            [table[:, o * BLK : (o + 1) * BLK] for o in range(SPAN + 1)], axis=0
        )
        forward = mm(wide_x, tall) + far_f
        backward = mm(wide_y, table, NT) + far_b
        for i in range(SPAN):
            fs[i, rows, :] = forward[GROUP * i : GROUP * (i + 1)].astype(BF16)
            bs[i, rows, :] = backward[GROUP * i : GROUP * (i + 1)].astype(BF16)
        own_x = jnp.concatenate(x[SPAN:], axis=0)
        pairs = mm(own_x, wide_y, TN)
        pairs = jnp.concatenate((jnp.where(causal, pairs[:, :BLK], 0.0), pairs[:, BLK:]), axis=1)
        total = pairs[0:8]
        for i in range(1, BLK // 8):
            total = total + roll_left(pairs[8 * i : 8 * (i + 1)], 8 * i)
        for bit in (1, 2, 4):
            total = jnp.where((sub_at & bit) != 0, roll_left(total, bit), total)
        lags = jnp.sum(total, axis=0, keepdims=True)
        lag_rows.append(lags)
        for o in range(SPAN + 1):
            cross = cross + lags[:, o * BLK : (o + 1) * BLK] * jnp.exp(
                -rate * (tok + float(o * BLK))
            )
        res_ref[g] = cross
    lag_ref[...] = jnp.concatenate(lag_rows, axis=0)
    for m, out in enumerate((o0, o1, o2, o3)):
        out[0] = fs[q ^ m]
        out[1] = bs[q ^ m]


def gate_kernel(q_ref, p0, p1, p2, p3, go_ref, v_ref, k_ref, gq_ref, gk_ref, gv_ref):
    q = q_ref[0]
    sub = p0.shape[1]
    for m, piece in enumerate((p0, p1, p2, p3)):
        at = pl.ds(pl.multiple_of((q ^ m) * sub, sub), sub)
        gq_ref[at, :] = (go_ref[at, :].astype(F32) * piece[0].astype(F32)).astype(BF16)
        grad = piece[1].astype(F32)
        gk_ref[at, :] = (grad * v_ref[at, :].astype(F32)).astype(BF16)
        gv_ref[at, :] = (grad * k_ref[at, :].astype(F32)).astype(BF16)


def body(query, key_in, value_in, grad_out, med_filter, residues, pole_rate):
    channels, length = query.shape
    groups = channels // GROUP
    devices = lax.axis_size("ctx")
    seq_total = length * devices
    ranks = SPAN
    units = devices // ranks
    sub = channels // ranks
    local = groups // ranks
    index = lax.axis_index("ctx")
    q = lax.rem(index, ranks).astype(jnp.int32)
    q_arr = q.reshape(1)

    def swap(value, m):
        return lax.ppermute(value, "ctx", [(i, i ^ m) for i in range(devices)])

    def shift(value, by):
        by = by * ranks
        return lax.ppermute(
            value, "ctx", [(i, i + by) for i in range(devices) if 0 <= i + by < devices]
        )

    def part(m):
        def cut(array):
            return lax.dynamic_slice_in_dim(array, (q ^ m) * sub, sub, 0).astype(F32)

        return jnp.stack(
            [
                (cut(key_in) * cut(value_in)).astype(BF16),
                (cut(grad_out) * cut(query)).astype(BF16),
            ]
        )

    pieces = [part(0)] + [swap(part(m), m) for m in range(1, ranks)]

    x_near = shift(jnp.stack([pieces[0][0], pieces[1][0]]), 1)
    y_near = shift(jnp.stack([pieces[0][1], pieces[1][1]]), -1)
    x_far = shift(jnp.stack([pieces[2][0], pieces[3][0]]), 1)
    y_far = shift(jnp.stack([pieces[2][1], pieces[3][1]]), -1)

    rate = lax.dynamic_slice_in_dim(pole_rate, q * local, local, 1).T / seq_total
    res = lax.dynamic_slice_in_dim(residues, q * local, local, 1).T
    med = lax.dynamic_slice_in_dim(med_filter, q * local, local, 0)
    root = jnp.sqrt(-jnp.expm1(-2.0 * rate))
    rate_wide = jnp.broadcast_to(rate[:, :, None], (local, GROUP, BLK))
    gain_wide = jnp.broadcast_to((res * root)[:, :, None], (local, GROUP, BLK))

    steps = local // STEP
    smem = pl.BlockSpec(memory_space=pltpu.SMEM)
    per_group = pl.BlockSpec((STEP, GROUP, BLK), lambda i: (i, 0, 0))
    packed = pl.BlockSpec((1, GROUP, BLK), lambda i: (i, 0, 0))
    rows = STEP * GROUP
    pair = pl.BlockSpec((2, rows, BLK), lambda i: (0, i, 0))
    params = pltpu.CompilerParams(vmem_limit_bytes=40 << 20)

    table = pl.pallas_call(
        table_kernel,
        grid=(steps,),
        in_specs=[per_group, per_group, pl.BlockSpec((STEP, SPAN * BLK), lambda i: (i, 0))],
        out_specs=pl.BlockSpec((STEP, BLK, WIDE), lambda i: (i, 0, 0)),
        out_shape=jax.ShapeDtypeStruct((local, BLK, WIDE), BF16),
        compiler_params=params,
        name="tables",
    )(rate_wide, gain_wide, med)

    ends, heads = pl.pallas_call(
        state_kernel,
        grid=(steps,),
        in_specs=[smem, per_group] + [pair] * 4,
        out_specs=[packed] * 2,
        out_shape=[jax.ShapeDtypeStruct((steps, GROUP, BLK), F32)] * 2,
        scratch_shapes=[pltpu.VMEM((SPAN, 2, rows, BLK), BF16)],
        compiler_params=params,
        name="states",
    )(q_arr, rate_wide, *pieces)

    rate_packed = jnp.repeat(
        jnp.transpose(rate.reshape(steps, STEP, GROUP), (0, 2, 1)), GROUP, axis=2
    )
    reach = 1
    while reach < units - 2:
        fade = jnp.exp(-rate_packed * float(reach * ranks * length))
        ends, heads = ends + fade * shift(ends, reach), heads + fade * shift(heads, -reach)
        reach *= 2
    before = shift(ends, 2)
    after = shift(heads, -2)

    outs = pl.pallas_call(
        main_kernel,
        grid=(steps,),
        in_specs=[
            smem,
            per_group,
            per_group,
            pl.BlockSpec((STEP, BLK, WIDE), lambda i: (i, 0, 0)),
            packed,
            packed,
        ]
        + [pair] * 8,
        out_specs=[pair] * 4 + [pl.BlockSpec((STEP, WIDE), lambda i: (i, 0)), per_group],
        out_shape=[jax.ShapeDtypeStruct((2, sub, BLK), BF16)] * 4
        + [
            jax.ShapeDtypeStruct((local, WIDE), F32),
            jax.ShapeDtypeStruct((local, GROUP, BLK), F32),
        ],
        scratch_shapes=[pltpu.VMEM((2 * SPAN, rows, BLK), BF16)] * 2
        + [pltpu.VMEM((SPAN, rows, BLK), BF16)] * 2,
        compiler_params=params,
        name="convs",
    )(q_arr, rate_wide, gain_wide, table, before, after, *pieces, x_near, x_far, y_near, y_far)

    back = [outs[0]] + [swap(outs[m], m) for m in range(1, ranks)]
    whole = pl.BlockSpec(memory_space=pltpu.VMEM)
    grads = pl.pallas_call(
        gate_kernel,
        in_specs=[smem] + [whole] * 7,
        out_specs=[whole] * 3,
        out_shape=[jax.ShapeDtypeStruct((channels, length), BF16)] * 3,
        compiler_params=params,
        name="gates",
    )(q_arr, *back, grad_out, value_in, key_in)

    scaling = 1.0 / math.sqrt(GROUP * seq_total)
    terms = jnp.sum(outs[5], axis=2) * root
    sums = jnp.concatenate([outs[4][:, : SPAN * BLK], terms], axis=1) * scaling
    hop = 1
    while hop < units:
        sums = sums + swap(sums, hop * ranks)
        hop *= 2
    gathered = jnp.zeros((groups, sums.shape[1]), F32)
    for m in range(ranks):
        got = sums if m == 0 else swap(sums, m)
        gathered = lax.dynamic_update_slice_in_dim(gathered, got, (q ^ m) * local, 0)
    return (
        grads[0],
        grads[1],
        grads[2],
        gathered[:, : SPAN * BLK],
        gathered[:, SPAN * BLK :].T,
    )


def solution(mesh):
    in_specs = (
        P("ch", "ctx"),
        P("ch", "ctx"),
        P("ch", "ctx"),
        P("ch", "ctx"),
        P("ch", None),
        P(None, "ch"),
        P(None, "ch"),
    )
    out_specs = (P("ch", "ctx"), P("ch", "ctx"), P("ch", "ctx"), P("ch", None), P(None, "ch"))
    return jax.shard_map(body, mesh=mesh, in_specs=in_specs, out_specs=out_specs, check_vma=False)
```

profile of v0, /device:TPU:0, one launch (start us, length us, event | category | flops | bytes accessed | tf_op | source)
XLA Modules:
  0.0 108.5 jit_solution(4987896871486549080)
XLA Ops:
  0.7 1.9 %fusion.6 = (bf16[1,512,128]{2,1,0:T(8,128)(2,1)S(1)}, bf16[1,512,128]{2,1,0:T(8,128)(2,1)S(1)}, bf16[1,512,128]{2,1,0:T(8,128)(2,1)S(1)}, bf16[1,512,128]{2,1,0...) fusion(bf16[2048,128]{1,0:T(8,128)(2,1)} %v_ref.1, ...), kind=kLoop, calls=%fused_computation.22 | loop fusion | flops 2097152 | bytes 3145744 | tf_op jit(solution)/shard_map/stack | solution.py:232
  2.6 0.5 collective-permute-start
  3.2 2.6 %collective-permute-start.1 = (bf16[2,512,128]{2,1,0:T(8,128)(2,1)S(1)}, bf16[2,512,128]{2,1,0:T(8,128)(2,1)S(1)}, u32[]{:S(2)}, u32[]{:S(2)}) collective-permute-start(bf16[2,512,128]{2,1,0:T(8,128)(2,1)S(1)} %pad_maximum_fusion.3), channel_id=1, source_target_pairs={{0,4},{2,6},{4,0},{6,2},{8,12},{10,14},{12,8},{14,10},{16,20},{18,... | collective-permute-start | bytes 786440 | tf_op jit(solution)/shard_map/ppermute | solution.py:220
  5.8 0.2 collective-permute-start.2
  5.9 0.8 constant_dynamic-slice_fusion.2
  6.8 0.8 constant_dynamic-slice_fusion.1
  7.7 0.1 broadcast_in_dim.20
  7.9 0.1 exp.12
  8.1 4.8 %collective-permute-done.1.p2 = bf16[2,512,128]{2,1,0:T(8,128)(2,1)S(1)} collective-permute-done((bf16[2,512,128]{2,1,0:T(8,128)(2,1)S(1)}, bf16[2,512,128]{2,1,0:T(8,128)(2,1)S(1)}, u32[]{:S(2)}, u32[]{:S(2)}) %collective-permute-start.1) | collective-permute-done | bytes 262176 | tf_op jit(solution)/shard_map/ppermute | solution.py:220
  12.9 5.2 %collective-permute-done.2.p3 = bf16[2,512,128]{2,1,0:T(8,128)(2,1)S(1)} collective-permute-done((bf16[2,512,128]{2,1,0:T(8,128)(2,1)S(1)}, bf16[2,512,128]{2,1,0:T(8,128)(2,1)S(1)}, u32[]{:S(2)}, u32[]{:S(2)}) %collective-permute-start.2) | collective-permute-done | bytes 262176 | tf_op jit(solution)/shard_map/ppermute | solution.py:220
  18.2 2.2 %states.1 = (f32[4,16,128]{2,1,0:T(8,128)S(1)}, f32[4,16,128]{2,1,0:T(8,128)S(1)}) custom-call(s32[1]{0:T(128)} %bitcast.q_ref, f32[32,16,128]{2,1,0:T(8,128)S(1)} %broadcast_in_dim.8.rate_ref, bf16[2,512,128]{2,1,0:T(8,128)(2,1)S(1)} %get-tuple-element.47.p0, bf16[2,512,128]{2,1,0:T(8,128)(2,1)S(1)} %collective-permute-done.p1, ...), custom_call_target="tpu_custom_call" | custom-call | tf_op jit(solution)/shard_map/states/pallas_call | solution.py:271
  20.4 3.5 %collective-permute-start.3 = (f32[4,16,128]{2,1,0:T(8,128)S(1)}, f32[4,16,128]{2,1,0:T(8,128)S(1)}, u32[]{:S(2)}, u32[]{:S(2)}) collective-permute-start(f32[4,16,128]{2,1,0:T(8,128)S(1)} %get-tuple-element.16), channel_id=1, source_target_pairs={{0,8},{2,10},{4,12},{6,14},{8,16},{10,18},{12,20},{14,22},{16,24},... | collective-permute-start | bytes 98312 | tf_op jit(solution)/shard_map/ppermute | solution.py:224
  24.0 1.3 %collective-permute-start.5 = (f32[4,16,128]{2,1,0:T(8,128)S(1)}, f32[4,16,128]{2,1,0:T(8,128)S(1)}, u32[]{:S(2)}, u32[]{:S(2)}) collective-permute-start(f32[4,16,128]{2,1,0:T(8,128)S(1)} %get-tuple-element.17), channel_id=1, source_target_pairs={{8,0},{10,2},{12,4},{14,6},{16,8},{18,10},{20,12},{22,14},{24,16},... | collective-permute-start | bytes 98312 | tf_op jit(solution)/shard_map/ppermute | solution.py:224
  25.3 4.6 %collective-permute-start.7 = (bf16[2,512,128]{2,1,0:T(8,128)(2,1)S(1)}, bf16[2,512,128]{2,1,0:T(8,128)(2,1)S(1)}, u32[]{:S(2)}, u32[]{:S(2)}) collective-permute-start(bf16[2,512,128]{2,1,0:T(8,128)(2,1)S(1)} %get-tuple-element.48), channel_id=1, source_target_pairs={{0,8},{2,10},{4,12},{6,14},{8,16},{10,18},{12,20},{14,22},{16,24},... | collective-permute-start | bytes 786440 | tf_op jit(solution)/shard_map/ppermute | solution.py:224
  29.9 1.3 %collective-permute-start.9 = (bf16[2,512,128]{2,1,0:T(8,128)(2,1)S(1)}, bf16[2,512,128]{2,1,0:T(8,128)(2,1)S(1)}, u32[]{:S(2)}, u32[]{:S(2)}) collective-permute-start(bf16[2,512,128]{2,1,0:T(8,128)(2,1)S(1)} %get-tuple-element.46), channel_id=1, source_target_pairs={{8,0},{10,2},{12,4},{14,6},{16,8},{18,10},{20,12},{22,14},{24,16},... | collective-permute-start | bytes 786440 | tf_op jit(solution)/shard_map/ppermute | solution.py:224
  31.2 1.3 %collective-permute-start.10 = (bf16[2,512,128]{2,1,0:T(8,128)(2,1)S(1)}, bf16[2,512,128]{2,1,0:T(8,128)(2,1)S(1)}, u32[]{:S(2)}, u32[]{:S(2)}) collective-permute-start(bf16[2,512,128]{2,1,0:T(8,128)(2,1)S(1)} %pad_maximum_fusion.7), channel_id=1, source_target_pairs={{8,0},{10,2},{12,4},{14,6},{16,8},{18,10},{20,12},{22,14},{24,16},... | collective-permute-start | bytes 786440 | tf_op jit(solution)/shard_map/ppermute | solution.py:224
  32.6 5.2 %collective-permute-start.8 = (bf16[2,512,128]{2,1,0:T(8,128)(2,1)S(1)}, bf16[2,512,128]{2,1,0:T(8,128)(2,1)S(1)}, u32[]{:S(2)}, u32[]{:S(2)}) collective-permute-start(bf16[2,512,128]{2,1,0:T(8,128)(2,1)S(1)} %pad_maximum_fusion.5), channel_id=1, source_target_pairs={{0,8},{2,10},{4,12},{6,14},{8,16},{10,18},{12,20},{14,22},{16,24},... | collective-permute-start | bytes 786440 | tf_op jit(solution)/shard_map/ppermute | solution.py:224
  37.8 4.9 %collective-permute-start.4 = (f32[4,16,128]{2,1,0:T(8,128)S(1)}, f32[4,16,128]{2,1,0:T(8,128)S(1)}, u32[]{:S(2)}, u32[]{:S(2)}) collective-permute-start(f32[4,16,128]{2,1,0:T(8,128)S(1)} %get-tuple-element.50), channel_id=1, source_target_pairs={{0,16},{2,18},{4,20},{6,22},{8,24},{10,26},{12,28},{14,30},{1,17},... | collective-permute-start | bytes 98312 | tf_op jit(solution)/shard_map/ppermute | solution.py:224
  42.8 1.6 %collective-permute-done.4.before_ref = f32[4,16,128]{2,1,0:T(8,128)S(1)} collective-permute-done((f32[4,16,128]{2,1,0:T(8,128)S(1)}, f32[4,16,128]{2,1,0:T(8,128)S(1)}, u32[]{:S(2)}, u32[]{:S(2)}) %collective-permute-start.4) | collective-permute-done | bytes 32800 | tf_op jit(solution)/shard_map/ppermute | solution.py:224
  44.3 1.3 %collective-permute-start.6 = (f32[4,16,128]{2,1,0:T(8,128)S(1)}, f32[4,16,128]{2,1,0:T(8,128)S(1)}, u32[]{:S(2)}, u32[]{:S(2)}) collective-permute-start(f32[4,16,128]{2,1,0:T(8,128)S(1)} %get-tuple-element.49), channel_id=1, source_target_pairs={{16,0},{18,2},{20,4},{22,6},{24,8},{26,10},{28,12},{30,14},{17,1},... | collective-permute-start | bytes 98312 | tf_op jit(solution)/shard_map/ppermute | solution.py:224
  45.6 0.1 broadcast_in_dim.9.gain_ref
  45.8 3.9 %tables.1.table_ref = bf16[32,128,640]{2,1,0:T(8,128)(2,1)S(1)} custom-call(f32[32,16,128]{2,1,0:T(8,128)S(1)} %broadcast_in_dim.8.rate_ref, f32[32,16,128]{2,1,0:T(8,128)S(1)} %broadcast_in_dim.9.gain_ref, bf16[32,512]{1,0:T(8,128)(2,1)S(1)} %constant_dynamic-slice_fusion.med_ref), custom_call_target="tpu_custom_call" | custom-call | tf_op jit(solution)/shard_map/tables/pallas_call | solution.py:261
  49.7 1.3 %collective-permute-done.6.after_ref = f32[4,16,128]{2,1,0:T(8,128)S(1)} collective-permute-done((f32[4,16,128]{2,1,0:T(8,128)S(1)}, f32[4,16,128]{2,1,0:T(8,128)S(1)}, u32[]{:S(2)}, u32[]{:S(2)}) %collective-permute-start.6) | collective-permute-done | bytes 32800 | tf_op jit(solution)/shard_map/ppermute | solution.py:224
  51.1 20.7 %convs.1 = (bf16[2,512,128]{2,1,0:T(8,128)(2,1)S(1)}, bf16[2,512,128]{2,1,0:T(8,128)(2,1)S(1)}, bf16[2,512,128]{2,1,0:T(8,128)(2,1)S(1)}, bf16[2,512,128]{2,1,0:...) custom-call(s32[1]{0:T(128)} %bitcast.q_ref, f32[32,16,128]{2,1,0:T(8,128)S(1)} %broadcast_in_dim.8.rate_ref, ...), custom_call_target="tpu_custom_call" | custom-call | tf_op jit(solution)/shard_map/convs/pallas_call | solution.py:293
  71.8 0.7 copy-done.4
  72.5 0.1 reduce_sum.9
  72.7 1.2 %collective-permute-start.14 = (f32[32,528]{1,0:T(8,128)S(1)}, f32[32,528]{1,0:T(8,128)S(1)}, u32[]{:S(2)}, u32[]{:S(2)}) collective-permute-start(f32[32,528]{1,0:T(8,128)S(1)} %maximum_multiply_fusion), channel_id=1, source_target_pairs={{0,8},{2,10},{4,12},{6,14},{8,0},{10,2},{12,4},{14,6},{16,24},{18,... | collective-permute-start | bytes 202760 | tf_op jit(solution)/shard_map/ppermute | solution.py:220
  73.9 3.5 %collective-permute-done.14 = f32[32,528]{1,0:T(8,128)S(1)} collective-permute-done((f32[32,528]{1,0:T(8,128)S(1)}, f32[32,528]{1,0:T(8,128)S(1)}, u32[]{:S(2)}, u32[]{:S(2)}) %collective-permute-start.14) | collective-permute-done | bytes 67616 | tf_op jit(solution)/shard_map/ppermute | solution.py:220
  77.4 2.1 %collective-permute-start.15 = (f32[32,528]{1,0:T(8,128)S(1)}, f32[32,528]{1,0:T(8,128)S(1)}, u32[]{:S(2)}, u32[]{:S(2)}) collective-permute-start(f32[32,528]{1,0:T(8,128)S(1)} %fusion.8), channel_id=1, source_target_pairs={{0,16},{2,18},{4,20},{6,22},{8,24},{10,26},{12,28},{14,30},{16,0},... | collective-permute-start | bytes 202760 | tf_op jit(solution)/shard_map/ppermute | solution.py:220
  79.5 4.2 %collective-permute-done.15 = f32[32,528]{1,0:T(8,128)S(1)} collective-permute-done((f32[32,528]{1,0:T(8,128)S(1)}, f32[32,528]{1,0:T(8,128)S(1)}, u32[]{:S(2)}, u32[]{:S(2)}) %collective-permute-start.15) | collective-permute-done | bytes 67616 | tf_op jit(solution)/shard_map/ppermute | solution.py:220
  83.7 0.6 add.59
  84.4 1.5 %collective-permute-start.17 = (f32[32,528]{1,0:T(8,128)}, f32[32,528]{1,0:T(8,128)}, u32[]{:S(2)}, u32[]{:S(2)}) collective-permute-start(f32[32,528]{1,0:T(8,128)} %add.59), channel_id=1, source_target_pairs={{0,4},{2,6},{4,0},{6,2},{8,12},{10,14},{12,8},{14,10},{16,20},{18,... | collective-permute-start | bytes 202760 | tf_op jit(solution)/shard_map/ppermute | solution.py:220
  85.8 0.4 collective-permute-start.18
  86.2 0.3 collective-permute-start.11
  86.5 1.5 %collective-permute-start.12 = (bf16[2,512,128]{2,1,0:T(8,128)(2,1)S(1)}, bf16[2,512,128]{2,1,0:T(8,128)(2,1)S(1)}, u32[]{:S(2)}, u32[]{:S(2)}) collective-permute-start(bf16[2,512,128]{2,1,0:T(8,128)(2,1)S(1)} %get-tuple-element.20), channel_id=1, source_target_pairs={{0,4},{2,6},{4,0},{6,2},{8,12},{10,14},{12,8},{14,10},{16,20},{18,... | collective-permute-start | bytes 786440 | tf_op jit(solution)/shard_map/ppermute | solution.py:220
  88.1 1.0 copy.15
  89.1 0.7 broadcast_in_dim.21
  89.8 2.4 %dynamic_update_slice.12 = f32[128,528]{0,1:T(8,128)} dynamic-update-slice(f32[128,528]{0,1:T(8,128)} %broadcast_in_dim.21, f32[32,528]{0,1:T(8,128)S(1)} %copy.15, s32[]{:T(128)S(6)} %select_n.16, s32[]{:T(128)} %constant.6.clone.1) | dynamic-update-slice | bytes 135172 | tf_op jit(solution)/shard_map/dynamic_update_slice | solution.py:338
  92.3 1.0 copy.16
  93.3 2.9 %dynamic_update_slice.13 = f32[128,528]{0,1:T(8,128)} dynamic-update-slice(f32[128,528]{0,1:T(8,128)} %dynamic_update_slice.12, f32[32,528]{0,1:T(8,128)S(1)} %copy.16, s32[]{:T(128)S(6)} %select_n.21, s32[]{:T(128)} %constant.6.clone.1) | dynamic-update-slice | bytes 135172 | tf_op jit(solution)/shard_map/dynamic_update_slice | solution.py:338
  96.2 1.0 copy.17
  97.2 2.9 %dynamic_update_slice.14 = f32[128,528]{0,1:T(8,128)} dynamic-update-slice(f32[128,528]{0,1:T(8,128)} %dynamic_update_slice.13, f32[32,528]{0,1:T(8,128)S(1)} %copy.17, s32[]{:T(128)S(6)} %select_n.22, s32[]{:T(128)} %constant.6.clone.1) | dynamic-update-slice | bytes 135172 | tf_op jit(solution)/shard_map/dynamic_update_slice | solution.py:338
  100.0 1.0 copy.18
  101.1 2.9 %dynamic_update_slice.15 = f32[128,528]{0,1:T(8,128)} dynamic-update-slice(f32[128,528]{0,1:T(8,128)} %dynamic_update_slice.14, f32[32,528]{0,1:T(8,128)S(1)} %copy.18, s32[]{:T(128)S(6)} %select_n.46, s32[]{:T(128)} %constant.6.clone.1) | dynamic-update-slice | bytes 135172 | tf_op jit(solution)/shard_map/dynamic_update_slice | solution.py:338
  103.9 1.0 slice.42
  104.9 0.8 copy.19
  105.7 1.3 %slice_bitcast_fusion = f32[16,128]{1,0:T(8,128)} fusion(f32[128,528]{0,1:T(8,128)} %dynamic_update_slice.15), kind=kLoop, calls=%fused_computation.32 | loop fusion | bytes 16384 | tf_op jit(solution)/shard_map/transpose | solution.py:344
  107.1 1.4 %gates.1 = (bf16[2048,128]{1,0:T(8,128)(2,1)}, bf16[2048,128]{1,0:T(8,128)(2,1)}, bf16[2048,128]{1,0:T(8,128)(2,1)}) custom-call(s32[1]{0:T(128)} %bitcast.q_ref, bf16[2,512,128]{2,1,0:T(8,128)(2,1)S(1)} %get-tuple-element.18.p0, bf16[2,512,128]{2,1,0:T(8,128)(2,1)S(1)} %collective-permute-done.11.p1, bf16[2,512,128]{2,1,0:T(8,128)(2,1)S(1)} %collective-permute-done.12.p2, ...), custom_call_target="tpu_custom_call" | custom-call | tf_op jit(solution)/shard_map/gates/pallas_call | solution.py:319
  (45 shorter events, 0.9 us)
Async XLA Ops:
  0.6 45.0 %copy-start = (bf16[128,512]{1,0:T(8,128)(2,1)S(1)}, bf16[128,512]{1,0:T(8,128)(2,1)}, u32[]{:S(2)}) copy-start(bf16[128,512]{1,0:T(8,128)(2,1)} %param.11) | copy-start | bytes 393220
  2.6 5.4 %collective-permute-start = (bf16[2,512,128]{2,1,0:T(8,128)(2,1)S(1)}, bf16[2,512,128]{2,1,0:T(8,128)(2,1)S(1)}, u32[]{:S(2)}, u32[]{:S(2)}) collective-permute-start(bf16[2,512,128]{2,1,0:T(8,128)(2,1)S(1)} %pad_maximum_fusion.2), channel_id=1, source_target_pairs={{0,2},{2,0},{4,6},{6,4},{8,10},{10,8},{12,14},{14,12},{16,18},{18,... | collective-permute-start | bytes 786440 | tf_op jit(solution)/shard_map/ppermute | solution.py:220
  3.2 9.7 %collective-permute-start.1 = (bf16[2,512,128]{2,1,0:T(8,128)(2,1)S(1)}, bf16[2,512,128]{2,1,0:T(8,128)(2,1)S(1)}, u32[]{:S(2)}, u32[]{:S(2)}) collective-permute-start(bf16[2,512,128]{2,1,0:T(8,128)(2,1)S(1)} %pad_maximum_fusion.3), channel_id=1, source_target_pairs={{0,4},{2,6},{4,0},{6,2},{8,12},{10,14},{12,8},{14,10},{16,20},{18,... | collective-permute-start | bytes 786440 | tf_op jit(solution)/shard_map/ppermute | solution.py:220
  5.8 12.3 %collective-permute-start.2 = (bf16[2,512,128]{2,1,0:T(8,128)(2,1)S(1)}, bf16[2,512,128]{2,1,0:T(8,128)(2,1)S(1)}, u32[]{:S(2)}, u32[]{:S(2)}) collective-permute-start(bf16[2,512,128]{2,1,0:T(8,128)(2,1)S(1)} %pad_maximum_fusion.4), channel_id=1, source_target_pairs={{0,6},{2,4},{4,2},{6,0},{8,14},{10,12},{12,10},{14,8},{16,22},{18,... | collective-permute-start | bytes 786440 | tf_op jit(solution)/shard_map/ppermute | solution.py:220
  20.4 12.1 %collective-permute-start.3 = (f32[4,16,128]{2,1,0:T(8,128)S(1)}, f32[4,16,128]{2,1,0:T(8,128)S(1)}, u32[]{:S(2)}, u32[]{:S(2)}) collective-permute-start(f32[4,16,128]{2,1,0:T(8,128)S(1)} %get-tuple-element.16), channel_id=1, source_target_pairs={{0,8},{2,10},{4,12},{6,14},{8,16},{10,18},{12,20},{14,22},{16,24},... | collective-permute-start | bytes 98312 | tf_op jit(solution)/shard_map/ppermute | solution.py:224
  24.0 13.8 %collective-permute-start.5 = (f32[4,16,128]{2,1,0:T(8,128)S(1)}, f32[4,16,128]{2,1,0:T(8,128)S(1)}, u32[]{:S(2)}, u32[]{:S(2)}) collective-permute-start(f32[4,16,128]{2,1,0:T(8,128)S(1)} %get-tuple-element.17), channel_id=1, source_target_pairs={{8,0},{10,2},{12,4},{14,6},{16,8},{18,10},{20,12},{22,14},{24,16},... | collective-permute-start | bytes 98312 | tf_op jit(solution)/shard_map/ppermute | solution.py:224
  25.3 25.7 %collective-permute-start.7 = (bf16[2,512,128]{2,1,0:T(8,128)(2,1)S(1)}, bf16[2,512,128]{2,1,0:T(8,128)(2,1)S(1)}, u32[]{:S(2)}, u32[]{:S(2)}) collective-permute-start(bf16[2,512,128]{2,1,0:T(8,128)(2,1)S(1)} %get-tuple-element.48), channel_id=1, source_target_pairs={{0,8},{2,10},{4,12},{6,14},{8,16},{10,18},{12,20},{14,22},{16,24},... | collective-permute-start | bytes 786440 | tf_op jit(solution)/shard_map/ppermute | solution.py:224
  29.9 21.2 %collective-permute-start.9 = (bf16[2,512,128]{2,1,0:T(8,128)(2,1)S(1)}, bf16[2,512,128]{2,1,0:T(8,128)(2,1)S(1)}, u32[]{:S(2)}, u32[]{:S(2)}) collective-permute-start(bf16[2,512,128]{2,1,0:T(8,128)(2,1)S(1)} %get-tuple-element.46), channel_id=1, source_target_pairs={{8,0},{10,2},{12,4},{14,6},{16,8},{18,10},{20,12},{22,14},{24,16},... | collective-permute-start | bytes 786440 | tf_op jit(solution)/shard_map/ppermute | solution.py:224
  31.2 19.8 %collective-permute-start.10 = (bf16[2,512,128]{2,1,0:T(8,128)(2,1)S(1)}, bf16[2,512,128]{2,1,0:T(8,128)(2,1)S(1)}, u32[]{:S(2)}, u32[]{:S(2)}) collective-permute-start(bf16[2,512,128]{2,1,0:T(8,128)(2,1)S(1)} %pad_maximum_fusion.7), channel_id=1, source_target_pairs={{8,0},{10,2},{12,4},{14,6},{16,8},{18,10},{20,12},{22,14},{24,16},... | collective-permute-start | bytes 786440 | tf_op jit(solution)/shard_map/ppermute | solution.py:224
  32.6 18.5 %collective-permute-start.8 = (bf16[2,512,128]{2,1,0:T(8,128)(2,1)S(1)}, bf16[2,512,128]{2,1,0:T(8,128)(2,1)S(1)}, u32[]{:S(2)}, u32[]{:S(2)}) collective-permute-start(bf16[2,512,128]{2,1,0:T(8,128)(2,1)S(1)} %pad_maximum_fusion.5), channel_id=1, source_target_pairs={{0,8},{2,10},{4,12},{6,14},{8,16},{10,18},{12,20},{14,22},{16,24},... | collective-permute-start | bytes 786440 | tf_op jit(solution)/shard_map/ppermute | solution.py:224
  37.8 6.5 %collective-permute-start.4 = (f32[4,16,128]{2,1,0:T(8,128)S(1)}, f32[4,16,128]{2,1,0:T(8,128)S(1)}, u32[]{:S(2)}, u32[]{:S(2)}) collective-permute-start(f32[4,16,128]{2,1,0:T(8,128)S(1)} %get-tuple-element.50), channel_id=1, source_target_pairs={{0,16},{2,18},{4,20},{6,22},{8,24},{10,26},{12,28},{14,30},{1,17},... | collective-permute-start | bytes 98312 | tf_op jit(solution)/shard_map/ppermute | solution.py:224
  44.3 6.7 %collective-permute-start.6 = (f32[4,16,128]{2,1,0:T(8,128)S(1)}, f32[4,16,128]{2,1,0:T(8,128)S(1)}, u32[]{:S(2)}, u32[]{:S(2)}) collective-permute-start(f32[4,16,128]{2,1,0:T(8,128)S(1)} %get-tuple-element.49), channel_id=1, source_target_pairs={{16,0},{18,2},{20,4},{22,6},{24,8},{26,10},{28,12},{30,14},{17,1},... | collective-permute-start | bytes 98312 | tf_op jit(solution)/shard_map/ppermute | solution.py:224
  49.7 57.4 %copy-start.1 = (bf16[2048,128]{1,0:T(8,128)(2,1)S(1)}, bf16[2048,128]{1,0:T(8,128)(2,1)}, u32[]{:S(2)}) copy-start(bf16[2048,128]{1,0:T(8,128)(2,1)} %v_ref.1) | copy-start | bytes 1572868
  49.7 57.4 %copy-start.2 = (bf16[2048,128]{1,0:T(8,128)(2,1)S(1)}, bf16[2048,128]{1,0:T(8,128)(2,1)}, u32[]{:S(2)}) copy-start(bf16[2048,128]{1,0:T(8,128)(2,1)} %k_ref.1) | copy-start | bytes 1572868
  49.7 57.4 %copy-start.3 = (bf16[2048,128]{1,0:T(8,128)(2,1)S(1)}, bf16[2048,128]{1,0:T(8,128)(2,1)}, u32[]{:S(2)}) copy-start(bf16[2048,128]{1,0:T(8,128)(2,1)} %go_ref.1) | copy-start | bytes 1572868
  71.8 0.7 copy-start.4
  72.7 4.7 %collective-permute-start.14 = (f32[32,528]{1,0:T(8,128)S(1)}, f32[32,528]{1,0:T(8,128)S(1)}, u32[]{:S(2)}, u32[]{:S(2)}) collective-permute-start(f32[32,528]{1,0:T(8,128)S(1)} %maximum_multiply_fusion), channel_id=1, source_target_pairs={{0,8},{2,10},{4,12},{6,14},{8,0},{10,2},{12,4},{14,6},{16,24},{18,... | collective-permute-start | bytes 202760 | tf_op jit(solution)/shard_map/ppermute | solution.py:220
  77.4 6.3 %collective-permute-start.15 = (f32[32,528]{1,0:T(8,128)S(1)}, f32[32,528]{1,0:T(8,128)S(1)}, u32[]{:S(2)}, u32[]{:S(2)}) collective-permute-start(f32[32,528]{1,0:T(8,128)S(1)} %fusion.8), channel_id=1, source_target_pairs={{0,16},{2,18},{4,20},{6,22},{8,24},{10,26},{12,28},{14,30},{16,0},... | collective-permute-start | bytes 202760 | tf_op jit(solution)/shard_map/ppermute | solution.py:220
  84.4 3.6 %collective-permute-start.16 = (f32[32,528]{1,0:T(8,128)}, f32[32,528]{1,0:T(8,128)}, u32[]{:S(2)}, u32[]{:S(2)}) collective-permute-start(f32[32,528]{1,0:T(8,128)} %add.59), channel_id=1, source_target_pairs={{0,2},{2,0},{4,6},{6,4},{8,10},{10,8},{12,14},{14,12},{16,18},{18,... | collective-permute-start | bytes 202760 | tf_op jit(solution)/shard_map/ppermute | solution.py:220
  84.4 11.8 %collective-permute-start.17 = (f32[32,528]{1,0:T(8,128)}, f32[32,528]{1,0:T(8,128)}, u32[]{:S(2)}, u32[]{:S(2)}) collective-permute-start(f32[32,528]{1,0:T(8,128)} %add.59), channel_id=1, source_target_pairs={{0,4},{2,6},{4,0},{6,2},{8,12},{10,14},{12,8},{14,10},{16,20},{18,... | collective-permute-start | bytes 202760 | tf_op jit(solution)/shard_map/ppermute | solution.py:220
  85.8 14.2 %collective-permute-start.18 = (f32[32,528]{1,0:T(8,128)}, f32[32,528]{1,0:T(8,128)}, u32[]{:S(2)}, u32[]{:S(2)}) collective-permute-start(f32[32,528]{1,0:T(8,128)} %add.59), channel_id=1, source_target_pairs={{0,6},{2,4},{4,2},{6,0},{8,14},{10,12},{12,10},{14,8},{16,22},{18,... | collective-permute-start | bytes 202760 | tf_op jit(solution)/shard_map/ppermute | solution.py:220
  86.2 20.8 %collective-permute-start.11 = (bf16[2,512,128]{2,1,0:T(8,128)(2,1)}, bf16[2,512,128]{2,1,0:T(8,128)(2,1)S(1)}, u32[]{:S(2)}, u32[]{:S(2)}) collective-permute-start(bf16[2,512,128]{2,1,0:T(8,128)(2,1)} %copy-done.4), channel_id=1, source_target_pairs={{0,2},{2,0},{4,6},{6,4},{8,10},{10,8},{12,14},{14,12},{16,18},{18,... | collective-permute-start | bytes 786440 | tf_op jit(solution)/shard_map/ppermute | solution.py:220
  86.5 20.5 %collective-permute-start.12 = (bf16[2,512,128]{2,1,0:T(8,128)(2,1)S(1)}, bf16[2,512,128]{2,1,0:T(8,128)(2,1)S(1)}, u32[]{:S(2)}, u32[]{:S(2)}) collective-permute-start(bf16[2,512,128]{2,1,0:T(8,128)(2,1)S(1)} %get-tuple-element.20), channel_id=1, source_target_pairs={{0,4},{2,6},{4,0},{6,2},{8,12},{10,14},{12,8},{14,10},{16,20},{18,... | collective-permute-start | bytes 786440 | tf_op jit(solution)/shard_map/ppermute | solution.py:220
  88.0 19.1 %collective-permute-start.13 = (bf16[2,512,128]{2,1,0:T(8,128)(2,1)S(1)}, bf16[2,512,128]{2,1,0:T(8,128)(2,1)S(1)}, u32[]{:S(2)}, u32[]{:S(2)}) collective-permute-start(bf16[2,512,128]{2,1,0:T(8,128)(2,1)S(1)} %get-tuple-element.21), channel_id=1, source_target_pairs={{0,6},{2,4},{4,2},{6,0},{8,14},{10,12},{12,10},{14,8},{16,22},{18,... | collective-permute-start | bytes 786440 | tf_op jit(solution)/shard_map/ppermute | solution.py:220
where the time goes:
time: 110 us; the launch traced here: 109 us
  starting transfers between devices  33.7 us (31%)
  Pallas kernels  28.3 us (26%)
  local copies, waits for them, and re-layouts  22 us (20%)
  waiting for transfers between devices  20.6 us (19%)
  other arithmetic  2.97 us (3%)
    ppermute x8, starting transfers between devices, shift(): lax.ppermute(value, 'ctx', [(i, i + by) for i in range(devices) if 0 <= i...  23.4 us
    pallas_call x1, Pallas kernels, body(): pl.pallas_call(main_kernel, grid=(steps,), in_specs=[smem, per_group, per...  20.7 us
    ppermute x11, waiting for transfers between devices, swap(): return lax.ppermute(value, 'ctx', [(i, i ^ m) for i in range(devices)])  17.7 us
    dynamic_update_slice x4, local copies, waits for them, and re-layouts, body(): lax.dynamic_update_slice_in_dim(gathered, got, (q ^ m) * local, 0)  11 us
    ppermute x11, starting transfers between devices, swap(): return lax.ppermute(value, 'ctx', [(i, i ^ m) for i in range(devices)])  10.3 us
    pallas_call x1, Pallas kernels, body(): pl.pallas_call(table_kernel, grid=(steps,), in_specs=[per_group, per_grou...  3.87 us
    ppermute x3, local copies, waits for them, and re-layouts, swap(): return lax.ppermute(value, 'ctx', [(i, i ^ m) for i in range(devices)])  3.05 us
    ppermute x8, waiting for transfers between devices, shift(): lax.ppermute(value, 'ctx', [(i, i + by) for i in range(devices) if 0 <= i...  2.93 us
  transfers between devices with their start and end apart: 19, of which 6 were waited for; matrix products, arithmetic and copies ran while one was open for 20% of the time, Pallas kernels for 4%

commit v1 on v0

v1 whole, which is shorter than its diff:
```python
import functools
import math

import jax
import jax.numpy as jnp
from jax import lax
from jax.experimental import pallas as pl
from jax.experimental.pallas import tpu as pltpu
from jax.sharding import PartitionSpec as P

GROUP = 16
BLK = 128
SPAN = 4
STEP = 8
PARTS = 2
WIDE = (SPAN + 1) * BLK
F32 = jnp.float32
BF16 = jnp.bfloat16
NT = (((1,), (1,)), ((), ()))
TN = (((0,), (0,)), ((), ()))
NN = (((1,), (0,)), ((), ()))


def mm(left, right, dims=NN):
    return lax.dot_general(left, right, dims, preferred_element_type=F32)


def halves(value):
    high = value.astype(BF16)
    return high, (value - high.astype(F32)).astype(BF16)


def lanes_of(rows):
    return lax.broadcasted_iota(jnp.int32, (rows, BLK), 1)


def table_kernel(rate_ref, gain_ref, med_ref, table_ref):
    lane = lanes_of(GROUP).astype(F32)
    for g in range(STEP):
        rate = rate_ref[g]
        gain = gain_ref[g]
        pieces = [jnp.zeros((1, BLK), F32)]
        for o in range(SPAN + 1):
            tail = jnp.sum(gain * jnp.exp(-rate * (lane + float(o * BLK))), axis=0, keepdims=True)
            if o < SPAN:
                tail = tail + med_ref[g : g + 1, o * BLK : (o + 1) * BLK].astype(F32)
            pieces.append(tail)
        taps = jnp.broadcast_to(jnp.concatenate(pieces, axis=1), (GROUP, WIDE + BLK))
        skewed = pltpu.roll(taps, 0, 1, stride=1, stride_axis=0)
        for i in range(BLK // GROUP):
            moved = skewed if i == 0 else pltpu.roll(skewed, GROUP * i, 1)
            table_ref[g, GROUP * i : GROUP * (i + 1), :] = moved[:, BLK:].astype(BF16)


def own_group(rows):
    row = lax.broadcasted_iota(jnp.int32, (rows, BLK), 0) // (rows // STEP)
    return row == lax.broadcasted_iota(jnp.int32, (rows, BLK), 1) // GROUP


def column_sum(value):
    total = value[0:GROUP]
    for g in range(1, STEP):
        total = total + value[GROUP * g : GROUP * (g + 1)]
    return total


def gather_blocks(q, pieces, near, far, xs, ys):
    for m, piece in enumerate(pieces):
        xs[SPAN + (q ^ m)] = piece[0]
        ys[q ^ m] = piece[1]
    for m in range(SPAN):
        x_part, y_part = near if m < 2 else far
        xs[q ^ m] = x_part[m % 2]
        ys[SPAN + (q ^ m)] = y_part[m % 2]


def state_kernel(
    q_ref, rate_ref, row_ref, p0, p1, p2, p3, xa, xb, ya, yb,
    car_ref, ret_ref, end_ref, ahead_ref, behind_ref, cross_ref, xs, ys,
):
    gather_blocks(q_ref[0], (p0, p1, p2, p3), (xa, ya), (xb, yb), xs, ys)
    rate = rate_ref[...].reshape(BLK, BLK)
    tok = lanes_of(BLK).astype(F32)
    row = row_ref[0, 0:1, :]
    decay = jnp.exp(-row * float(BLK))
    skip = jnp.exp(-row * float(SPAN * BLK))
    same = own_group(BLK)
    fin = jnp.concatenate(halves(jnp.exp(-rate * (BLK - 1.0 - tok))), axis=0)
    ini = jnp.concatenate(halves(jnp.exp(-rate * (tok + 1.0))), axis=0)

    def state(blocks, j, weights):
        both = mm(blocks[j], weights, NT)
        return jnp.where(same, both[:, :BLK] + both[:, BLK:], 0.0)

    carried = state(xs, 0, fin)
    for i in range(1, SPAN):
        car_ref[0, i - 1] = carried.astype(BF16)
        carried = carried * decay + state(xs, i, fin)
    own = [state(xs, SPAN + i, fin) for i in range(SPAN)]
    end = own[0]
    for i in range(1, SPAN):
        end = end * decay + own[i]
    end_ref[0] = column_sum(end)
    ahead_ref[0] = column_sum(end + skip * carried)

    returned = state(ys, 2 * SPAN - 1, ini)
    cross = jnp.zeros((BLK, BLK), F32)
    for i in range(SPAN - 2, -1, -1):
        ret_ref[0, i] = returned.astype(BF16)
        cross = cross + own[i] * returned
        returned = returned * decay + state(ys, SPAN + i, ini)
    head = state(ys, SPAN - 1, ini)
    for i in range(SPAN - 2, -1, -1):
        head = head * decay + state(ys, i, ini)
    behind_ref[0] = column_sum(head + skip * returned)
    cross_ref[0] = column_sum(cross) * skip


def roll_left(value, amount):
    width = value.shape[1]
    return value if amount % width == 0 else pltpu.roll(value, width - amount, 1)


def fold(value):
    for step in (64, 32, 16):
        value = value + pltpu.roll(value, step, 1)
    return value


def lag_kernel(
    q_ref, rate_ref, row_ref, root_ref, cross_ref, p0, p1, p2, p3, ya, yb, lag_ref, xs, ys,
    *, scale,
):
    q = q_ref[0]
    for m, piece in enumerate((p0, p1, p2, p3)):
        xs[q ^ m] = piece[0]
        ys[q ^ m] = piece[1]
        ys[SPAN + (q ^ m)] = (ya if m < 2 else yb)[m % 2]
    row_at = lax.broadcasted_iota(jnp.int32, (BLK, BLK), 0)
    causal = lanes_of(BLK) >= row_at
    sub_at = lax.broadcasted_iota(jnp.int32, (8, WIDE), 0)
    lag_rows = []
    for g in range(STEP):
        rows = slice(GROUP * g, GROUP * (g + 1))
        y = [ys[j, rows, :] for j in range(2 * SPAN)]
        wide_y = jnp.concatenate(
            [jnp.concatenate(y[o : o + SPAN], axis=0) for o in range(SPAN + 1)], axis=1
        )
        own_x = jnp.concatenate([xs[j, rows, :] for j in range(SPAN)], axis=0)
        pairs = mm(own_x, wide_y, TN)
        pairs = jnp.concatenate((jnp.where(causal, pairs[:, :BLK], 0.0), pairs[:, BLK:]), axis=1)
        total = pairs[0:8]
        for i in range(1, BLK // 8):
            total = total + roll_left(pairs[8 * i : 8 * (i + 1)], 8 * i)
        for bit in (1, 2, 4):
            total = jnp.where((sub_at & bit) != 0, roll_left(total, bit), total)
        lag_rows.append(jnp.sum(total, axis=0, keepdims=True))
    lags = jnp.concatenate(lag_rows, axis=0)
    rate = rate_ref[...].reshape(BLK, BLK)
    row = row_ref[0, 0:1, :]
    fade = jnp.concatenate(halves(jnp.exp(-rate * lanes_of(BLK).astype(F32))), axis=0)
    split = jnp.concatenate(halves(lags), axis=0)
    coef = jnp.zeros((STEP, BLK), F32)
    for o in range(SPAN + 1):
        both = mm(split[:, o * BLK : (o + 1) * BLK], fade, NT)
        term = both[:STEP, :BLK] + both[:STEP, BLK:] + both[STEP:, :BLK]
        coef = coef + term * jnp.exp(-row * float(o * BLK))
    cross = jnp.sum(cross_ref[0], axis=0, keepdims=True)
    coef = fold(jnp.where(own_group(STEP), (coef + cross) * root_ref[0, 0:1, :], 0.0))
    lag_ref[...] = jnp.concatenate((lags[:, : SPAN * BLK], coef), axis=1) * scale


def join_kernel(row_ref, root_ref, end_ref, after_ref, lag_ref, out_ref, *, scale):
    for step in range(row_ref.shape[0]):
        rows = slice(STEP * step, STEP * (step + 1))
        skip = jnp.exp(-row_ref[step, 0:1, :] * float(SPAN * BLK))
        cross = jnp.sum(end_ref[step] * after_ref[step], axis=0, keepdims=True)
        cross = cross * skip * root_ref[step, 0:1, :] * scale
        coef = fold(jnp.where(own_group(STEP), cross, 0.0))
        out_ref[rows, : SPAN * BLK] = lag_ref[rows, : SPAN * BLK]
        out_ref[rows, SPAN * BLK :] = lag_ref[rows, SPAN * BLK :] + coef


def main_kernel(
    q_ref, rate_ref, gain_ref, row_ref, table_ref, car_ref, ret_ref, before_ref, after_ref,
    p0, p1, p2, p3, xa, xb, ya, yb, o0, o1, o2, o3, xs, ys, fs, bs,
):
    q = q_ref[0]
    gather_blocks(q, (p0, p1, p2, p3), (xa, ya), (xb, yb), xs, ys)
    rate = rate_ref[...].reshape(BLK, BLK)
    gain = gain_ref[...].reshape(BLK, BLK)
    tok = lanes_of(BLK).astype(F32)
    row = row_ref[0, 0:1, :]
    same = own_group(BLK)
    shift = float(SPAN * BLK)
    out_f = (gain * jnp.exp(-rate * (tok + 1.0 + shift))).astype(BF16)
    out_b = (gain * jnp.exp(-rate * (BLK - 1.0 - tok + shift))).astype(BF16)
    out_f = jnp.concatenate((out_f, out_f), axis=0)
    out_b = jnp.concatenate((out_b, out_b), axis=0)

    def spread(ref):
        return jnp.where(same, jnp.concatenate([ref[0]] * STEP, axis=0), 0.0)

    start = spread(before_ref)
    stop = spread(after_ref)
    none = jnp.zeros((BLK, BLK), BF16)
    far_f, far_b = [], []
    for i in range(SPAN):
        left = none if i == 0 else car_ref[0, i - 1]
        rest = (start * jnp.exp(-row * float(BLK * i))).astype(BF16)
        far_f.append(mm(jnp.concatenate((left, rest), axis=1), out_f))
        left = none if i == SPAN - 1 else ret_ref[0, i]
        rest = (stop * jnp.exp(-row * float(BLK * (SPAN - 1 - i)))).astype(BF16)
        far_b.append(mm(jnp.concatenate((left, rest), axis=1), out_b))
    for i in range(SPAN):
        fs[i] = far_f[i]
        bs[i] = far_b[i]
    for g in range(STEP):
        rows = slice(GROUP * g, GROUP * (g + 1))
        x = [xs[j, rows, :] for j in range(2 * SPAN)]
        y = [ys[j, rows, :] for j in range(2 * SPAN)]
        wide_x = jnp.concatenate(
            [jnp.concatenate(x[SPAN - o : 2 * SPAN - o], axis=0) for o in range(SPAN + 1)], axis=1
        )
        wide_y = jnp.concatenate(
            [jnp.concatenate(y[o : o + SPAN], axis=0) for o in range(SPAN + 1)], axis=1
        )
        table = table_ref[g]
        tall = jnp.concatenate(
            [table[:, o * BLK : (o + 1) * BLK] for o in range(SPAN + 1)], axis=0
        )
        forward = mm(wide_x, tall)
        backward = mm(wide_y, table, NT)
        for i in range(SPAN):
            cut = slice(GROUP * i, GROUP * (i + 1))
            fs[i, rows, :] += forward[cut]
            bs[i, rows, :] += backward[cut]
    for m, out in enumerate((o0, o1, o2, o3)):
        out[0] = fs[q ^ m].astype(BF16)
        out[1] = bs[q ^ m].astype(BF16)


def sum_kernel(q_ref, s0, s1, s2, s3, med_ref, res_ref, turned):
    q = q_ref[0]
    local = s0.shape[0]
    for m, part in enumerate((s0, s1, s2, s3)):
        at = pl.ds(pl.multiple_of((q ^ m) * local, local), local)
        med_ref[at, :] = part[:, : SPAN * BLK]
        turned[at, :] = part[:, SPAN * BLK :]
    res_ref[...] = turned[...].T[:GROUP]


def gate_kernel(q_ref, *refs):
    q = q_ref[0]
    pieces, (go_ref, v_ref, k_ref, gq_ref, gk_ref, gv_ref) = refs[:-6], refs[-6:]
    part = pieces[0].shape[1]
    parts = len(pieces) // SPAN
    for h in range(parts):
        for m in range(SPAN):
            piece = pieces[h * SPAN + m]
            at = pl.ds(pl.multiple_of((q ^ m) * (part * parts) + h * part, part), part)
            gq_ref[at, :] = (go_ref[at, :].astype(F32) * piece[0].astype(F32)).astype(BF16)
            grad = piece[1].astype(F32)
            gk_ref[at, :] = (grad * v_ref[at, :].astype(F32)).astype(BF16)
            gv_ref[at, :] = (grad * k_ref[at, :].astype(F32)).astype(BF16)


def body(query, key_in, value_in, grad_out, med_filter, residues, pole_rate):
    channels, length = query.shape
    groups = channels // GROUP
    devices = lax.axis_size("ctx")
    seq_total = length * devices
    ranks = SPAN
    units = devices // ranks
    sub = channels // ranks
    local = groups // ranks
    index = lax.axis_index("ctx")
    q = lax.rem(index, ranks).astype(jnp.int32)
    q_arr = q.reshape(1)

    def swap(value, m):
        return lax.ppermute(value, "ctx", [(i, i ^ m) for i in range(devices)])

    def shift(value, by):
        by = by * ranks
        return lax.ppermute(
            value, "ctx", [(i, i + by) for i in range(devices) if 0 <= i + by < devices]
        )

    def part(m):
        def cut(array):
            return lax.dynamic_slice_in_dim(array, (q ^ m) * sub, sub, 0).astype(F32)

        return jnp.stack(
            [
                (cut(key_in) * cut(value_in)).astype(BF16),
                (cut(grad_out) * cut(query)).astype(BF16),
            ]
        )

    pieces = [part(0)] + [swap(part(m), m) for m in range(1, ranks)]

    x_near = shift(jnp.stack([pieces[0][0], pieces[1][0]]), 1)
    y_near = shift(jnp.stack([pieces[0][1], pieces[1][1]]), -1)
    x_far = shift(jnp.stack([pieces[2][0], pieces[3][0]]), 1)
    y_far = shift(jnp.stack([pieces[2][1], pieces[3][1]]), -1)

    rate = lax.dynamic_slice_in_dim(pole_rate, q * local, local, 1).T / seq_total
    res = lax.dynamic_slice_in_dim(residues, q * local, local, 1).T
    med = lax.dynamic_slice_in_dim(med_filter, q * local, local, 0)
    root = jnp.sqrt(-jnp.expm1(-2.0 * rate))
    rate_wide = jnp.broadcast_to(rate[:, :, None], (local, GROUP, BLK))
    gain_wide = jnp.broadcast_to((res * root)[:, :, None], (local, GROUP, BLK))

    steps = local // STEP
    rows = STEP * GROUP

    def flat(value):
        return jnp.broadcast_to(value.reshape(steps, 1, BLK), (steps, 8, BLK))

    rate_row = flat(rate)
    root_row = flat(root)
    scale = 1.0 / math.sqrt(GROUP * seq_total)
    params = pltpu.CompilerParams(vmem_limit_bytes=40 << 20)
    smem = pl.BlockSpec(memory_space=pltpu.SMEM)
    whole = pl.BlockSpec(memory_space=pltpu.VMEM)

    def block(shape, axis, offset=0):
        def at(i):
            return tuple(i + offset if d == axis else 0 for d in range(len(shape)))

        return pl.BlockSpec(shape, at)

    def specs(offset=0):
        return dict(
            group=block((STEP, GROUP, BLK), 0, offset),
            row=block((1, 8, BLK), 0, offset),
            packed=block((1, GROUP, BLK), 0, offset),
            pair=block((2, rows, BLK), 1, offset),
            states=block((1, SPAN - 1, BLK, BLK), 0, offset),
            table=block((STEP, BLK, WIDE), 0, offset),
            lag=block((STEP, WIDE), 0, offset),
        )

    sp = specs()
    table = pl.pallas_call(
        table_kernel,
        grid=(steps,),
        in_specs=[sp["group"], sp["group"], block((STEP, SPAN * BLK), 0)],
        out_specs=sp["table"],
        out_shape=jax.ShapeDtypeStruct((local, BLK, WIDE), BF16),
        compiler_params=params,
        name="tables",
    )(rate_wide, gain_wide, med)

    store = jax.ShapeDtypeStruct((steps, SPAN - 1, BLK, BLK), BF16)
    small = jax.ShapeDtypeStruct((steps, GROUP, BLK), F32)
    blocks = pltpu.VMEM((2 * SPAN, rows, BLK), BF16)
    halo = (x_near, x_far, y_near, y_far)
    carried, returned, ends, ahead, behind, cross = pl.pallas_call(
        state_kernel,
        grid=(steps,),
        in_specs=[smem, sp["group"], sp["row"]] + [sp["pair"]] * 8,
        out_specs=[sp["states"]] * 2 + [sp["packed"]] * 4,
        out_shape=[store] * 2 + [small] * 4,
        scratch_shapes=[blocks] * 2,
        compiler_params=params,
        name="states",
    )(q_arr, rate_wide, rate_row, *pieces, *halo)

    reach = 2
    while reach < units - 2:
        fade = jnp.exp(-rate_row[:, :1] * float(reach * ranks * length))
        ahead, behind = ahead + fade * shift(ahead, reach), behind + fade * shift(behind, -reach)
        reach *= 2
    before = shift(ahead, 2)
    after = shift(behind, -2)

    lag = pl.pallas_call(
        functools.partial(lag_kernel, scale=scale),
        grid=(steps,),
        in_specs=[smem, sp["group"], sp["row"], sp["row"], sp["packed"]] + [sp["pair"]] * 6,
        out_specs=sp["lag"],
        out_shape=jax.ShapeDtypeStruct((local, WIDE), F32),
        scratch_shapes=[pltpu.VMEM((SPAN, rows, BLK), BF16), blocks],
        compiler_params=params,
        name="lags",
    )(q_arr, rate_wide, rate_row, root_row, cross, *pieces, y_near, y_far)

    sums = pl.pallas_call(
        functools.partial(join_kernel, scale=scale),
        in_specs=[whole] * 5,
        out_specs=whole,
        out_shape=jax.ShapeDtypeStruct((local, WIDE), F32),
        compiler_params=params,
        name="joins",
    )(rate_row, root_row, ends, after, lag)

    back = []
    parts = PARTS
    for h in range(parts):
        sh = specs(h * (steps // parts))
        so = specs()
        outs = pl.pallas_call(
            main_kernel,
            grid=(steps // parts,),
            in_specs=[smem, sh["group"], sh["group"], sh["row"], sh["table"]]
            + [sh["states"]] * 2
            + [sh["packed"]] * 2
            + [sh["pair"]] * 8,
            out_specs=[so["pair"]] * 4,
            out_shape=[jax.ShapeDtypeStruct((2, sub // parts, BLK), BF16)] * 4,
            scratch_shapes=[blocks] * 2 + [pltpu.VMEM((SPAN, rows, BLK), F32)] * 2,
            compiler_params=params,
            name="convs",
        )(
            q_arr, rate_wide, gain_wide, rate_row, table, carried, returned, before, after,
            *pieces, *halo,
        )
        back += [outs[0]] + [swap(outs[m], m) for m in range(1, ranks)]

    hop = 1
    while hop < units:
        sums = sums + swap(sums, hop * ranks)
        hop *= 2
    parts_of = [sums] + [swap(sums, m) for m in range(1, ranks)]

    grads = pl.pallas_call(
        gate_kernel,
        in_specs=[smem] + [whole] * (len(back) + 3),
        out_specs=[whole] * 3,
        out_shape=[jax.ShapeDtypeStruct((channels, length), BF16)] * 3,
        compiler_params=params,
        name="gates",
    )(q_arr, *back, grad_out, value_in, key_in)
    grad_med, grad_res = pl.pallas_call(
        sum_kernel,
        in_specs=[smem] + [whole] * ranks,
        out_specs=[whole] * 2,
        out_shape=[
            jax.ShapeDtypeStruct((groups, SPAN * BLK), F32),
            jax.ShapeDtypeStruct((GROUP, groups), F32),
        ],
        scratch_shapes=[pltpu.VMEM((groups, BLK), F32)],
        compiler_params=params,
        name="sums",
    )(q_arr, *parts_of)
    return (*grads, grad_med, grad_res)


def solution(mesh):
    in_specs = (
        P("ch", "ctx"),
        P("ch", "ctx"),
        P("ch", "ctx"),
        P("ch", "ctx"),
        P("ch", None),
        P(None, "ch"),
        P(None, "ch"),
    )
    out_specs = (P("ch", "ctx"), P("ch", "ctx"), P("ch", "ctx"), P("ch", None), P(None, "ch"))
    return jax.shard_map(body, mesh=mesh, in_specs=in_specs, out_specs=out_specs, check_vma=False)
```

time: 110 us -> 81.7 us (0.74); the launches traced: 109 us -> 81.4 us
  local copies, waits for them, and re-layouts: 22 us -> 0.75 us
  Pallas kernels: 28.3 us -> 20.2 us
  waiting for transfers between devices: 20.6 us -> 27.7 us
  starting transfers between devices: 33.7 us -> 28.5 us
    dynamic_update_slice x4 -> x0, local copies, waits for them, and re-layouts: 11 us -> none  [body(): lax.dynamic_update_slice_in_dim(gathered, got, (q ^ m) * local, 0)]
    ppermute x8 -> x6, waiting for transfers between devices: 2.93 us -> 12.8 us  [shift(): lax.ppermute(value, 'ctx', [(i, i + by) for i in range(devices) if 0 <= i...]
    pallas_call x4 -> x8, Pallas kernels: 28.3 us -> 20.2 us  [the longest x1 7.23 us: body(): pl.pallas_call(functools.partial(lag_kernel, scale=scale), grid=(steps,),...]
    ppermute x8 -> x6, starting transfers between devices: 23.4 us -> 16.6 us  [shift(): lax.ppermute(value, 'ctx', [(i, i + by) for i in range(devices) if 0 <= i...]
    ppermute x3 -> x0, local copies, waits for them, and re-layouts: 3.05 us -> none  [swap(): return lax.ppermute(value, 'ctx', [(i, i ^ m) for i in range(devices)])]
    ppermute x11 -> x14, waiting for transfers between devices: 17.7 us -> 14.9 us  [swap(): return lax.ppermute(value, 'ctx', [(i, i ^ m) for i in range(devices)])]
    unnamed x13 -> x12, local copies, waits for them, and re-layouts: 1.72 us -> 0.04 us
    ppermute x11 -> x14, starting transfers between devices: 10.3 us -> 11.9 us  [swap(): return lax.ppermute(value, 'ctx', [(i, i ^ m) for i in range(devices)])]
  transfers between devices with their start and end apart: 19 -> 20, of which waited for: 6 -> 9; matrix products, arithmetic and copies ran while one was open for 20% -> 2% of each run, Pallas kernels for 4% -> 21%
where the time goes in v1:
time: 81.7 us; the launch traced here: 81.4 us
  starting transfers between devices  28.5 us (35%)
  waiting for transfers between devices  27.7 us (34%)
  Pallas kernels  20.2 us (25%)
  other arithmetic  3.26 us (4%)
  between operations  0.99 us (1%)
    ppermute x6, starting transfers between devices, shift(): lax.ppermute(value, 'ctx', [(i, i + by) for i in range(devices) if 0 <= i...  16.6 us
    ppermute x14, waiting for transfers between devices, swap(): return lax.ppermute(value, 'ctx', [(i, i ^ m) for i in range(devices)])  14.9 us
    ppermute x6, waiting for transfers between devices, shift(): lax.ppermute(value, 'ctx', [(i, i + by) for i in range(devices) if 0 <= i...  12.8 us
    ppermute x14, starting transfers between devices, swap(): return lax.ppermute(value, 'ctx', [(i, i ^ m) for i in range(devices)])  11.9 us
    pallas_call x1, Pallas kernels, body(): pl.pallas_call(functools.partial(lag_kernel, scale=scale), grid=(steps,),...  7.23 us
    pallas_call x2, Pallas kernels, body(): pl.pallas_call(main_kernel, grid=(steps // parts,), in_specs=[smem, sh['g...  4.47 us
    pallas_call x1, Pallas kernels, body(): pl.pallas_call(table_kernel, grid=(steps,), in_specs=[sp['group'], sp['gr...  3.87 us
    pallas_call x1, Pallas kernels, body(): pl.pallas_call(state_kernel, grid=(steps,), in_specs=[smem, sp['group'],...  2.18 us
  transfers between devices with their start and end apart: 20, of which 9 were waited for; matrix products, arithmetic and copies ran while one was open for 2% of the time, Pallas kernels for 21%

profile of v1, /device:TPU:0, one launch (start us, length us, event | category | flops | bytes accessed | tf_op | source)
XLA Modules:
  0.0 81.4 jit_solution(6007853079105755615)
XLA Ops:
  0.7 1.9 %fusion.6 = (bf16[1,512,128]{2,1,0:T(8,128)(2,1)S(1)}, bf16[1,512,128]{2,1,0:T(8,128)(2,1)S(1)}, bf16[1,512,128]{2,1,0:T(8,128)(2,1)S(1)}, bf16[1,512,128]{2,1,0...) fusion(bf16[2048,128]{1,0:T(8,128)(2,1)} %refs_9_.1, ...), kind=kLoop, calls=%fused_computation.22 | loop fusion | flops 2097152 | bytes 3145744 | tf_op jit(solution)/shard_map/stack | solution.py:294
  2.6 0.5 collective-permute-start
  3.2 2.6 %collective-permute-start.1 = (bf16[2,512,128]{2,1,0:T(8,128)(2,1)S(1)}, bf16[2,512,128]{2,1,0:T(8,128)(2,1)S(1)}, u32[]{:S(2)}, u32[]{:S(2)}) collective-permute-start(bf16[2,512,128]{2,1,0:T(8,128)(2,1)S(1)} %pad_maximum_fusion.3), channel_id=1, source_target_pairs={{0,4},{2,6},{4,0},{6,2},{8,12},{10,14},{12,8},{14,10},{16,20},{18,... | collective-permute-start | bytes 786440 | tf_op jit(solution)/shard_map/ppermute | solution.py:282
  5.8 0.2 collective-permute-start.2
  6.0 3.7 %collective-permute-start.3 = (bf16[2,512,128]{2,1,0:T(8,128)(2,1)S(1)}, bf16[2,512,128]{2,1,0:T(8,128)(2,1)S(1)}, u32[]{:S(2)}, u32[]{:S(2)}) collective-permute-start(bf16[2,512,128]{2,1,0:T(8,128)(2,1)S(1)} %get-tuple-element.59), channel_id=1, source_target_pairs={{0,8},{2,10},{4,12},{6,14},{8,16},{10,18},{12,20},{14,22},{16,24},... | collective-permute-start | bytes 786440 | tf_op jit(solution)/shard_map/ppermute | solution.py:286
  9.8 8.3 %collective-permute-done.2.p3 = bf16[2,512,128]{2,1,0:T(8,128)(2,1)S(1)} collective-permute-done((bf16[2,512,128]{2,1,0:T(8,128)(2,1)S(1)}, bf16[2,512,128]{2,1,0:T(8,128)(2,1)S(1)}, u32[]{:S(2)}, u32[]{:S(2)}) %collective-permute-start.2) | collective-permute-done | bytes 262176 | tf_op jit(solution)/shard_map/ppermute | solution.py:282
  18.2 3.5 %collective-permute-start.4 = (bf16[2,512,128]{2,1,0:T(8,128)(2,1)S(1)}, bf16[2,512,128]{2,1,0:T(8,128)(2,1)S(1)}, u32[]{:S(2)}, u32[]{:S(2)}) collective-permute-start(bf16[2,512,128]{2,1,0:T(8,128)(2,1)S(1)} %pad_maximum_fusion.5), channel_id=1, source_target_pairs={{0,8},{2,10},{4,12},{6,14},{8,16},{10,18},{12,20},{14,22},{16,24},... | collective-permute-start | bytes 786440 | tf_op jit(solution)/shard_map/ppermute | solution.py:286
  21.8 1.3 %collective-permute-start.5 = (bf16[2,512,128]{2,1,0:T(8,128)(2,1)S(1)}, bf16[2,512,128]{2,1,0:T(8,128)(2,1)S(1)}, u32[]{:S(2)}, u32[]{:S(2)}) collective-permute-start(bf16[2,512,128]{2,1,0:T(8,128)(2,1)S(1)} %get-tuple-element.57), channel_id=1, source_target_pairs={{8,0},{10,2},{12,4},{14,6},{16,8},{18,10},{20,12},{22,14},{24,16},... | collective-permute-start | bytes 786440 | tf_op jit(solution)/shard_map/ppermute | solution.py:286
  23.1 1.3 %collective-permute-start.6 = (bf16[2,512,128]{2,1,0:T(8,128)(2,1)S(1)}, bf16[2,512,128]{2,1,0:T(8,128)(2,1)S(1)}, u32[]{:S(2)}, u32[]{:S(2)}) collective-permute-start(bf16[2,512,128]{2,1,0:T(8,128)(2,1)S(1)} %pad_maximum_fusion.7), channel_id=1, source_target_pairs={{8,0},{10,2},{12,4},{14,6},{16,8},{18,10},{20,12},{22,14},{24,16},... | collective-permute-start | bytes 786440 | tf_op jit(solution)/shard_map/ppermute | solution.py:286
  24.4 0.1 sqrt_bitcast_fusion
  24.5 0.1 copy.14
  24.6 0.1 broadcast_in_dim.28
  24.7 3.0 %collective-permute-done.4.xb = bf16[2,512,128]{2,1,0:T(8,128)(2,1)S(1)} collective-permute-done((bf16[2,512,128]{2,1,0:T(8,128)(2,1)S(1)}, bf16[2,512,128]{2,1,0:T(8,128)(2,1)S(1)}, u32[]{:S(2)}, u32[]{:S(2)}) %collective-permute-start.4) | collective-permute-done | bytes 262176 | tf_op jit(solution)/shard_map/ppermute | solution.py:286
  27.7 5.1 %collective-permute-done.5.ya = bf16[2,512,128]{2,1,0:T(8,128)(2,1)S(1)} collective-permute-done((bf16[2,512,128]{2,1,0:T(8,128)(2,1)S(1)}, bf16[2,512,128]{2,1,0:T(8,128)(2,1)S(1)}, u32[]{:S(2)}, u32[]{:S(2)}) %collective-permute-start.5) | collective-permute-done | bytes 262176 | tf_op jit(solution)/shard_map/ppermute | solution.py:286
  32.8 4.6 %collective-permute-done.6.yb = bf16[2,512,128]{2,1,0:T(8,128)(2,1)S(1)} collective-permute-done((bf16[2,512,128]{2,1,0:T(8,128)(2,1)S(1)}, bf16[2,512,128]{2,1,0:T(8,128)(2,1)S(1)}, u32[]{:S(2)}, u32[]{:S(2)}) %collective-permute-start.6) | collective-permute-done | bytes 262176 | tf_op jit(solution)/shard_map/ppermute | solution.py:286
  37.4 0.1 broadcast_in_dim.12.rate_ref
  37.6 2.2 %states.1 = (bf16[4,3,128,128]{3,2,1,0:T(8,128)(2,1)S(1)}, bf16[4,3,128,128]{3,2,1,0:T(8,128)(2,1)S(1)}, f32[4,16,128]{2,1,0:T(8,128)S(1)}, f32[4,16,128]{2,1,0:...) custom-call(s32[1]{0:T(128)} %bitcast.q_ref, f32[32,16,128]{2,1,0:T(8,128)S(1)} %broadcast_in_dim.12.rate_ref, ...), custom_call_target="tpu_custom_call" | custom-call | tf_op jit(solution)/shard_map/states/pallas_call | solution.py:360
  39.8 1.3 %collective-permute-start.8 = (f32[4,16,128]{2,1,0:T(8,128)S(1)}, f32[4,16,128]{2,1,0:T(8,128)S(1)}, u32[]{:S(2)}, u32[]{:S(2)}) collective-permute-start(f32[4,16,128]{2,1,0:T(8,128)S(1)} %get-tuple-element.27), channel_id=1, source_target_pairs={{16,0},{18,2},{20,4},{22,6},{24,8},{26,10},{28,12},{30,14},{17,1},... | collective-permute-start | bytes 98312 | tf_op jit(solution)/shard_map/ppermute | solution.py:286
  41.1 0.1 copy.17
  41.2 0.1 broadcast_in_dim.30
  41.2 5.4 %collective-permute-start.7 = (f32[4,16,128]{2,1,0:T(8,128)S(1)}, f32[4,16,128]{2,1,0:T(8,128)S(1)}, u32[]{:S(2)}, u32[]{:S(2)}) collective-permute-start(f32[4,16,128]{2,1,0:T(8,128)S(1)} %get-tuple-element.26), channel_id=1, source_target_pairs={{0,16},{2,18},{4,20},{6,22},{8,24},{10,26},{12,28},{14,30},{1,17},... | collective-permute-start | bytes 98312 | tf_op jit(solution)/shard_map/ppermute | solution.py:286
  46.7 7.2 %lags.1.lag_ref = f32[32,640]{1,0:T(8,128)S(1)} custom-call(s32[1]{0:T(128)} %bitcast.q_ref, f32[32,16,128]{2,1,0:T(8,128)S(1)} %broadcast_in_dim.12.rate_ref, f32[4,8,128]{2,1,0:T(8,128)S(1)} %broadcast_in_dim.29.row_ref, f32[4,8,128]{2,1,0:T(8,128)S(1)} %broadcast_in_dim.31.root_ref, f32[4,16,128]{2,1,0:T(8,128)S(1)} %get-tuple-element.40.cross_ref, ...), custom_call_target="tpu_custom_call" | custom-call | tf_op jit(solution)/shard_map/lags/pallas_call | solution.py:379
  53.9 0.2 joins.1
  54.2 1.6 %collective-permute-start.15 = (f32[32,640]{1,0:T(8,128)S(1)}, f32[32,640]{1,0:T(8,128)}, u32[]{:S(2)}, u32[]{:S(2)}) collective-permute-start(f32[32,640]{1,0:T(8,128)S(1)} %joins.1), channel_id=1, source_target_pairs={{0,8},{2,10},{4,12},{6,14},{8,0},{10,2},{12,4},{14,6},{16,24},{18,... | collective-permute-start | bytes 245768 | tf_op jit(solution)/shard_map/ppermute | solution.py:282
  55.8 0.1 bitcast_multiply_fusion
  55.9 0.1 copy.15
  55.9 0.1 broadcast_in_dim.13.gain_ref
  56.1 3.9 %tables.1.table_ref = bf16[32,128,640]{2,1,0:T(8,128)(2,1)S(1)} custom-call(f32[32,16,128]{2,1,0:T(8,128)S(1)} %broadcast_in_dim.12.rate_ref, f32[32,16,128]{2,1,0:T(8,128)S(1)} %broadcast_in_dim.13.gain_ref, bf16[32,512]{1,0:T(8,128)(2,1)S(1)} %constant_dynamic-slice_fusion.med_ref), custom_call_target="tpu_custom_call" | custom-call | tf_op jit(solution)/shard_map/tables/pallas_call | solution.py:346
  60.0 2.3 %convs.2 = (bf16[2,256,128]{2,1,0:T(8,128)(2,1)S(1)}, bf16[2,256,128]{2,1,0:T(8,128)(2,1)S(1)}, bf16[2,256,128]{2,1,0:T(8,128)(2,1)S(1)}, bf16[2,256,128]{2,1,0:T(8,128)(2,1)S(1)}) custom-call(s32[1]{0:T(128)} %bitcast.q_ref, f32[32,16,128]{2,1,0:T(8,128)S(1)} %broadcast_in_dim.12.rate_ref, f32[32,16,128]{2,1,0:T(8,128)S(1)} %broadcast_in_dim.13.gain_ref, ...), custom_call_target="tpu_custom_call" | custom-call | tf_op jit(solution)/shard_map/convs/pallas_call | solution.py:404
  62.3 0.1 collective-permute-start.9
  62.3 1.0 %add.19 = f32[32,640]{1,0:T(8,128)S(1)} add(f32[32,640]{1,0:T(8,128)S(1)} %joins.1, f32[32,640]{1,0:T(8,128)} %collective-permute-done.15) | non-fusion elementwise | flops 20480 | bytes 245760 | tf_op jit(solution)/shard_map/add | solution.py:424
  63.3 0.1 collective-permute-start.16
  63.4 1.6 %collective-permute-start.10 = (bf16[2,256,128]{2,1,0:T(8,128)(2,1)S(1)}, bf16[2,256,128]{2,1,0:T(8,128)(2,1)S(1)}, u32[]{:S(2)}, u32[]{:S(2)}) collective-permute-start(bf16[2,256,128]{2,1,0:T(8,128)(2,1)S(1)} %get-tuple-element.30), channel_id=1, source_target_pairs={{0,4},{2,6},{4,0},{6,2},{8,12},{10,14},{12,8},{14,10},{16,20},{18,... | collective-permute-start | bytes 393224 | tf_op jit(solution)/shard_map/ppermute | solution.py:282
  65.0 0.2 collective-permute-start.11
  65.2 2.2 %convs.3 = (bf16[2,256,128]{2,1,0:T(8,128)(2,1)S(1)}, bf16[2,256,128]{2,1,0:T(8,128)(2,1)S(1)}, bf16[2,256,128]{2,1,0:T(8,128)(2,1)S(1)}, bf16[2,256,128]{2,1,0:T(8,128)(2,1)S(1)}) custom-call(s32[1]{0:T(128)} %bitcast.q_ref, f32[32,16,128]{2,1,0:T(8,128)S(1)} %broadcast_in_dim.12.rate_ref, f32[32,16,128]{2,1,0:T(8,128)S(1)} %broadcast_in_dim.13.gain_ref, ...), custom_call_target="tpu_custom_call" | custom-call | tf_op jit(solution)/shard_map/convs/pallas_call | solution.py:404
  67.4 0.5 collective-permute-start.12
  67.9 1.5 %collective-permute-start.13 = (bf16[2,256,128]{2,1,0:T(8,128)(2,1)S(1)}, bf16[2,256,128]{2,1,0:T(8,128)(2,1)S(1)}, u32[]{:S(2)}, u32[]{:S(2)}) collective-permute-start(bf16[2,256,128]{2,1,0:T(8,128)(2,1)S(1)} %get-tuple-element.34), channel_id=1, source_target_pairs={{0,4},{2,6},{4,0},{6,2},{8,12},{10,14},{12,8},{14,10},{16,20},{18,... | collective-permute-start | bytes 393224 | tf_op jit(solution)/shard_map/ppermute | solution.py:282
  69.4 1.2 %collective-permute-done.16 = f32[32,640]{1,0:T(8,128)S(1)} collective-permute-done((f32[32,640]{1,0:T(8,128)S(1)}, f32[32,640]{1,0:T(8,128)S(1)}, u32[]{:S(2)}, u32[]{:S(2)}) %collective-permute-start.16) | collective-permute-done | bytes 81952 | tf_op jit(solution)/shard_map/ppermute | solution.py:282
  70.7 1.2 %collective-permute-start.14 = (bf16[2,256,128]{2,1,0:T(8,128)(2,1)S(1)}, bf16[2,256,128]{2,1,0:T(8,128)(2,1)S(1)}, u32[]{:S(2)}, u32[]{:S(2)}) collective-permute-start(bf16[2,256,128]{2,1,0:T(8,128)(2,1)S(1)} %get-tuple-element.35), channel_id=1, source_target_pairs={{0,6},{2,4},{4,2},{6,0},{8,14},{10,12},{12,10},{14,8},{16,22},{18,... | collective-permute-start | bytes 393224 | tf_op jit(solution)/shard_map/ppermute | solution.py:282
  71.9 0.5 collective-permute-start.17
  72.4 0.6 collective-permute-start.18
  73.0 0.8 collective-permute-start.19
  73.8 1.6 %collective-permute-done.13.refs_6_ = bf16[2,256,128]{2,1,0:T(8,128)(2,1)S(1)} collective-permute-done((bf16[2,256,128]{2,1,0:T(8,128)(2,1)S(1)}, bf16[2,256,128]{2,1,0:T(8,128)(2,1)S(1)}, u32[]{:S(2)}, u32[]{:S(2)}) %collective-permute-start.13) | collective-permute-done | bytes 131104 | tf_op jit(solution)/shard_map/ppermute | solution.py:282
  75.4 1.8 %collective-permute-done.14.refs_7_ = bf16[2,256,128]{2,1,0:T(8,128)(2,1)S(1)} collective-permute-done((bf16[2,256,128]{2,1,0:T(8,128)(2,1)S(1)}, bf16[2,256,128]{2,1,0:T(8,128)(2,1)S(1)}, u32[]{:S(2)}, u32[]{:S(2)}) %collective-permute-start.14) | collective-permute-done | bytes 131104 | tf_op jit(solution)/shard_map/ppermute | solution.py:282
  77.3 1.5 %gates.1 = (bf16[2048,128]{1,0:T(8,128)(2,1)}, bf16[2048,128]{1,0:T(8,128)(2,1)}, bf16[2048,128]{1,0:T(8,128)(2,1)}) custom-call(s32[1]{0:T(128)} %bitcast.q_ref, bf16[2,256,128]{2,1,0:T(8,128)(2,1)S(1)} %get-tuple-element.28.refs_0_, bf16[2,256,128]{2,1,0:T(8,128)(2,1)S(1)} %collective-permute-done.9.refs_1_, ...), custom_call_target="tpu_custom_call" | custom-call | tf_op jit(solution)/shard_map/gates/pallas_call | solution.py:428
  78.8 1.2 %collective-permute-done.18.s2 = f32[32,640]{1,0:T(8,128)S(1)} collective-permute-done((f32[32,640]{1,0:T(8,128)S(1)}, f32[32,640]{1,0:T(8,128)S(1)}, u32[]{:S(2)}, u32[]{:S(2)}) %collective-permute-start.18) | collective-permute-done | bytes 81952 | tf_op jit(solution)/shard_map/ppermute | solution.py:282
  80.0 0.7 collective-permute-done.19.s3
  80.7 0.7 sums.1
  (36 shorter events, 0.3 us)
Async XLA Ops:
  0.6 40.4 %copy-start = (bf16[128,512]{1,0:T(8,128)(2,1)S(1)}, bf16[128,512]{1,0:T(8,128)(2,1)}, u32[]{:S(2)}) copy-start(bf16[128,512]{1,0:T(8,128)(2,1)} %param.11) | copy-start | bytes 393220
  0.6 23.8 %copy-start.4 = (f32[16,128]{1,0:T(8,128)S(1)}, f32[16,128]{1,0:T(8,128)}, u32[]{:S(2)}) copy-start(f32[16,128]{1,0:T(8,128)} %param.13) | copy-start | bytes 24580
  2.6 53.2 %copy-start.5 = (f32[16,128]{1,0:T(8,128)S(1)}, f32[16,128]{1,0:T(8,128)}, u32[]{:S(2)}) copy-start(f32[16,128]{1,0:T(8,128)} %param.12) | copy-start | bytes 24580
  2.6 3.3 %collective-permute-start = (bf16[2,512,128]{2,1,0:T(8,128)(2,1)S(1)}, bf16[2,512,128]{2,1,0:T(8,128)(2,1)S(1)}, u32[]{:S(2)}, u32[]{:S(2)}) collective-permute-start(bf16[2,512,128]{2,1,0:T(8,128)(2,1)S(1)} %pad_maximum_fusion.2), channel_id=1, source_target_pairs={{0,2},{2,0},{4,6},{6,4},{8,10},{10,8},{12,14},{14,12},{16,18},{18,... | collective-permute-start | bytes 786440 | tf_op jit(solution)/shard_map/ppermute | solution.py:282
  3.2 15.0 %collective-permute-start.1 = (bf16[2,512,128]{2,1,0:T(8,128)(2,1)S(1)}, bf16[2,512,128]{2,1,0:T(8,128)(2,1)S(1)}, u32[]{:S(2)}, u32[]{:S(2)}) collective-permute-start(bf16[2,512,128]{2,1,0:T(8,128)(2,1)S(1)} %pad_maximum_fusion.3), channel_id=1, source_target_pairs={{0,4},{2,6},{4,0},{6,2},{8,12},{10,14},{12,8},{14,10},{16,20},{18,... | collective-permute-start | bytes 786440 | tf_op jit(solution)/shard_map/ppermute | solution.py:282
  5.8 12.3 %collective-permute-start.2 = (bf16[2,512,128]{2,1,0:T(8,128)(2,1)S(1)}, bf16[2,512,128]{2,1,0:T(8,128)(2,1)S(1)}, u32[]{:S(2)}, u32[]{:S(2)}) collective-permute-start(bf16[2,512,128]{2,1,0:T(8,128)(2,1)S(1)} %pad_maximum_fusion.4), channel_id=1, source_target_pairs={{0,6},{2,4},{4,2},{6,0},{8,14},{10,12},{12,10},{14,8},{16,22},{18,... | collective-permute-start | bytes 786440 | tf_op jit(solution)/shard_map/ppermute | solution.py:282
  6.0 18.6 %collective-permute-start.3 = (bf16[2,512,128]{2,1,0:T(8,128)(2,1)S(1)}, bf16[2,512,128]{2,1,0:T(8,128)(2,1)S(1)}, u32[]{:S(2)}, u32[]{:S(2)}) collective-permute-start(bf16[2,512,128]{2,1,0:T(8,128)(2,1)S(1)} %get-tuple-element.59), channel_id=1, source_target_pairs={{0,8},{2,10},{4,12},{6,14},{8,16},{10,18},{12,20},{14,22},{16,24},... | collective-permute-start | bytes 786440 | tf_op jit(solution)/shard_map/ppermute | solution.py:286
  18.2 9.5 %collective-permute-start.4 = (bf16[2,512,128]{2,1,0:T(8,128)(2,1)S(1)}, bf16[2,512,128]{2,1,0:T(8,128)(2,1)S(1)}, u32[]{:S(2)}, u32[]{:S(2)}) collective-permute-start(bf16[2,512,128]{2,1,0:T(8,128)(2,1)S(1)} %pad_maximum_fusion.5), channel_id=1, source_target_pairs={{0,8},{2,10},{4,12},{6,14},{8,16},{10,18},{12,20},{14,22},{16,24},... | collective-permute-start | bytes 786440 | tf_op jit(solution)/shard_map/ppermute | solution.py:286
  21.8 11.1 %collective-permute-start.5 = (bf16[2,512,128]{2,1,0:T(8,128)(2,1)S(1)}, bf16[2,512,128]{2,1,0:T(8,128)(2,1)S(1)}, u32[]{:S(2)}, u32[]{:S(2)}) collective-permute-start(bf16[2,512,128]{2,1,0:T(8,128)(2,1)S(1)} %get-tuple-element.57), channel_id=1, source_target_pairs={{8,0},{10,2},{12,4},{14,6},{16,8},{18,10},{20,12},{22,14},{24,16},... | collective-permute-start | bytes 786440 | tf_op jit(solution)/shard_map/ppermute | solution.py:286
  23.1 14.3 %collective-permute-start.6 = (bf16[2,512,128]{2,1,0:T(8,128)(2,1)S(1)}, bf16[2,512,128]{2,1,0:T(8,128)(2,1)S(1)}, u32[]{:S(2)}, u32[]{:S(2)}) collective-permute-start(bf16[2,512,128]{2,1,0:T(8,128)(2,1)S(1)} %pad_maximum_fusion.7), channel_id=1, source_target_pairs={{8,0},{10,2},{12,4},{14,6},{16,8},{18,10},{20,12},{22,14},{24,16},... | collective-permute-start | bytes 786440 | tf_op jit(solution)/shard_map/ppermute | solution.py:286
  39.8 14.2 %collective-permute-start.8 = (f32[4,16,128]{2,1,0:T(8,128)S(1)}, f32[4,16,128]{2,1,0:T(8,128)S(1)}, u32[]{:S(2)}, u32[]{:S(2)}) collective-permute-start(f32[4,16,128]{2,1,0:T(8,128)S(1)} %get-tuple-element.27), channel_id=1, source_target_pairs={{16,0},{18,2},{20,4},{22,6},{24,8},{26,10},{28,12},{30,14},{17,1},... | collective-permute-start | bytes 98312 | tf_op jit(solution)/shard_map/ppermute | solution.py:286
  41.2 18.7 %collective-permute-start.7 = (f32[4,16,128]{2,1,0:T(8,128)S(1)}, f32[4,16,128]{2,1,0:T(8,128)S(1)}, u32[]{:S(2)}, u32[]{:S(2)}) collective-permute-start(f32[4,16,128]{2,1,0:T(8,128)S(1)} %get-tuple-element.26), channel_id=1, source_target_pairs={{0,16},{2,18},{4,20},{6,22},{8,24},{10,26},{12,28},{14,30},{1,17},... | collective-permute-start | bytes 98312 | tf_op jit(solution)/shard_map/ppermute | solution.py:286
  54.2 8.2 %collective-permute-start.15 = (f32[32,640]{1,0:T(8,128)S(1)}, f32[32,640]{1,0:T(8,128)}, u32[]{:S(2)}, u32[]{:S(2)}) collective-permute-start(f32[32,640]{1,0:T(8,128)S(1)} %joins.1), channel_id=1, source_target_pairs={{0,8},{2,10},{4,12},{6,14},{8,0},{10,2},{12,4},{14,6},{16,24},{18,... | collective-permute-start | bytes 245768 | tf_op jit(solution)/shard_map/ppermute | solution.py:282
  62.2 15.1 %copy-start.1 = (bf16[2048,128]{1,0:T(8,128)(2,1)S(1)}, bf16[2048,128]{1,0:T(8,128)(2,1)}, u32[]{:S(2)}) copy-start(bf16[2048,128]{1,0:T(8,128)(2,1)} %refs_9_.1) | copy-start | bytes 1572868
  62.2 15.0 %copy-start.2 = (bf16[2048,128]{1,0:T(8,128)(2,1)S(1)}, bf16[2048,128]{1,0:T(8,128)(2,1)}, u32[]{:S(2)}) copy-start(bf16[2048,128]{1,0:T(8,128)(2,1)} %refs_10_.1) | copy-start | bytes 1572868
  62.2 15.0 %copy-start.3 = (bf16[2048,128]{1,0:T(8,128)(2,1)S(1)}, bf16[2048,128]{1,0:T(8,128)(2,1)}, u32[]{:S(2)}) copy-start(bf16[2048,128]{1,0:T(8,128)(2,1)} %refs_8_.1) | copy-start | bytes 1572868
  62.3 5.7 %collective-permute-start.9 = (bf16[2,256,128]{2,1,0:T(8,128)(2,1)S(1)}, bf16[2,256,128]{2,1,0:T(8,128)(2,1)S(1)}, u32[]{:S(2)}, u32[]{:S(2)}) collective-permute-start(bf16[2,256,128]{2,1,0:T(8,128)(2,1)S(1)} %get-tuple-element.29), channel_id=1, source_target_pairs={{0,2},{2,0},{4,6},{6,4},{8,10},{10,8},{12,14},{14,12},{16,18},{18,... | collective-permute-start | bytes 393224 | tf_op jit(solution)/shard_map/ppermute | solution.py:282
  63.3 7.3 %collective-permute-start.16 = (f32[32,640]{1,0:T(8,128)S(1)}, f32[32,640]{1,0:T(8,128)S(1)}, u32[]{:S(2)}, u32[]{:S(2)}) collective-permute-start(f32[32,640]{1,0:T(8,128)S(1)} %add.19), channel_id=1, source_target_pairs={{0,16},{2,18},{4,20},{6,22},{8,24},{10,26},{12,28},{14,30},{16,0},... | collective-permute-start | bytes 245768 | tf_op jit(solution)/shard_map/ppermute | solution.py:282
  63.4 8.4 %collective-permute-start.10 = (bf16[2,256,128]{2,1,0:T(8,128)(2,1)S(1)}, bf16[2,256,128]{2,1,0:T(8,128)(2,1)S(1)}, u32[]{:S(2)}, u32[]{:S(2)}) collective-permute-start(bf16[2,256,128]{2,1,0:T(8,128)(2,1)S(1)} %get-tuple-element.30), channel_id=1, source_target_pairs={{0,4},{2,6},{4,0},{6,2},{8,12},{10,14},{12,8},{14,10},{16,20},{18,... | collective-permute-start | bytes 393224 | tf_op jit(solution)/shard_map/ppermute | solution.py:282
  65.0 7.4 %collective-permute-start.11 = (bf16[2,256,128]{2,1,0:T(8,128)(2,1)S(1)}, bf16[2,256,128]{2,1,0:T(8,128)(2,1)S(1)}, u32[]{:S(2)}, u32[]{:S(2)}) collective-permute-start(bf16[2,256,128]{2,1,0:T(8,128)(2,1)S(1)} %get-tuple-element.31), channel_id=1, source_target_pairs={{0,6},{2,4},{4,2},{6,0},{8,14},{10,12},{12,10},{14,8},{16,22},{18,... | collective-permute-start | bytes 393224 | tf_op jit(solution)/shard_map/ppermute | solution.py:282
  67.4 5.6 %collective-permute-start.12 = (bf16[2,256,128]{2,1,0:T(8,128)(2,1)S(1)}, bf16[2,256,128]{2,1,0:T(8,128)(2,1)S(1)}, u32[]{:S(2)}, u32[]{:S(2)}) collective-permute-start(bf16[2,256,128]{2,1,0:T(8,128)(2,1)S(1)} %get-tuple-element.33), channel_id=1, source_target_pairs={{0,2},{2,0},{4,6},{6,4},{8,10},{10,8},{12,14},{14,12},{16,18},{18,... | collective-permute-start | bytes 393224 | tf_op jit(solution)/shard_map/ppermute | solution.py:282
  67.9 7.5 %collective-permute-start.13 = (bf16[2,256,128]{2,1,0:T(8,128)(2,1)S(1)}, bf16[2,256,128]{2,1,0:T(8,128)(2,1)S(1)}, u32[]{:S(2)}, u32[]{:S(2)}) collective-permute-start(bf16[2,256,128]{2,1,0:T(8,128)(2,1)S(1)} %get-tuple-element.34), channel_id=1, source_target_pairs={{0,4},{2,6},{4,0},{6,2},{8,12},{10,14},{12,8},{14,10},{16,20},{18,... | collective-permute-start | bytes 393224 | tf_op jit(solution)/shard_map/ppermute | solution.py:282
  70.7 6.6 %collective-permute-start.14 = (bf16[2,256,128]{2,1,0:T(8,128)(2,1)S(1)}, bf16[2,256,128]{2,1,0:T(8,128)(2,1)S(1)}, u32[]{:S(2)}, u32[]{:S(2)}) collective-permute-start(bf16[2,256,128]{2,1,0:T(8,128)(2,1)S(1)} %get-tuple-element.35), channel_id=1, source_target_pairs={{0,6},{2,4},{4,2},{6,0},{8,14},{10,12},{12,10},{14,8},{16,22},{18,... | collective-permute-start | bytes 393224 | tf_op jit(solution)/shard_map/ppermute | solution.py:282
  71.9 6.9 %collective-permute-start.17 = (f32[32,640]{1,0:T(8,128)S(1)}, f32[32,640]{1,0:T(8,128)S(1)}, u32[]{:S(2)}, u32[]{:S(2)}) collective-permute-start(f32[32,640]{1,0:T(8,128)S(1)} %add.20.s0), channel_id=1, source_target_pairs={{0,2},{2,0},{4,6},{6,4},{8,10},{10,8},{12,14},{14,12},{16,18},{18,... | collective-permute-start | bytes 245768 | tf_op jit(solution)/shard_map/ppermute | solution.py:282
  72.4 7.6 %collective-permute-start.18 = (f32[32,640]{1,0:T(8,128)S(1)}, f32[32,640]{1,0:T(8,128)S(1)}, u32[]{:S(2)}, u32[]{:S(2)}) collective-permute-start(f32[32,640]{1,0:T(8,128)S(1)} %add.20.s0), channel_id=1, source_target_pairs={{0,4},{2,6},{4,0},{6,2},{8,12},{10,14},{12,8},{14,10},{16,20},{18,... | collective-permute-start | bytes 245768 | tf_op jit(solution)/shard_map/ppermute | solution.py:282
  73.0 7.6 %collective-permute-start.19 = (f32[32,640]{1,0:T(8,128)S(1)}, f32[32,640]{1,0:T(8,128)S(1)}, u32[]{:S(2)}, u32[]{:S(2)}) collective-permute-start(f32[32,640]{1,0:T(8,128)S(1)} %add.20.s0), channel_id=1, source_target_pairs={{0,6},{2,4},{4,2},{6,0},{8,14},{10,12},{12,10},{14,8},{16,22},{18,... | collective-permute-start | bytes 245768 | tf_op jit(solution)/shard_map/ppermute | solution.py:282

commit v2 on v1

--- a/solution.py
+++ b/solution.py
@@ -34,7 +34,8 @@
     return lax.broadcasted_iota(jnp.int32, (rows, BLK), 1)
 
 
-def table_kernel(rate_ref, gain_ref, med_ref, table_ref):
+def table_kernel(row_ref, rate_ref, gain_ref, med_ref, table_ref, next_ref):
+    next_ref[...] = row_ref[...]
     lane = lanes_of(GROUP).astype(F32)
     for g in range(STEP):
         rate = rate_ref[g]
@@ -76,9 +77,9 @@
 
 def state_kernel(
     q_ref, rate_ref, row_ref, p0, p1, p2, p3, xa, xb, ya, yb,
-    car_ref, ret_ref, end_ref, ahead_ref, behind_ref, cross_ref, xs, ys,
+    car_ref, ret_ref, end_ref, ahead_ref, behind_ref, mail_ref, cross_ref, xs, ys,
 ):
-    gather_blocks(q_ref[0], (p0, p1, p2, p3), (xa, ya), (xb, yb), xs, ys)
+    gather_blocks(q_ref[0] & 3, (p0, p1, p2, p3), (xa, ya), (xb, yb), xs, ys)
     rate = rate_ref[...].reshape(BLK, BLK)
     tok = lanes_of(BLK).astype(F32)
     row = row_ref[0, 0:1, :]
@@ -101,7 +102,8 @@
     for i in range(1, SPAN):
         end = end * decay + own[i]
     end_ref[0] = column_sum(end)
-    ahead_ref[0] = column_sum(end + skip * carried)
+    ahead = column_sum(end + skip * carried)
+    ahead_ref[0] = ahead
 
     returned = state(ys, 2 * SPAN - 1, ini)
     cross = jnp.zeros((BLK, BLK), F32)
@@ -112,7 +114,9 @@
     head = state(ys, SPAN - 1, ini)
     for i in range(SPAN - 2, -1, -1):
         head = head * decay + state(ys, i, ini)
-    behind_ref[0] = column_sum(head + skip * returned)
+    behind = column_sum(head + skip * returned)
+    behind_ref[0] = behind
+    mail_ref[0] = jnp.where((q_ref[0] & 4) > 0, ahead, behind)
     cross_ref[0] = column_sum(cross) * skip
 
 
@@ -128,18 +132,17 @@
 
 
 def lag_kernel(
-    q_ref, rate_ref, row_ref, root_ref, cross_ref, p0, p1, p2, p3, ya, yb, lag_ref, xs, ys,
+    q_ref, rate_ref, row_ref, root_ref, cross_ref, p0, p1, p2, p3, ya, yb, lag_ref, xs, ys, sums,
     *, scale,
 ):
-    q = q_ref[0]
+    q = q_ref[0] & 3
     for m, piece in enumerate((p0, p1, p2, p3)):
         xs[q ^ m] = piece[0]
         ys[q ^ m] = piece[1]
         ys[SPAN + (q ^ m)] = (ya if m < 2 else yb)[m % 2]
     row_at = lax.broadcasted_iota(jnp.int32, (BLK, BLK), 0)
     causal = lanes_of(BLK) >= row_at
-    sub_at = lax.broadcasted_iota(jnp.int32, (8, WIDE), 0)
-    lag_rows = []
+    lane8 = lanes_of(8)
     for g in range(STEP):
         rows = slice(GROUP * g, GROUP * (g + 1))
         y = [ys[j, rows, :] for j in range(2 * SPAN)]
@@ -148,14 +151,26 @@
         )
         own_x = jnp.concatenate([xs[j, rows, :] for j in range(SPAN)], axis=0)
         pairs = mm(own_x, wide_y, TN)
-        pairs = jnp.concatenate((jnp.where(causal, pairs[:, :BLK], 0.0), pairs[:, BLK:]), axis=1)
-        total = pairs[0:8]
-        for i in range(1, BLK // 8):
-            total = total + roll_left(pairs[8 * i : 8 * (i + 1)], 8 * i)
-        for bit in (1, 2, 4):
-            total = jnp.where((sub_at & bit) != 0, roll_left(total, bit), total)
-        lag_rows.append(jnp.sum(total, axis=0, keepdims=True))
-    lags = jnp.concatenate(lag_rows, axis=0)
+        tiles = [pairs[:, o * BLK : (o + 1) * BLK] for o in range(SPAN + 1)]
+        tiles[0] = jnp.where(causal, tiles[0], 0.0)
+        count = BLK // 8
+        parts = [[tile[8 * i : 8 * (i + 1)] for i in range(count)] for tile in tiles]
+        while count > 1:
+            count //= 2
+            keep = lane8 < BLK - 8 * count
+            moved = [
+                [pltpu.roll(part[i + count], BLK - 8 * count, 1) for i in range(count)]
+                for part in parts
+            ]
+            for o in range(SPAN + 1):
+                for i in range(count):
+                    after = moved[o + 1][i] if o < SPAN else 0.0
+                    parts[o][i] = parts[o][i] + jnp.where(keep, moved[o][i], after)
+        for o in range(SPAN + 1):
+            sums[g, :, o * BLK : (o + 1) * BLK] = parts[o][0]
+    lags = sums[:, 0, :]
+    for r in range(1, 8):
+        lags = lags + roll_left(sums[:, r, :], r)
     rate = rate_ref[...].reshape(BLK, BLK)
     row = row_ref[0, 0:1, :]
     fade = jnp.concatenate(halves(jnp.exp(-rate * lanes_of(BLK).astype(F32))), axis=0)
@@ -170,13 +185,13 @@
     lag_ref[...] = jnp.concatenate((lags[:, : SPAN * BLK], coef), axis=1) * scale
 
 
-def join_kernel(row_ref, root_ref, end_ref, after_ref, lag_ref, out_ref, *, scale):
+def join_kernel(q_ref, row_ref, root_ref, end_ref, after_ref, lag_ref, out_ref, *, scale):
     for step in range(row_ref.shape[0]):
         rows = slice(STEP * step, STEP * (step + 1))
         skip = jnp.exp(-row_ref[step, 0:1, :] * float(SPAN * BLK))
         cross = jnp.sum(end_ref[step] * after_ref[step], axis=0, keepdims=True)
         cross = cross * skip * root_ref[step, 0:1, :] * scale
-        coef = fold(jnp.where(own_group(STEP), cross, 0.0))
+        coef = fold(jnp.where(own_group(STEP) & ((q_ref[0] & 16) > 0), cross, 0.0))
         out_ref[rows, : SPAN * BLK] = lag_ref[rows, : SPAN * BLK]
         out_ref[rows, SPAN * BLK :] = lag_ref[rows, SPAN * BLK :] + coef
 
@@ -185,7 +200,7 @@
     q_ref, rate_ref, gain_ref, row_ref, table_ref, car_ref, ret_ref, before_ref, after_ref,
     p0, p1, p2, p3, xa, xb, ya, yb, o0, o1, o2, o3, xs, ys, fs, bs,
 ):
-    q = q_ref[0]
+    q = q_ref[0] & 3
     gather_blocks(q, (p0, p1, p2, p3), (xa, ya), (xb, yb), xs, ys)
     rate = rate_ref[...].reshape(BLK, BLK)
     gain = gain_ref[...].reshape(BLK, BLK)
@@ -198,11 +213,11 @@
     out_f = jnp.concatenate((out_f, out_f), axis=0)
     out_b = jnp.concatenate((out_b, out_b), axis=0)
 
-    def spread(ref):
-        return jnp.where(same, jnp.concatenate([ref[0]] * STEP, axis=0), 0.0)
-
-    start = spread(before_ref)
-    stop = spread(after_ref)
+    def spread(ref, flag):
+        return jnp.where(same & (flag > 0), jnp.concatenate([ref[0]] * STEP, axis=0), 0.0)
+
+    start = spread(before_ref, q_ref[0] & 8)
+    stop = spread(after_ref, q_ref[0] & 16)
     none = jnp.zeros((BLK, BLK), BF16)
     far_f, far_b = [], []
     for i in range(SPAN):
@@ -241,7 +256,7 @@
 
 
 def sum_kernel(q_ref, s0, s1, s2, s3, med_ref, res_ref, turned):
-    q = q_ref[0]
+    q = q_ref[0] & 3
     local = s0.shape[0]
     for m, part in enumerate((s0, s1, s2, s3)):
         at = pl.ds(pl.multiple_of((q ^ m) * local, local), local)
@@ -251,7 +266,7 @@
 
 
 def gate_kernel(q_ref, *refs):
-    q = q_ref[0]
+    q = q_ref[0] & 3
     pieces, (go_ref, v_ref, k_ref, gq_ref, gk_ref, gv_ref) = refs[:-6], refs[-6:]
     part = pieces[0].shape[1]
     parts = len(pieces) // SPAN
@@ -276,7 +291,10 @@
     local = groups // ranks
     index = lax.axis_index("ctx")
     q = lax.rem(index, ranks).astype(jnp.int32)
-    q_arr = q.reshape(1)
+    low = (index < 2 * ranks).astype(jnp.int32)
+    one = jnp.int32(1)
+    ahead_on, behind_on = (one - low, low) if units == 4 else (one, one)
+    q_arr = (q + 4 * low + 8 * ahead_on + 16 * behind_on).reshape(1)
 
     def swap(value, m):
         return lax.ppermute(value, "ctx", [(i, i ^ m) for i in range(devices)])
@@ -302,9 +320,6 @@
 
     x_near = shift(jnp.stack([pieces[0][0], pieces[1][0]]), 1)
     y_near = shift(jnp.stack([pieces[0][1], pieces[1][1]]), -1)
-    x_far = shift(jnp.stack([pieces[2][0], pieces[3][0]]), 1)
-    y_far = shift(jnp.stack([pieces[2][1], pieces[3][1]]), -1)
-
     rate = lax.dynamic_slice_in_dim(pole_rate, q * local, local, 1).T / seq_total
     res = lax.dynamic_slice_in_dim(residues, q * local, local, 1).T
     med = lax.dynamic_slice_in_dim(med_filter, q * local, local, 0)
@@ -321,7 +336,7 @@
     rate_row = flat(rate)
     root_row = flat(root)
     scale = 1.0 / math.sqrt(GROUP * seq_total)
-    params = pltpu.CompilerParams(vmem_limit_bytes=40 << 20)
+    params = pltpu.CompilerParams(vmem_limit_bytes=8 << 20)
     smem = pl.BlockSpec(memory_space=pltpu.SMEM)
     whole = pl.BlockSpec(memory_space=pltpu.VMEM)
 
@@ -343,38 +358,53 @@
         )
 
     sp = specs()
-    table = pl.pallas_call(
+    pieces[2], pieces[3], x_near, y_near, rate_row, root_row = lax.optimization_barrier(
+        (pieces[2], pieces[3], x_near, y_near, rate_row, root_row)
+    )
+    x_far = shift(jnp.stack([pieces[2][0], pieces[3][0]]), 1)
+    y_far = shift(jnp.stack([pieces[2][1], pieces[3][1]]), -1)
+
+    table, rate_row = pl.pallas_call(
         table_kernel,
         grid=(steps,),
-        in_specs=[sp["group"], sp["group"], block((STEP, SPAN * BLK), 0)],
-        out_specs=sp["table"],
-        out_shape=jax.ShapeDtypeStruct((local, BLK, WIDE), BF16),
+        in_specs=[sp["row"], sp["group"], sp["group"], block((STEP, SPAN * BLK), 0)],
+        out_specs=[sp["table"], sp["row"]],
+        out_shape=[
+            jax.ShapeDtypeStruct((local, BLK, WIDE), BF16),
+            jax.ShapeDtypeStruct(rate_row.shape, F32),
+        ],
         compiler_params=params,
         name="tables",
-    )(rate_wide, gain_wide, med)
+    )(rate_row, rate_wide, gain_wide, med)
 
     store = jax.ShapeDtypeStruct((steps, SPAN - 1, BLK, BLK), BF16)
     small = jax.ShapeDtypeStruct((steps, GROUP, BLK), F32)
     blocks = pltpu.VMEM((2 * SPAN, rows, BLK), BF16)
     halo = (x_near, x_far, y_near, y_far)
-    carried, returned, ends, ahead, behind, cross = pl.pallas_call(
+    carried, returned, ends, ahead, behind, mail, cross = pl.pallas_call(
         state_kernel,
         grid=(steps,),
         in_specs=[smem, sp["group"], sp["row"]] + [sp["pair"]] * 8,
-        out_specs=[sp["states"]] * 2 + [sp["packed"]] * 4,
-        out_shape=[store] * 2 + [small] * 4,
+        out_specs=[sp["states"]] * 2 + [sp["packed"]] * 5,
+        out_shape=[store] * 2 + [small] * 5,
         scratch_shapes=[blocks] * 2,
         compiler_params=params,
         name="states",
     )(q_arr, rate_wide, rate_row, *pieces, *halo)
 
-    reach = 2
-    while reach < units - 2:
-        fade = jnp.exp(-rate_row[:, :1] * float(reach * ranks * length))
-        ahead, behind = ahead + fade * shift(ahead, reach), behind + fade * shift(behind, -reach)
-        reach *= 2
-    before = shift(ahead, 2)
-    after = shift(behind, -2)
+    if units == 4:
+        before = after = swap(mail, 2 * ranks)
+    else:
+        reach = 2
+        while reach < units - 2:
+            fade = jnp.exp(-rate_row[:, :1] * float(reach * ranks * length))
+            ahead, behind = (
+                ahead + fade * shift(ahead, reach),
+                behind + fade * shift(behind, -reach),
+            )
+            reach *= 2
+        before = shift(ahead, 2)
+        after = shift(behind, -2)
 
     lag = pl.pallas_call(
         functools.partial(lag_kernel, scale=scale),
@@ -382,22 +412,28 @@
         in_specs=[smem, sp["group"], sp["row"], sp["row"], sp["packed"]] + [sp["pair"]] * 6,
         out_specs=sp["lag"],
         out_shape=jax.ShapeDtypeStruct((local, WIDE), F32),
-        scratch_shapes=[pltpu.VMEM((SPAN, rows, BLK), BF16), blocks],
+        scratch_shapes=[
+            pltpu.VMEM((SPAN, rows, BLK), BF16),
+            blocks,
+            pltpu.VMEM((STEP, 8, WIDE), F32),
+        ],
         compiler_params=params,
         name="lags",
     )(q_arr, rate_wide, rate_row, root_row, cross, *pieces, y_near, y_far)
+    before, after, lag = lax.optimization_barrier((before, after, lag))
 
     sums = pl.pallas_call(
         functools.partial(join_kernel, scale=scale),
-        in_specs=[whole] * 5,
+        in_specs=[smem] + [whole] * 5,
         out_specs=whole,
         out_shape=jax.ShapeDtypeStruct((local, WIDE), F32),
         compiler_params=params,
         name="joins",
-    )(rate_row, root_row, ends, after, lag)
+    )(q_arr, rate_row, root_row, ends, after, lag)
 
     back = []
     parts = PARTS
+    q_next = q_arr
     for h in range(parts):
         sh = specs(h * (steps // parts))
         so = specs()
@@ -414,13 +450,17 @@
             compiler_params=params,
             name="convs",
         )(
-            q_arr, rate_wide, gain_wide, rate_row, table, carried, returned, before, after,
+            q_next, rate_wide, gain_wide, rate_row, table, carried, returned, before, after,
             *pieces, *halo,
         )
+        outs = list(outs)
+        outs[0], q_next = lax.optimization_barrier((outs[0], q_arr))
         back += [outs[0]] + [swap(outs[m], m) for m in range(1, ranks)]
 
     hop = 1
     while hop < units:
+        if hop == 2:
+            back[2], back[3], sums = lax.optimization_barrier((back[2], back[3], sums))
         sums = sums + swap(sums, hop * ranks)
         hop *= 2
     parts_of = [sums] + [swap(sums, m) for m in range(1, ranks)]

time: 81.7 us -> 67.8 us (0.83)
  waiting for transfers between devices: 27.7 us -> 19.5 us
  starting transfers between devices: 28.5 us -> 24.3 us
  other arithmetic: 3.26 us -> 2.3 us
    ppermute x6 -> x4, waiting for transfers between devices: 12.8 us -> 4.27 us  [shift(): lax.ppermute(value, 'ctx', [(i, i + by) for i in range(devices) if 0 <= i...]
    ppermute x6 -> x4, starting transfers between devices: 16.6 us -> 11.1 us  [shift(): lax.ppermute(value, 'ctx', [(i, i + by) for i in range(devices) if 0 <= i...]
    ppermute x14 -> x15, starting transfers between devices: 11.9 us -> 13.2 us  [swap(): return lax.ppermute(value, 'ctx', [(i, i ^ m) for i in range(devices)])]
    pallas_call x1, Pallas kernels: 7.23 us -> 6 us  [body(): pl.pallas_call(functools.partial(lag_kernel, scale=scale), grid=(steps,),...]
    add x2, other arithmetic: 1 us -> 0.02 us  [body(): sums = sums + swap(sums, hop * ranks)]
    ppermute x14 -> x15, waiting for transfers between devices: 14.9 us -> 15.3 us  [swap(): return lax.ppermute(value, 'ctx', [(i, i ^ m) for i in range(devices)])]
    another operation x4 -> x5, other arithmetic: 1.97 us -> 2.05 us  [part(): jnp.stack([(cut(key_in) * cut(value_in)).astype(BF16), (cut(grad_out) * c...]
  transfers between devices with their start and end apart: 20 -> 19, of which waited for: 9 -> 9; matrix products, arithmetic and copies ran while one was open for 2% -> 1% of each run, Pallas kernels for 21% -> 21%
where the time goes in v2:
time: 67.8 us; the launch traced here: 67.6 us
  starting transfers between devices  24.3 us (36%)
  Pallas kernels  19.7 us (29%)
  waiting for transfers between devices  19.5 us (29%)
  other arithmetic  2.3 us (3%)
  between operations  0.97 us (1%)
  local copies, waits for them, and re-layouts  0.74 us (1%)
    ppermute x15, waiting for transfers between devices, swap(): return lax.ppermute(value, 'ctx', [(i, i ^ m) for i in range(devices)])  15.3 us
    ppermute x15, starting transfers between devices, swap(): return lax.ppermute(value, 'ctx', [(i, i ^ m) for i in range(devices)])  13.2 us
    ppermute x4, starting transfers between devices, shift(): lax.ppermute(value, 'ctx', [(i, i + by) for i in range(devices) if 0 <= i...  11.1 us
    pallas_call x1, Pallas kernels, body(): pl.pallas_call(functools.partial(lag_kernel, scale=scale), grid=(steps,),...  6 us
    pallas_call x2, Pallas kernels, body(): pl.pallas_call(main_kernel, grid=(steps // parts,), in_specs=[smem, sh['g...  4.55 us
    ppermute x4, waiting for transfers between devices, shift(): lax.ppermute(value, 'ctx', [(i, i + by) for i in range(devices) if 0 <= i...  4.27 us
    pallas_call x1, Pallas kernels, body(): pl.pallas_call(table_kernel, grid=(steps,), in_specs=[sp['row'], sp['grou...  3.87 us
    pallas_call x1, Pallas kernels, body(): pl.pallas_call(state_kernel, grid=(steps,), in_specs=[smem, sp['group'],...  2.86 us
  transfers between devices with their start and end apart: 19, of which 9 were waited for; matrix products, arithmetic and copies ran while one was open for 1% of the time, Pallas kernels for 21%

profile of v2, /device:TPU:0, one launch (start us, length us, event | category | flops | bytes accessed | tf_op | source)
XLA Modules:
  0.0 67.6 jit_solution(18368547240498261214)
XLA Ops:
  0.6 0.0 copy-start
  0.7 1.9 %fusion.5 = (bf16[1,512,128]{2,1,0:T(8,128)(2,1)S(1)}, bf16[1,512,128]{2,1,0:T(8,128)(2,1)S(1)}, bf16[1,512,128]{2,1,0:T(8,128)(2,1)S(1)}, bf16[1,512,128]{2,1,0...) fusion(bf16[2048,128]{1,0:T(8,128)(2,1)} %refs_9_.1, ...), kind=kLoop, calls=%fused_computation.21 | loop fusion | flops 2097152 | bytes 3145744 | tf_op jit(solution)/shard_map/stack | solution.py:312
  2.6 0.5 collective-permute-start.2
  3.2 2.6 %collective-permute-start = (bf16[2,512,128]{2,1,0:T(8,128)(2,1)S(1)}, bf16[2,512,128]{2,1,0:T(8,128)(2,1)S(1)}, u32[]{:S(2)}, u32[]{:S(2)}) collective-permute-start(bf16[2,512,128]{2,1,0:T(8,128)(2,1)S(1)} %pad_maximum_fusion.2), channel_id=1, source_target_pairs={{0,4},{2,6},{4,0},{6,2},{8,12},{10,14},{12,8},{14,10},{16,20},{18,... | collective-permute-start | bytes 786440 | tf_op jit(solution)/shard_map/ppermute | solution.py:300
  5.8 0.2 collective-permute-start.1
  6.0 0.1 pad_maximum_fusion
  6.1 1.3 %collective-permute-start.4 = (bf16[2,512,128]{2,1,0:T(8,128)(2,1)S(1)}, bf16[2,512,128]{2,1,0:T(8,128)(2,1)S(1)}, u32[]{:S(2)}, u32[]{:S(2)}) collective-permute-start(bf16[2,512,128]{2,1,0:T(8,128)(2,1)S(1)} %get-tuple-element.90), channel_id=1, source_target_pairs={{8,0},{10,2},{12,4},{14,6},{16,8},{18,10},{20,12},{22,14},{24,16},... | collective-permute-start | bytes 786440 | tf_op jit(solution)/shard_map/ppermute | solution.py:304
  7.4 4.6 %collective-permute-start.3 = (bf16[2,512,128]{2,1,0:T(8,128)(2,1)S(1)}, bf16[2,512,128]{2,1,0:T(8,128)(2,1)S(1)}, u32[]{:S(2)}, u32[]{:S(2)}) collective-permute-start(bf16[2,512,128]{2,1,0:T(8,128)(2,1)S(1)} %get-tuple-element.91), channel_id=1, source_target_pairs={{0,8},{2,10},{4,12},{6,14},{8,16},{10,18},{12,20},{14,22},{16,24},... | collective-permute-start | bytes 786440 | tf_op jit(solution)/shard_map/ppermute | solution.py:304
  11.9 0.1 sqrt_bitcast_fusion
  12.0 0.1 copy.17
  12.1 0.1 broadcast_in_dim.30
  12.2 0.1 copy.14
  12.3 0.1 broadcast_in_dim.28
  12.4 0.6 collective-permute-done.p2
  12.9 5.2 %collective-permute-done.1.p3 = bf16[2,512,128]{2,1,0:T(8,128)(2,1)S(1)} collective-permute-done((bf16[2,512,128]{2,1,0:T(8,128)(2,1)S(1)}, bf16[2,512,128]{2,1,0:T(8,128)(2,1)S(1)}, u32[]{:S(2)}, u32[]{:S(2)}) %collective-permute-start.1) | collective-permute-done | bytes 262176 | tf_op jit(solution)/shard_map/ppermute | solution.py:300
  18.3 4.0 %collective-permute-start.5 = (bf16[2,512,128]{2,1,0:T(8,128)(2,1)S(1)}, bf16[2,512,128]{2,1,0:T(8,128)(2,1)S(1)}, u32[]{:S(2)}, u32[]{:S(2)}) collective-permute-start(bf16[2,512,128]{2,1,0:T(8,128)(2,1)S(1)} %pad_maximum_fusion.6), channel_id=1, source_target_pairs={{0,8},{2,10},{4,12},{6,14},{8,16},{10,18},{12,20},{14,22},{16,24},... | collective-permute-start | bytes 786440 | tf_op jit(solution)/shard_map/ppermute | solution.py:304
  22.3 1.3 %collective-permute-start.6 = (bf16[2,512,128]{2,1,0:T(8,128)(2,1)S(1)}, bf16[2,512,128]{2,1,0:T(8,128)(2,1)S(1)}, u32[]{:S(2)}, u32[]{:S(2)}) collective-permute-start(bf16[2,512,128]{2,1,0:T(8,128)(2,1)S(1)} %pad_maximum_fusion.7), channel_id=1, source_target_pairs={{8,0},{10,2},{12,4},{14,6},{16,8},{18,10},{20,12},{22,14},{24,16},... | collective-permute-start | bytes 786440 | tf_op jit(solution)/shard_map/ppermute | solution.py:304
  23.6 0.1 bitcast_multiply_fusion
  23.7 0.1 copy.15
  23.8 0.1 broadcast_in_dim.12.rate_ref
  23.9 0.1 broadcast_in_dim.13.gain_ref
  24.0 3.9 %tables.1 = (bf16[32,128,640]{2,1,0:T(8,128)(2,1)S(1)}, f32[4,8,128]{2,1,0:T(8,128)S(1)}) custom-call(f32[4,8,128]{2,1,0:T(8,128)S(1)} %broadcast_in_dim.29.row_ref, f32[32,16,128]{2,1,0:T(8,128)S(1)} %broadcast_in_dim.12.rate_ref, f32[32,16,128]{2,1,0:T(8,128)S(1)} %broadcast_in_dim.13.gain_ref, bf16[32,512]{1,0:T(8,128)(2,1)S(1)} %constant_dynamic-slice_fusion.med_ref), custom_call_target="tpu_custom_call" | custom-call | tf_op jit(solution)/shard_map/tables/pallas_call | solution.py:367
  27.9 0.1 collective-permute-done.5.xb
  28.0 4.2 %collective-permute-done.6.yb = bf16[2,512,128]{2,1,0:T(8,128)(2,1)S(1)} collective-permute-done((bf16[2,512,128]{2,1,0:T(8,128)(2,1)S(1)}, bf16[2,512,128]{2,1,0:T(8,128)(2,1)S(1)}, u32[]{:S(2)}, u32[]{:S(2)}) %collective-permute-start.6) | collective-permute-done | bytes 262176 | tf_op jit(solution)/shard_map/ppermute | solution.py:304
  32.2 2.9 %states.1 = (bf16[4,3,128,128]{3,2,1,0:T(8,128)(2,1)S(1)}, bf16[4,3,128,128]{3,2,1,0:T(8,128)(2,1)S(1)}, f32[4,16,128]{2,1,0:T(8,128)S(1)}, f32[4,16,128]{2,1,0:...) custom-call(s32[1]{0:T(128)} %bitcast.q_ref, ...), custom_call_target="tpu_custom_call" | custom-call | tf_op jit(solution)/shard_map/states/pallas_call | solution.py:384
  35.0 2.6 %collective-permute-start.7 = (f32[4,16,128]{2,1,0:T(8,128)S(1)}, f32[4,16,128]{2,1,0:T(8,128)S(1)}, u32[]{:S(2)}, u32[]{:S(2)}) collective-permute-start(f32[4,16,128]{2,1,0:T(8,128)S(1)} %get-tuple-element.49), channel_id=1, source_target_pairs={{0,16},{2,18},{4,20},{6,22},{8,24},{10,26},{12,28},{14,30},{16,0},... | collective-permute-start | bytes 98312 | tf_op jit(solution)/shard_map/ppermute | solution.py:300
  37.6 6.0 %lags.1.lag_ref = f32[32,640]{1,0:T(8,128)S(1)} custom-call(s32[1]{0:T(128)} %bitcast.q_ref, f32[32,16,128]{2,1,0:T(8,128)S(1)} %broadcast_in_dim.12.rate_ref, f32[4,8,128]{2,1,0:T(8,128)S(1)} %get-tuple-element.41.row_ref, f32[4,8,128]{2,1,0:T(8,128)S(1)} %broadcast_in_dim.31.root_ref, f32[4,16,128]{2,1,0:T(8,128)S(1)} %get-tuple-element.51.cross_ref, ...), custom_call_target="tpu_custom_call" | custom-call | tf_op jit(solution)/shard_map/lags/pallas_call | solution.py:409
  43.6 2.3 %convs.2 = (bf16[2,256,128]{2,1,0:T(8,128)(2,1)S(1)}, bf16[2,256,128]{2,1,0:T(8,128)(2,1)S(1)}, bf16[2,256,128]{2,1,0:T(8,128)(2,1)S(1)}, bf16[2,256,128]{2,1,0:T(8,128)(2,1)S(1)}) custom-call(s32[1]{0:T(128)} %bitcast.q_ref, f32[32,16,128]{2,1,0:T(8,128)S(1)} %broadcast_in_dim.12.rate_ref, f32[32,16,128]{2,1,0:T(8,128)S(1)} %broadcast_in_dim.13.gain_ref, ...), custom_call_target="tpu_custom_call" | custom-call | tf_op jit(solution)/shard_map/convs/pallas_call | solution.py:440
  45.9 0.0 copy-start.1
  45.9 0.0 copy-start.3
  46.0 1.5 %collective-permute-start.9 = (bf16[2,256,128]{2,1,0:T(8,128)(2,1)S(1)}, bf16[2,256,128]{2,1,0:T(8,128)(2,1)S(1)}, u32[]{:S(2)}, u32[]{:S(2)}) collective-permute-start(bf16[2,256,128]{2,1,0:T(8,128)(2,1)S(1)} %get-tuple-element.57), channel_id=1, source_target_pairs={{0,4},{2,6},{4,0},{6,2},{8,12},{10,14},{12,8},{14,10},{16,20},{18,... | collective-permute-start | bytes 393224 | tf_op jit(solution)/shard_map/ppermute | solution.py:300
  47.5 0.2 joins.1
  47.7 0.0 collective-permute-start.11
  47.8 2.3 %convs.3 = (bf16[2,256,128]{2,1,0:T(8,128)(2,1)S(1)}, bf16[2,256,128]{2,1,0:T(8,128)(2,1)S(1)}, bf16[2,256,128]{2,1,0:T(8,128)(2,1)S(1)}, bf16[2,256,128]{2,1,0:T(8,128)(2,1)S(1)}) custom-call(s32[1]{0:T(128)} %bitcast.q_ref, f32[32,16,128]{2,1,0:T(8,128)S(1)} %broadcast_in_dim.12.rate_ref, f32[32,16,128]{2,1,0:T(8,128)S(1)} %broadcast_in_dim.13.gain_ref, ...), custom_call_target="tpu_custom_call" | custom-call | tf_op jit(solution)/shard_map/convs/pallas_call | solution.py:440
  50.0 0.7 %collective-permute-start.12 = (bf16[2,256,128]{2,1,0:T(8,128)(2,1)S(1)}, bf16[2,256,128]{2,1,0:T(8,128)(2,1)S(1)}, u32[]{:S(2)}, u32[]{:S(2)}) collective-permute-start(bf16[2,256,128]{2,1,0:T(8,128)(2,1)S(1)} %get-tuple-element.66), channel_id=1, source_target_pairs={{0,2},{2,0},{4,6},{6,4},{8,10},{10,8},{12,14},{14,12},{16,18},{18,... | collective-permute-start | bytes 393224 | tf_op jit(solution)/shard_map/ppermute | solution.py:300
  50.8 1.5 %collective-permute-start.13 = (bf16[2,256,128]{2,1,0:T(8,128)(2,1)S(1)}, bf16[2,256,128]{2,1,0:T(8,128)(2,1)S(1)}, u32[]{:S(2)}, u32[]{:S(2)}) collective-permute-start(bf16[2,256,128]{2,1,0:T(8,128)(2,1)S(1)} %get-tuple-element.67), channel_id=1, source_target_pairs={{0,4},{2,6},{4,0},{6,2},{8,12},{10,14},{12,8},{14,10},{16,20},{18,... | collective-permute-start | bytes 393224 | tf_op jit(solution)/shard_map/ppermute | solution.py:300
  52.3 0.5 collective-permute-done.11
  52.8 0.5 collective-permute-done.10.refs_3_
  53.3 0.7 collective-permute-start.15
  53.9 1.0 %collective-permute-start.14 = (bf16[2,256,128]{2,1,0:T(8,128)(2,1)S(1)}, bf16[2,256,128]{2,1,0:T(8,128)(2,1)S(1)}, u32[]{:S(2)}, u32[]{:S(2)}) collective-permute-start(bf16[2,256,128]{2,1,0:T(8,128)(2,1)S(1)} %get-tuple-element.68), channel_id=1, source_target_pairs={{0,6},{2,4},{4,2},{6,0},{8,14},{10,12},{12,10},{14,8},{16,22},{18,... | collective-permute-start | bytes 393224 | tf_op jit(solution)/shard_map/ppermute | solution.py:300
  54.9 5.4 %collective-permute-done.15 = f32[32,640]{1,0:T(8,128)S(1)} collective-permute-done((f32[32,640]{1,0:T(8,128)S(1)}, f32[32,640]{1,0:T(8,128)S(1)}, u32[]{:S(2)}, u32[]{:S(2)}) %collective-permute-start.15) | collective-permute-done | bytes 81952 | tf_op jit(solution)/shard_map/ppermute | solution.py:300
  60.3 0.4 collective-permute-start.18
  60.7 1.3 %collective-permute-start.17 = (f32[32,640]{1,0:T(8,128)S(1)}, f32[32,640]{1,0:T(8,128)S(1)}, u32[]{:S(2)}, u32[]{:S(2)}) collective-permute-start(f32[32,640]{1,0:T(8,128)S(1)} %add.53.s0), channel_id=1, source_target_pairs={{0,4},{2,6},{4,0},{6,2},{8,12},{10,14},{12,8},{14,10},{16,20},{18,... | collective-permute-start | bytes 245768 | tf_op jit(solution)/shard_map/ppermute | solution.py:300
  62.0 0.2 collective-permute-start.16
  62.3 1.5 %gates.1 = (bf16[2048,128]{1,0:T(8,128)(2,1)}, bf16[2048,128]{1,0:T(8,128)(2,1)}, bf16[2048,128]{1,0:T(8,128)(2,1)}) custom-call(s32[1]{0:T(128)} %bitcast.q_ref, bf16[2,256,128]{2,1,0:T(8,128)(2,1)S(1)} %get-tuple-element.55.refs_0_, bf16[2,256,128]{2,1,0:T(8,128)(2,1)S(1)} %collective-permute-done.8.refs_1_, ...), custom_call_target="tpu_custom_call" | custom-call | tf_op jit(solution)/shard_map/gates/pallas_call | solution.py:468
  63.8 1.1 %collective-permute-done.18.s3 = f32[32,640]{1,0:T(8,128)S(1)} collective-permute-done((f32[32,640]{1,0:T(8,128)S(1)}, f32[32,640]{1,0:T(8,128)S(1)}, u32[]{:S(2)}, u32[]{:S(2)}) %collective-permute-start.18) | collective-permute-done | bytes 81952 | tf_op jit(solution)/shard_map/ppermute | solution.py:300
  64.9 2.0 %collective-permute-done.17.s2 = f32[32,640]{1,0:T(8,128)S(1)} collective-permute-done((f32[32,640]{1,0:T(8,128)S(1)}, f32[32,640]{1,0:T(8,128)S(1)}, u32[]{:S(2)}, u32[]{:S(2)}) %collective-permute-start.17) | collective-permute-done | bytes 81952 | tf_op jit(solution)/shard_map/ppermute | solution.py:300
  66.9 0.7 %sums.1 = (f32[128,512]{1,0:T(8,128)}, f32[16,128]{1,0:T(8,128)}) custom-call(s32[1]{0:T(128)} %bitcast.q_ref, f32[32,640]{1,0:T(8,128)S(1)} %add.53.s0, f32[32,640]{1,0:T(8,128)S(1)} %collective-permute-done.16.s1, f32[32,640]{1,0:T(8,128)S(1)} %collective-permute-done.17.s2, f32[32,640]{1,0:T(8,128)S(1)} %collective-permute-done.18.s3), custom_call_target="tpu_custom_call" | custom-call | tf_op jit(solution)/shard_map/sums/pallas_call | solution.py:476
  (34 shorter events, 0.3 us)
Async XLA Ops:
  0.6 23.1 %copy-start = (bf16[128,512]{1,0:T(8,128)(2,1)S(1)}, bf16[128,512]{1,0:T(8,128)(2,1)}, u32[]{:S(2)}) copy-start(bf16[128,512]{1,0:T(8,128)(2,1)} %param.11) | copy-start | bytes 393220
  0.6 11.3 %copy-start.4 = (f32[16,128]{1,0:T(8,128)S(1)}, f32[16,128]{1,0:T(8,128)}, u32[]{:S(2)}) copy-start(f32[16,128]{1,0:T(8,128)} %param.13) | copy-start | bytes 24580
  0.7 22.9 %copy-start.5 = (f32[16,128]{1,0:T(8,128)S(1)}, f32[16,128]{1,0:T(8,128)}, u32[]{:S(2)}) copy-start(f32[16,128]{1,0:T(8,128)} %param.12) | copy-start | bytes 24580
  2.6 3.3 %collective-permute-start.2 = (bf16[2,512,128]{2,1,0:T(8,128)(2,1)S(1)}, bf16[2,512,128]{2,1,0:T(8,128)(2,1)S(1)}, u32[]{:S(2)}, u32[]{:S(2)}) collective-permute-start(bf16[2,512,128]{2,1,0:T(8,128)(2,1)S(1)} %pad_maximum_fusion.4), channel_id=1, source_target_pairs={{0,2},{2,0},{4,6},{6,4},{8,10},{10,8},{12,14},{14,12},{16,18},{18,... | collective-permute-start | bytes 786440 | tf_op jit(solution)/shard_map/ppermute | solution.py:300
  3.2 9.7 %collective-permute-start = (bf16[2,512,128]{2,1,0:T(8,128)(2,1)S(1)}, bf16[2,512,128]{2,1,0:T(8,128)(2,1)S(1)}, u32[]{:S(2)}, u32[]{:S(2)}) collective-permute-start(bf16[2,512,128]{2,1,0:T(8,128)(2,1)S(1)} %pad_maximum_fusion.2), channel_id=1, source_target_pairs={{0,4},{2,6},{4,0},{6,2},{8,12},{10,14},{12,8},{14,10},{16,20},{18,... | collective-permute-start | bytes 786440 | tf_op jit(solution)/shard_map/ppermute | solution.py:300
  5.8 12.3 %collective-permute-start.1 = (bf16[2,512,128]{2,1,0:T(8,128)(2,1)S(1)}, bf16[2,512,128]{2,1,0:T(8,128)(2,1)S(1)}, u32[]{:S(2)}, u32[]{:S(2)}) collective-permute-start(bf16[2,512,128]{2,1,0:T(8,128)(2,1)S(1)} %pad_maximum_fusion.3), channel_id=1, source_target_pairs={{0,6},{2,4},{4,2},{6,0},{8,14},{10,12},{12,10},{14,8},{16,22},{18,... | collective-permute-start | bytes 786440 | tf_op jit(solution)/shard_map/ppermute | solution.py:300
  6.1 12.1 %collective-permute-start.4 = (bf16[2,512,128]{2,1,0:T(8,128)(2,1)S(1)}, bf16[2,512,128]{2,1,0:T(8,128)(2,1)S(1)}, u32[]{:S(2)}, u32[]{:S(2)}) collective-permute-start(bf16[2,512,128]{2,1,0:T(8,128)(2,1)S(1)} %get-tuple-element.90), channel_id=1, source_target_pairs={{8,0},{10,2},{12,4},{14,6},{16,8},{18,10},{20,12},{22,14},{24,16},... | collective-permute-start | bytes 786440 | tf_op jit(solution)/shard_map/ppermute | solution.py:304
  7.4 10.8 %collective-permute-start.3 = (bf16[2,512,128]{2,1,0:T(8,128)(2,1)S(1)}, bf16[2,512,128]{2,1,0:T(8,128)(2,1)S(1)}, u32[]{:S(2)}, u32[]{:S(2)}) collective-permute-start(bf16[2,512,128]{2,1,0:T(8,128)(2,1)S(1)} %get-tuple-element.91), channel_id=1, source_target_pairs={{0,8},{2,10},{4,12},{6,14},{8,16},{10,18},{12,20},{14,22},{16,24},... | collective-permute-start | bytes 786440 | tf_op jit(solution)/shard_map/ppermute | solution.py:304
  18.3 9.8 %collective-permute-start.5 = (bf16[2,512,128]{2,1,0:T(8,128)(2,1)S(1)}, bf16[2,512,128]{2,1,0:T(8,128)(2,1)S(1)}, u32[]{:S(2)}, u32[]{:S(2)}) collective-permute-start(bf16[2,512,128]{2,1,0:T(8,128)(2,1)S(1)} %pad_maximum_fusion.6), channel_id=1, source_target_pairs={{0,8},{2,10},{4,12},{6,14},{8,16},{10,18},{12,20},{14,22},{16,24},... | collective-permute-start | bytes 786440 | tf_op jit(solution)/shard_map/ppermute | solution.py:304
  22.3 9.9 %collective-permute-start.6 = (bf16[2,512,128]{2,1,0:T(8,128)(2,1)S(1)}, bf16[2,512,128]{2,1,0:T(8,128)(2,1)S(1)}, u32[]{:S(2)}, u32[]{:S(2)}) collective-permute-start(bf16[2,512,128]{2,1,0:T(8,128)(2,1)S(1)} %pad_maximum_fusion.7), channel_id=1, source_target_pairs={{8,0},{10,2},{12,4},{14,6},{16,8},{18,10},{20,12},{22,14},{24,16},... | collective-permute-start | bytes 786440 | tf_op jit(solution)/shard_map/ppermute | solution.py:304
  35.0 8.6 %collective-permute-start.7 = (f32[4,16,128]{2,1,0:T(8,128)S(1)}, f32[4,16,128]{2,1,0:T(8,128)S(1)}, u32[]{:S(2)}, u32[]{:S(2)}) collective-permute-start(f32[4,16,128]{2,1,0:T(8,128)S(1)} %get-tuple-element.49), channel_id=1, source_target_pairs={{0,16},{2,18},{4,20},{6,22},{8,24},{10,26},{12,28},{14,30},{16,0},... | collective-permute-start | bytes 98312 | tf_op jit(solution)/shard_map/ppermute | solution.py:300
  45.9 16.3 %copy-start.1 = (bf16[2048,128]{1,0:T(8,128)(2,1)S(1)}, bf16[2048,128]{1,0:T(8,128)(2,1)}, u32[]{:S(2)}) copy-start(bf16[2048,128]{1,0:T(8,128)(2,1)} %refs_9_.1) | copy-start | bytes 1572868
  45.9 16.3 %copy-start.2 = (bf16[2048,128]{1,0:T(8,128)(2,1)S(1)}, bf16[2048,128]{1,0:T(8,128)(2,1)}, u32[]{:S(2)}) copy-start(bf16[2048,128]{1,0:T(8,128)(2,1)} %refs_10_.1) | copy-start | bytes 1572868
  45.9 16.3 %copy-start.3 = (bf16[2048,128]{1,0:T(8,128)(2,1)S(1)}, bf16[2048,128]{1,0:T(8,128)(2,1)}, u32[]{:S(2)}) copy-start(bf16[2048,128]{1,0:T(8,128)(2,1)} %refs_8_.1) | copy-start | bytes 1572868
  46.0 6.8 %collective-permute-start.9 = (bf16[2,256,128]{2,1,0:T(8,128)(2,1)S(1)}, bf16[2,256,128]{2,1,0:T(8,128)(2,1)S(1)}, u32[]{:S(2)}, u32[]{:S(2)}) collective-permute-start(bf16[2,256,128]{2,1,0:T(8,128)(2,1)S(1)} %get-tuple-element.57), channel_id=1, source_target_pairs={{0,4},{2,6},{4,0},{6,2},{8,12},{10,14},{12,8},{14,10},{16,20},{18,... | collective-permute-start | bytes 393224 | tf_op jit(solution)/shard_map/ppermute | solution.py:300
  47.5 5.8 %collective-permute-start.10 = (bf16[2,256,128]{2,1,0:T(8,128)(2,1)S(1)}, bf16[2,256,128]{2,1,0:T(8,128)(2,1)S(1)}, u32[]{:S(2)}, u32[]{:S(2)}) collective-permute-start(bf16[2,256,128]{2,1,0:T(8,128)(2,1)S(1)} %get-tuple-element.58), channel_id=1, source_target_pairs={{0,6},{2,4},{4,2},{6,0},{8,14},{10,12},{12,10},{14,8},{16,22},{18,... | collective-permute-start | bytes 393224 | tf_op jit(solution)/shard_map/ppermute | solution.py:300
  47.7 5.0 %collective-permute-start.11 = (f32[32,640]{1,0:T(8,128)S(1)}, f32[32,640]{1,0:T(8,128)S(1)}, u32[]{:S(2)}, u32[]{:S(2)}) collective-permute-start(f32[32,640]{1,0:T(8,128)S(1)} %joins.1), channel_id=1, source_target_pairs={{0,8},{2,10},{4,12},{6,14},{8,0},{10,2},{12,4},{14,6},{16,24},{18,... | collective-permute-start | bytes 245768 | tf_op jit(solution)/shard_map/ppermute | solution.py:300
  50.0 10.7 %collective-permute-start.12 = (bf16[2,256,128]{2,1,0:T(8,128)(2,1)S(1)}, bf16[2,256,128]{2,1,0:T(8,128)(2,1)S(1)}, u32[]{:S(2)}, u32[]{:S(2)}) collective-permute-start(bf16[2,256,128]{2,1,0:T(8,128)(2,1)S(1)} %get-tuple-element.66), channel_id=1, source_target_pairs={{0,2},{2,0},{4,6},{6,4},{8,10},{10,8},{12,14},{14,12},{16,18},{18,... | collective-permute-start | bytes 393224 | tf_op jit(solution)/shard_map/ppermute | solution.py:300
  50.8 11.3 %collective-permute-start.13 = (bf16[2,256,128]{2,1,0:T(8,128)(2,1)S(1)}, bf16[2,256,128]{2,1,0:T(8,128)(2,1)S(1)}, u32[]{:S(2)}, u32[]{:S(2)}) collective-permute-start(bf16[2,256,128]{2,1,0:T(8,128)(2,1)S(1)} %get-tuple-element.67), channel_id=1, source_target_pairs={{0,4},{2,6},{4,0},{6,2},{8,12},{10,14},{12,8},{14,10},{16,20},{18,... | collective-permute-start | bytes 393224 | tf_op jit(solution)/shard_map/ppermute | solution.py:300
  53.3 7.0 %collective-permute-start.15 = (f32[32,640]{1,0:T(8,128)S(1)}, f32[32,640]{1,0:T(8,128)S(1)}, u32[]{:S(2)}, u32[]{:S(2)}) collective-permute-start(f32[32,640]{1,0:T(8,128)S(1)} %add.52), channel_id=1, source_target_pairs={{0,16},{2,18},{4,20},{6,22},{8,24},{10,26},{12,28},{14,30},{16,0},... | collective-permute-start | bytes 245768 | tf_op jit(solution)/shard_map/ppermute | solution.py:300
  53.9 8.3 %collective-permute-start.14 = (bf16[2,256,128]{2,1,0:T(8,128)(2,1)S(1)}, bf16[2,256,128]{2,1,0:T(8,128)(2,1)S(1)}, u32[]{:S(2)}, u32[]{:S(2)}) collective-permute-start(bf16[2,256,128]{2,1,0:T(8,128)(2,1)S(1)} %get-tuple-element.68), channel_id=1, source_target_pairs={{0,6},{2,4},{4,2},{6,0},{8,14},{10,12},{12,10},{14,8},{16,22},{18,... | collective-permute-start | bytes 393224 | tf_op jit(solution)/shard_map/ppermute | solution.py:300
  54.9 7.3 %collective-permute-start.8 = (bf16[2,256,128]{2,1,0:T(8,128)(2,1)S(1)}, bf16[2,256,128]{2,1,0:T(8,128)(2,1)S(1)}, u32[]{:S(2)}, u32[]{:S(2)}) collective-permute-start(bf16[2,256,128]{2,1,0:T(8,128)(2,1)S(1)} %get-tuple-element.56), channel_id=1, source_target_pairs={{0,2},{2,0},{4,6},{6,4},{8,10},{10,8},{12,14},{14,12},{16,18},{18,... | collective-permute-start | bytes 393224 | tf_op jit(solution)/shard_map/ppermute | solution.py:300
  60.3 4.6 %collective-permute-start.18 = (f32[32,640]{1,0:T(8,128)S(1)}, f32[32,640]{1,0:T(8,128)S(1)}, u32[]{:S(2)}, u32[]{:S(2)}) collective-permute-start(f32[32,640]{1,0:T(8,128)S(1)} %add.53.s0), channel_id=1, source_target_pairs={{0,6},{2,4},{4,2},{6,0},{8,14},{10,12},{12,10},{14,8},{16,22},{18,... | collective-permute-start | bytes 245768 | tf_op jit(solution)/shard_map/ppermute | solution.py:300
  60.7 6.1 %collective-permute-start.17 = (f32[32,640]{1,0:T(8,128)S(1)}, f32[32,640]{1,0:T(8,128)S(1)}, u32[]{:S(2)}, u32[]{:S(2)}) collective-permute-start(f32[32,640]{1,0:T(8,128)S(1)} %add.53.s0), channel_id=1, source_target_pairs={{0,4},{2,6},{4,0},{6,2},{8,12},{10,14},{12,8},{14,10},{16,20},{18,... | collective-permute-start | bytes 245768 | tf_op jit(solution)/shard_map/ppermute | solution.py:300
  62.0 4.8 %collective-permute-start.16 = (f32[32,640]{1,0:T(8,128)S(1)}, f32[32,640]{1,0:T(8,128)S(1)}, u32[]{:S(2)}, u32[]{:S(2)}) collective-permute-start(f32[32,640]{1,0:T(8,128)S(1)} %add.53.s0), channel_id=1, source_target_pairs={{0,2},{2,0},{4,6},{6,4},{8,10},{10,8},{12,14},{14,12},{16,18},{18,... | collective-permute-start | bytes 245768 | tf_op jit(solution)/shard_map/ppermute | solution.py:300

commit v3 on v2

--- a/solution.py
+++ b/solution.py
@@ -260,8 +260,8 @@
     local = s0.shape[0]
     for m, part in enumerate((s0, s1, s2, s3)):
         at = pl.ds(pl.multiple_of((q ^ m) * local, local), local)
-        med_ref[at, :] = part[:, : SPAN * BLK]
-        turned[at, :] = part[:, SPAN * BLK :]
+        med_ref[at, :] = part[:, : SPAN * BLK].astype(F32)
+        turned[at, :] = part[:, SPAN * BLK :].astype(F32)
     res_ref[...] = turned[...].T[:GROUP]
 
 
@@ -421,15 +421,6 @@
         name="lags",
     )(q_arr, rate_wide, rate_row, root_row, cross, *pieces, y_near, y_far)
     before, after, lag = lax.optimization_barrier((before, after, lag))
-
-    sums = pl.pallas_call(
-        functools.partial(join_kernel, scale=scale),
-        in_specs=[smem] + [whole] * 5,
-        out_specs=whole,
-        out_shape=jax.ShapeDtypeStruct((local, WIDE), F32),
-        compiler_params=params,
-        name="joins",
-    )(q_arr, rate_row, root_row, ends, after, lag)
 
     back = []
     parts = PARTS
@@ -457,12 +448,24 @@
         outs[0], q_next = lax.optimization_barrier((outs[0], q_arr))
         back += [outs[0]] + [swap(outs[m], m) for m in range(1, ranks)]
 
+    back[0], lag = lax.optimization_barrier((back[0], lag))
+    sums = pl.pallas_call(
+        functools.partial(join_kernel, scale=scale),
+        in_specs=[smem] + [whole] * 5,
+        out_specs=whole,
+        out_shape=jax.ShapeDtypeStruct((local, WIDE), F32),
+        compiler_params=params,
+        name="joins",
+    )(q_arr, rate_row, root_row, ends, after, lag)
+
     hop = 1
     while hop < units:
         if hop == 2:
-            back[2], back[3], sums = lax.optimization_barrier((back[2], back[3], sums))
-        sums = sums + swap(sums, hop * ranks)
+            back[4], sums = lax.optimization_barrier((back[4], sums))
+        total = sums.astype(F32) + swap(sums, hop * ranks).astype(F32)
+        sums = lax.reduce_precision(total, 8, 7).astype(BF16)
         hop *= 2
+    back[2], back[3], sums = lax.optimization_barrier((back[2], back[3], sums))
     parts_of = [sums] + [swap(sums, m) for m in range(1, ranks)]
 
     grads = pl.pallas_call(

time: 67.8 us -> 64.8 us (0.956)
  starting transfers between devices: 24.3 us -> 21.6 us
    ppermute x15, starting transfers between devices: 13.2 us -> 11.6 us  [swap(): return lax.ppermute(value, 'ctx', [(i, i ^ m) for i in range(devices)])]
    ppermute x4, starting transfers between devices: 11.1 us -> 10.1 us  [shift(): lax.ppermute(value, 'ctx', [(i, i + by) for i in range(devices) if 0 <= i...]
  transfers between devices with their start and end apart: 19 -> 19, of which waited for: 9 -> 10; matrix products, arithmetic and copies ran while one was open for 1% -> 2% of each run, Pallas kernels for 21% -> 21%
where the time goes in v3:
time: 64.8 us; the launch traced here: 64.6 us
  starting transfers between devices  21.6 us (33%)
  Pallas kernels  19.7 us (30%)
  waiting for transfers between devices  19.2 us (30%)
  other arithmetic  2.31 us (4%)
  between operations  0.96 us (1%)
  local copies, waits for them, and re-layouts  0.74 us (1%)
    ppermute x15, waiting for transfers between devices, swap(): return lax.ppermute(value, 'ctx', [(i, i ^ m) for i in range(devices)])  15.2 us
    ppermute x15, starting transfers between devices, swap(): return lax.ppermute(value, 'ctx', [(i, i ^ m) for i in range(devices)])  11.6 us
    ppermute x4, starting transfers between devices, shift(): lax.ppermute(value, 'ctx', [(i, i + by) for i in range(devices) if 0 <= i...  10.1 us
    pallas_call x1, Pallas kernels, body(): pl.pallas_call(functools.partial(lag_kernel, scale=scale), grid=(steps,),...  5.99 us
    pallas_call x2, Pallas kernels, body(): pl.pallas_call(main_kernel, grid=(steps // parts,), in_specs=[smem, sh['g...  4.55 us
    ppermute x4, waiting for transfers between devices, shift(): lax.ppermute(value, 'ctx', [(i, i + by) for i in range(devices) if 0 <= i...  4.01 us
    pallas_call x1, Pallas kernels, body(): pl.pallas_call(table_kernel, grid=(steps,), in_specs=[sp['row'], sp['grou...  3.87 us
    pallas_call x1, Pallas kernels, body(): pl.pallas_call(state_kernel, grid=(steps,), in_specs=[smem, sp['group'],...  2.86 us
  transfers between devices with their start and end apart: 19, of which 10 were waited for; matrix products, arithmetic and copies ran while one was open for 2% of the time, Pallas kernels for 21%

profile of v3, /device:TPU:0, one launch (start us, length us, event | category | flops | bytes accessed | tf_op | source)
XLA Modules:
  0.0 64.6 jit_solution(10179012845036252610)
XLA Ops:
  0.6 0.0 copy-start
  0.7 1.9 %fusion.5 = (bf16[1,512,128]{2,1,0:T(8,128)(2,1)S(1)}, bf16[1,512,128]{2,1,0:T(8,128)(2,1)S(1)}, bf16[1,512,128]{2,1,0:T(8,128)(2,1)S(1)}, bf16[1,512,128]{2,1,0...) fusion(bf16[2048,128]{1,0:T(8,128)(2,1)} %refs_9_.1, ...), kind=kLoop, calls=%fused_computation.21 | loop fusion | flops 2097152 | bytes 3145744 | tf_op jit(solution)/shard_map/stack | solution.py:312
  2.6 0.5 collective-permute-start.2
  3.2 2.7 %collective-permute-start.1 = (bf16[2,512,128]{2,1,0:T(8,128)(2,1)S(1)}, bf16[2,512,128]{2,1,0:T(8,128)(2,1)S(1)}, u32[]{:S(2)}, u32[]{:S(2)}) collective-permute-start(bf16[2,512,128]{2,1,0:T(8,128)(2,1)S(1)} %pad_maximum_fusion.3), channel_id=1, source_target_pairs={{0,6},{2,4},{4,2},{6,0},{8,14},{10,12},{12,10},{14,8},{16,22},{18,... | collective-permute-start | bytes 786440 | tf_op jit(solution)/shard_map/ppermute | solution.py:300
  5.9 0.1 collective-permute-start
  6.0 0.1 pad_maximum_fusion
  6.1 4.0 %collective-permute-start.3 = (bf16[2,512,128]{2,1,0:T(8,128)(2,1)S(1)}, bf16[2,512,128]{2,1,0:T(8,128)(2,1)S(1)}, u32[]{:S(2)}, u32[]{:S(2)}) collective-permute-start(bf16[2,512,128]{2,1,0:T(8,128)(2,1)S(1)} %get-tuple-element.99), channel_id=1, source_target_pairs={{0,8},{2,10},{4,12},{6,14},{8,16},{10,18},{12,20},{14,22},{16,24},... | collective-permute-start | bytes 786440 | tf_op jit(solution)/shard_map/ppermute | solution.py:304
  10.1 1.3 %collective-permute-start.4 = (bf16[2,512,128]{2,1,0:T(8,128)(2,1)S(1)}, bf16[2,512,128]{2,1,0:T(8,128)(2,1)S(1)}, u32[]{:S(2)}, u32[]{:S(2)}) collective-permute-start(bf16[2,512,128]{2,1,0:T(8,128)(2,1)S(1)} %get-tuple-element.98), channel_id=1, source_target_pairs={{8,0},{10,2},{12,4},{14,6},{16,8},{18,10},{20,12},{22,14},{24,16},... | collective-permute-start | bytes 786440 | tf_op jit(solution)/shard_map/ppermute | solution.py:304
  11.4 0.1 sqrt_bitcast_fusion
  11.5 0.1 copy.14
  11.6 0.1 broadcast_in_dim.28
  11.7 0.1 copy.17
  11.7 0.1 broadcast_in_dim.30
  11.8 0.7 %collective-permute-done.1.p3 = bf16[2,512,128]{2,1,0:T(8,128)(2,1)S(1)} collective-permute-done((bf16[2,512,128]{2,1,0:T(8,128)(2,1)S(1)}, bf16[2,512,128]{2,1,0:T(8,128)(2,1)S(1)}, u32[]{:S(2)}, u32[]{:S(2)}) %collective-permute-start.1) | collective-permute-done | bytes 262176 | tf_op jit(solution)/shard_map/ppermute | solution.py:300
  12.5 5.8 %collective-permute-done.p2 = bf16[2,512,128]{2,1,0:T(8,128)(2,1)S(1)} collective-permute-done((bf16[2,512,128]{2,1,0:T(8,128)(2,1)S(1)}, bf16[2,512,128]{2,1,0:T(8,128)(2,1)S(1)}, u32[]{:S(2)}, u32[]{:S(2)}) %collective-permute-start) | collective-permute-done | bytes 262176 | tf_op jit(solution)/shard_map/ppermute | solution.py:300
  18.3 1.3 %collective-permute-done.4.ya = bf16[2,512,128]{2,1,0:T(8,128)(2,1)S(1)} collective-permute-done((bf16[2,512,128]{2,1,0:T(8,128)(2,1)S(1)}, bf16[2,512,128]{2,1,0:T(8,128)(2,1)S(1)}, u32[]{:S(2)}, u32[]{:S(2)}) %collective-permute-start.4) | collective-permute-done | bytes 262176 | tf_op jit(solution)/shard_map/ppermute | solution.py:304
  19.7 3.5 %collective-permute-start.5 = (bf16[2,512,128]{2,1,0:T(8,128)(2,1)S(1)}, bf16[2,512,128]{2,1,0:T(8,128)(2,1)S(1)}, u32[]{:S(2)}, u32[]{:S(2)}) collective-permute-start(bf16[2,512,128]{2,1,0:T(8,128)(2,1)S(1)} %pad_maximum_fusion.6), channel_id=1, source_target_pairs={{0,8},{2,10},{4,12},{6,14},{8,16},{10,18},{12,20},{14,22},{16,24},... | collective-permute-start | bytes 786440 | tf_op jit(solution)/shard_map/ppermute | solution.py:304
  23.3 1.3 %collective-permute-start.6 = (bf16[2,512,128]{2,1,0:T(8,128)(2,1)S(1)}, bf16[2,512,128]{2,1,0:T(8,128)(2,1)S(1)}, u32[]{:S(2)}, u32[]{:S(2)}) collective-permute-start(bf16[2,512,128]{2,1,0:T(8,128)(2,1)S(1)} %pad_maximum_fusion.7), channel_id=1, source_target_pairs={{8,0},{10,2},{12,4},{14,6},{16,8},{18,10},{20,12},{22,14},{24,16},... | collective-permute-start | bytes 786440 | tf_op jit(solution)/shard_map/ppermute | solution.py:304
  24.6 0.1 bitcast_multiply_fusion
  24.7 0.1 copy.15
  24.8 0.1 broadcast_in_dim.12.rate_ref
  24.9 0.1 broadcast_in_dim.13.gain_ref
  25.0 3.9 %tables.1 = (bf16[32,128,640]{2,1,0:T(8,128)(2,1)S(1)}, f32[4,8,128]{2,1,0:T(8,128)S(1)}) custom-call(f32[4,8,128]{2,1,0:T(8,128)S(1)} %broadcast_in_dim.29.row_ref, f32[32,16,128]{2,1,0:T(8,128)S(1)} %broadcast_in_dim.12.rate_ref, f32[32,16,128]{2,1,0:T(8,128)S(1)} %broadcast_in_dim.13.gain_ref, bf16[32,512]{1,0:T(8,128)(2,1)S(1)} %constant_dynamic-slice_fusion.med_ref), custom_call_target="tpu_custom_call" | custom-call | tf_op jit(solution)/shard_map/tables/pallas_call | solution.py:367
  28.9 2.7 %collective-permute-done.6.yb = bf16[2,512,128]{2,1,0:T(8,128)(2,1)S(1)} collective-permute-done((bf16[2,512,128]{2,1,0:T(8,128)(2,1)S(1)}, bf16[2,512,128]{2,1,0:T(8,128)(2,1)S(1)}, u32[]{:S(2)}, u32[]{:S(2)}) %collective-permute-start.6) | collective-permute-done | bytes 262176 | tf_op jit(solution)/shard_map/ppermute | solution.py:304
  31.6 2.9 %states.1 = (bf16[4,3,128,128]{3,2,1,0:T(8,128)(2,1)S(1)}, bf16[4,3,128,128]{3,2,1,0:T(8,128)(2,1)S(1)}, f32[4,16,128]{2,1,0:T(8,128)S(1)}, f32[4,16,128]{2,1,0:...) custom-call(s32[1]{0:T(128)} %bitcast.q_ref, ...), custom_call_target="tpu_custom_call" | custom-call | tf_op jit(solution)/shard_map/states/pallas_call | solution.py:384
  34.5 2.4 %collective-permute-start.7 = (f32[4,16,128]{2,1,0:T(8,128)S(1)}, f32[4,16,128]{2,1,0:T(8,128)S(1)}, u32[]{:S(2)}, u32[]{:S(2)}) collective-permute-start(f32[4,16,128]{2,1,0:T(8,128)S(1)} %get-tuple-element.53), channel_id=1, source_target_pairs={{0,16},{2,18},{4,20},{6,22},{8,24},{10,26},{12,28},{14,30},{16,0},... | collective-permute-start | bytes 98312 | tf_op jit(solution)/shard_map/ppermute | solution.py:300
  36.9 6.0 %lags.1.lag_ref = f32[32,640]{1,0:T(8,128)S(1)} custom-call(s32[1]{0:T(128)} %bitcast.q_ref, f32[32,16,128]{2,1,0:T(8,128)S(1)} %broadcast_in_dim.12.rate_ref, f32[4,8,128]{2,1,0:T(8,128)S(1)} %get-tuple-element.45.row_ref, f32[4,8,128]{2,1,0:T(8,128)S(1)} %broadcast_in_dim.31.root_ref, f32[4,16,128]{2,1,0:T(8,128)S(1)} %get-tuple-element.55.cross_ref, ...), custom_call_target="tpu_custom_call" | custom-call | tf_op jit(solution)/shard_map/lags/pallas_call | solution.py:409
  42.9 2.3 %convs.2 = (bf16[2,256,128]{2,1,0:T(8,128)(2,1)S(1)}, bf16[2,256,128]{2,1,0:T(8,128)(2,1)S(1)}, bf16[2,256,128]{2,1,0:T(8,128)(2,1)S(1)}, bf16[2,256,128]{2,1,0:T(8,128)(2,1)S(1)}) custom-call(s32[1]{0:T(128)} %bitcast.q_ref, f32[32,16,128]{2,1,0:T(8,128)S(1)} %broadcast_in_dim.12.rate_ref, f32[32,16,128]{2,1,0:T(8,128)S(1)} %broadcast_in_dim.13.gain_ref, ...), custom_call_target="tpu_custom_call" | custom-call | tf_op jit(solution)/shard_map/convs/pallas_call | solution.py:431
  45.2 0.0 copy-start.1
  45.2 0.0 copy-start.2
  45.2 0.0 copy-start.3
  45.2 0.2 joins.1
  45.4 0.0 collective-permute-start.11
  45.5 2.3 %convs.3 = (bf16[2,256,128]{2,1,0:T(8,128)(2,1)S(1)}, bf16[2,256,128]{2,1,0:T(8,128)(2,1)S(1)}, bf16[2,256,128]{2,1,0:T(8,128)(2,1)S(1)}, bf16[2,256,128]{2,1,0:T(8,128)(2,1)S(1)}) custom-call(s32[1]{0:T(128)} %bitcast.q_ref, f32[32,16,128]{2,1,0:T(8,128)S(1)} %broadcast_in_dim.12.rate_ref, f32[32,16,128]{2,1,0:T(8,128)S(1)} %broadcast_in_dim.13.gain_ref, ...), custom_call_target="tpu_custom_call" | custom-call | tf_op jit(solution)/shard_map/convs/pallas_call | solution.py:431
  47.7 0.1 collective-permute-start.10
  47.8 2.1 %collective-permute-done.11 = f32[32,640]{1,0:T(8,128)S(1)} collective-permute-done((f32[32,640]{1,0:T(8,128)S(1)}, f32[32,640]{1,0:T(8,128)S(1)}, u32[]{:S(2)}, u32[]{:S(2)}) %collective-permute-start.11) | collective-permute-done | bytes 81952 | tf_op jit(solution)/shard_map/ppermute | solution.py:300
  49.9 0.6 collective-permute-start.12
  50.5 1.5 %collective-permute-start.9 = (bf16[2,256,128]{2,1,0:T(8,128)(2,1)S(1)}, bf16[2,256,128]{2,1,0:T(8,128)(2,1)S(1)}, u32[]{:S(2)}, u32[]{:S(2)}) collective-permute-start(bf16[2,256,128]{2,1,0:T(8,128)(2,1)S(1)} %get-tuple-element.63), channel_id=1, source_target_pairs={{0,4},{2,6},{4,0},{6,2},{8,12},{10,14},{12,8},{14,10},{16,20},{18,... | collective-permute-start | bytes 393224 | tf_op jit(solution)/shard_map/ppermute | solution.py:300
  52.0 1.0 %collective-permute-start.14 = (bf16[2,256,128]{2,1,0:T(8,128)(2,1)S(1)}, bf16[2,256,128]{2,1,0:T(8,128)(2,1)S(1)}, u32[]{:S(2)}, u32[]{:S(2)}) collective-permute-start(bf16[2,256,128]{2,1,0:T(8,128)(2,1)S(1)} %get-tuple-element.75), channel_id=1, source_target_pairs={{0,4},{2,6},{4,0},{6,2},{8,12},{10,14},{12,8},{14,10},{16,20},{18,... | collective-permute-start | bytes 393224 | tf_op jit(solution)/shard_map/ppermute | solution.py:300
  53.0 2.3 %collective-permute-done.12 = bf16[32,640]{1,0:T(8,128)(2,1)S(1)} collective-permute-done((bf16[32,640]{1,0:T(8,128)(2,1)S(1)}, bf16[32,640]{1,0:T(8,128)(2,1)S(1)}, u32[]{:S(2)}, u32[]{:S(2)}) %collective-permute-start.12) | collective-permute-done | bytes 40992 | tf_op jit(solution)/shard_map/ppermute | solution.py:300
  55.3 1.2 %collective-permute-start.8 = (bf16[2,256,128]{2,1,0:T(8,128)(2,1)S(1)}, bf16[2,256,128]{2,1,0:T(8,128)(2,1)S(1)}, u32[]{:S(2)}, u32[]{:S(2)}) collective-permute-start(bf16[2,256,128]{2,1,0:T(8,128)(2,1)S(1)} %get-tuple-element.62), channel_id=1, source_target_pairs={{0,2},{2,0},{4,6},{6,4},{8,10},{10,8},{12,14},{14,12},{16,18},{18,... | collective-permute-start | bytes 393224 | tf_op jit(solution)/shard_map/ppermute | solution.py:300
  56.5 0.3 collective-permute-done.9.refs_2_
  56.9 1.5 %collective-permute-start.17 = (bf16[32,640]{1,0:T(8,128)(2,1)S(1)}, bf16[32,640]{1,0:T(8,128)(2,1)S(1)}, u32[]{:S(2)}, u32[]{:S(2)}) collective-permute-start(bf16[32,640]{1,0:T(8,128)(2,1)S(1)} %reduce-precision_convert_fusion.s0), channel_id=1, source_target_pairs={{0,4},{2,6},{4,0},{6,2},{8,12},{10,14},{12,8},{14,10},{16,20},{18,... | collective-permute-start | bytes 122888 | tf_op jit(solution)/shard_map/ppermute | solution.py:300
  58.4 1.3 %collective-permute-done.14.refs_6_ = bf16[2,256,128]{2,1,0:T(8,128)(2,1)S(1)} collective-permute-done((bf16[2,256,128]{2,1,0:T(8,128)(2,1)S(1)}, bf16[2,256,128]{2,1,0:T(8,128)(2,1)S(1)}, u32[]{:S(2)}, u32[]{:S(2)}) %collective-permute-start.14) | collective-permute-done | bytes 131104 | tf_op jit(solution)/shard_map/ppermute | solution.py:300
  59.7 2.4 %collective-permute-done.15.refs_7_ = bf16[2,256,128]{2,1,0:T(8,128)(2,1)S(1)} collective-permute-done((bf16[2,256,128]{2,1,0:T(8,128)(2,1)S(1)}, bf16[2,256,128]{2,1,0:T(8,128)(2,1)S(1)}, u32[]{:S(2)}, u32[]{:S(2)}) %collective-permute-start.15) | collective-permute-done | bytes 131104 | tf_op jit(solution)/shard_map/ppermute | solution.py:300
  62.1 1.5 %gates.1 = (bf16[2048,128]{1,0:T(8,128)(2,1)}, bf16[2048,128]{1,0:T(8,128)(2,1)}, bf16[2048,128]{1,0:T(8,128)(2,1)}) custom-call(s32[1]{0:T(128)} %bitcast.q_ref, bf16[2,256,128]{2,1,0:T(8,128)(2,1)S(1)} %get-tuple-element.61.refs_0_, bf16[2,256,128]{2,1,0:T(8,128)(2,1)S(1)} %collective-permute-done.8.refs_1_, ...), custom_call_target="tpu_custom_call" | custom-call | tf_op jit(solution)/shard_map/gates/pallas_call | solution.py:471
  63.6 0.2 collective-permute-done.18.s3
  63.9 0.7 %sums.1 = (f32[128,512]{1,0:T(8,128)}, f32[16,128]{1,0:T(8,128)}) custom-call(s32[1]{0:T(128)} %bitcast.q_ref, bf16[32,640]{1,0:T(8,128)(2,1)S(1)} %reduce-precision_convert_fusion.s0, bf16[32,640]{1,0:T(8,128)(2,1)S(1)} %collective-permute-done.16.s1, bf16[32,640]{1,0:T(8,128)(2,1)S(1)} %collective-permute-done.17.s2, ...), custom_call_target="tpu_custom_call" | custom-call | tf_op jit(solution)/shard_map/sums/pallas_call | solution.py:479
  (34 shorter events, 0.3 us)
Async XLA Ops:
  0.6 24.1 %copy-start = (bf16[128,512]{1,0:T(8,128)(2,1)S(1)}, bf16[128,512]{1,0:T(8,128)(2,1)}, u32[]{:S(2)}) copy-start(bf16[128,512]{1,0:T(8,128)(2,1)} %param.11) | copy-start | bytes 393220
  0.6 10.7 %copy-start.4 = (f32[16,128]{1,0:T(8,128)S(1)}, f32[16,128]{1,0:T(8,128)}, u32[]{:S(2)}) copy-start(f32[16,128]{1,0:T(8,128)} %param.13) | copy-start | bytes 24580
  0.7 23.9 %copy-start.5 = (f32[16,128]{1,0:T(8,128)S(1)}, f32[16,128]{1,0:T(8,128)}, u32[]{:S(2)}) copy-start(f32[16,128]{1,0:T(8,128)} %param.12) | copy-start | bytes 24580
  2.6 3.3 %collective-permute-start.2 = (bf16[2,512,128]{2,1,0:T(8,128)(2,1)S(1)}, bf16[2,512,128]{2,1,0:T(8,128)(2,1)S(1)}, u32[]{:S(2)}, u32[]{:S(2)}) collective-permute-start(bf16[2,512,128]{2,1,0:T(8,128)(2,1)S(1)} %pad_maximum_fusion.4), channel_id=1, source_target_pairs={{0,2},{2,0},{4,6},{6,4},{8,10},{10,8},{12,14},{14,12},{16,18},{18,... | collective-permute-start | bytes 786440 | tf_op jit(solution)/shard_map/ppermute | solution.py:300
  3.2 9.3 %collective-permute-start.1 = (bf16[2,512,128]{2,1,0:T(8,128)(2,1)S(1)}, bf16[2,512,128]{2,1,0:T(8,128)(2,1)S(1)}, u32[]{:S(2)}, u32[]{:S(2)}) collective-permute-start(bf16[2,512,128]{2,1,0:T(8,128)(2,1)S(1)} %pad_maximum_fusion.3), channel_id=1, source_target_pairs={{0,6},{2,4},{4,2},{6,0},{8,14},{10,12},{12,10},{14,8},{16,22},{18,... | collective-permute-start | bytes 786440 | tf_op jit(solution)/shard_map/ppermute | solution.py:300
  5.9 12.5 %collective-permute-start = (bf16[2,512,128]{2,1,0:T(8,128)(2,1)S(1)}, bf16[2,512,128]{2,1,0:T(8,128)(2,1)S(1)}, u32[]{:S(2)}, u32[]{:S(2)}) collective-permute-start(bf16[2,512,128]{2,1,0:T(8,128)(2,1)S(1)} %pad_maximum_fusion.2), channel_id=1, source_target_pairs={{0,4},{2,6},{4,0},{6,2},{8,12},{10,14},{12,8},{14,10},{16,20},{18,... | collective-permute-start | bytes 786440 | tf_op jit(solution)/shard_map/ppermute | solution.py:300
  6.1 12.3 %collective-permute-start.3 = (bf16[2,512,128]{2,1,0:T(8,128)(2,1)S(1)}, bf16[2,512,128]{2,1,0:T(8,128)(2,1)S(1)}, u32[]{:S(2)}, u32[]{:S(2)}) collective-permute-start(bf16[2,512,128]{2,1,0:T(8,128)(2,1)S(1)} %get-tuple-element.99), channel_id=1, source_target_pairs={{0,8},{2,10},{4,12},{6,14},{8,16},{10,18},{12,20},{14,22},{16,24},... | collective-permute-start | bytes 786440 | tf_op jit(solution)/shard_map/ppermute | solution.py:304
  10.1 9.6 %collective-permute-start.4 = (bf16[2,512,128]{2,1,0:T(8,128)(2,1)S(1)}, bf16[2,512,128]{2,1,0:T(8,128)(2,1)S(1)}, u32[]{:S(2)}, u32[]{:S(2)}) collective-permute-start(bf16[2,512,128]{2,1,0:T(8,128)(2,1)S(1)} %get-tuple-element.98), channel_id=1, source_target_pairs={{8,0},{10,2},{12,4},{14,6},{16,8},{18,10},{20,12},{22,14},{24,16},... | collective-permute-start | bytes 786440 | tf_op jit(solution)/shard_map/ppermute | solution.py:304
  19.7 9.2 %collective-permute-start.5 = (bf16[2,512,128]{2,1,0:T(8,128)(2,1)S(1)}, bf16[2,512,128]{2,1,0:T(8,128)(2,1)S(1)}, u32[]{:S(2)}, u32[]{:S(2)}) collective-permute-start(bf16[2,512,128]{2,1,0:T(8,128)(2,1)S(1)} %pad_maximum_fusion.6), channel_id=1, source_target_pairs={{0,8},{2,10},{4,12},{6,14},{8,16},{10,18},{12,20},{14,22},{16,24},... | collective-permute-start | bytes 786440 | tf_op jit(solution)/shard_map/ppermute | solution.py:304
  23.3 8.4 %collective-permute-start.6 = (bf16[2,512,128]{2,1,0:T(8,128)(2,1)S(1)}, bf16[2,512,128]{2,1,0:T(8,128)(2,1)S(1)}, u32[]{:S(2)}, u32[]{:S(2)}) collective-permute-start(bf16[2,512,128]{2,1,0:T(8,128)(2,1)S(1)} %pad_maximum_fusion.7), channel_id=1, source_target_pairs={{8,0},{10,2},{12,4},{14,6},{16,8},{18,10},{20,12},{22,14},{24,16},... | collective-permute-start | bytes 786440 | tf_op jit(solution)/shard_map/ppermute | solution.py:304
  34.5 8.4 %collective-permute-start.7 = (f32[4,16,128]{2,1,0:T(8,128)S(1)}, f32[4,16,128]{2,1,0:T(8,128)S(1)}, u32[]{:S(2)}, u32[]{:S(2)}) collective-permute-start(f32[4,16,128]{2,1,0:T(8,128)S(1)} %get-tuple-element.53), channel_id=1, source_target_pairs={{0,16},{2,18},{4,20},{6,22},{8,24},{10,26},{12,28},{14,30},{16,0},... | collective-permute-start | bytes 98312 | tf_op jit(solution)/shard_map/ppermute | solution.py:300
  45.2 16.9 %copy-start.1 = (bf16[2048,128]{1,0:T(8,128)(2,1)S(1)}, bf16[2048,128]{1,0:T(8,128)(2,1)}, u32[]{:S(2)}) copy-start(bf16[2048,128]{1,0:T(8,128)(2,1)} %refs_9_.1) | copy-start | bytes 1572868
  45.2 16.9 %copy-start.2 = (bf16[2048,128]{1,0:T(8,128)(2,1)S(1)}, bf16[2048,128]{1,0:T(8,128)(2,1)}, u32[]{:S(2)}) copy-start(bf16[2048,128]{1,0:T(8,128)(2,1)} %refs_10_.1) | copy-start | bytes 1572868
  45.2 16.9 %copy-start.3 = (bf16[2048,128]{1,0:T(8,128)(2,1)S(1)}, bf16[2048,128]{1,0:T(8,128)(2,1)}, u32[]{:S(2)}) copy-start(bf16[2048,128]{1,0:T(8,128)(2,1)} %refs_8_.1) | copy-start | bytes 1572868
  45.4 4.4 %collective-permute-start.11 = (f32[32,640]{1,0:T(8,128)S(1)}, f32[32,640]{1,0:T(8,128)S(1)}, u32[]{:S(2)}, u32[]{:S(2)}) collective-permute-start(f32[32,640]{1,0:T(8,128)S(1)} %joins.1), channel_id=1, source_target_pairs={{0,8},{2,10},{4,12},{6,14},{8,0},{10,2},{12,4},{14,6},{16,24},{18,... | collective-permute-start | bytes 245768 | tf_op jit(solution)/shard_map/ppermute | solution.py:300
  47.7 7.6 %collective-permute-start.10 = (bf16[2,256,128]{2,1,0:T(8,128)(2,1)S(1)}, bf16[2,256,128]{2,1,0:T(8,128)(2,1)S(1)}, u32[]{:S(2)}, u32[]{:S(2)}) collective-permute-start(bf16[2,256,128]{2,1,0:T(8,128)(2,1)S(1)} %get-tuple-element.64), channel_id=1, source_target_pairs={{0,6},{2,4},{4,2},{6,0},{8,14},{10,12},{12,10},{14,8},{16,22},{18,... | collective-permute-start | bytes 393224 | tf_op jit(solution)/shard_map/ppermute | solution.py:300
  49.9 5.4 %collective-permute-start.12 = (bf16[32,640]{1,0:T(8,128)(2,1)S(1)}, bf16[32,640]{1,0:T(8,128)(2,1)S(1)}, u32[]{:S(2)}, u32[]{:S(2)}) collective-permute-start(bf16[32,640]{1,0:T(8,128)(2,1)S(1)} %reduce-precision_convert_fusion.1), channel_id=1, source_target_pairs={{0,16},{2,18},{4,20},{6,22},{8,24},{10,26},{12,28},{14,30},{16,0},... | collective-permute-start | bytes 122888 | tf_op jit(solution)/shard_map/ppermute | solution.py:300
  50.5 6.4 %collective-permute-start.9 = (bf16[2,256,128]{2,1,0:T(8,128)(2,1)S(1)}, bf16[2,256,128]{2,1,0:T(8,128)(2,1)S(1)}, u32[]{:S(2)}, u32[]{:S(2)}) collective-permute-start(bf16[2,256,128]{2,1,0:T(8,128)(2,1)S(1)} %get-tuple-element.63), channel_id=1, source_target_pairs={{0,4},{2,6},{4,0},{6,2},{8,12},{10,14},{12,8},{14,10},{16,20},{18,... | collective-permute-start | bytes 393224 | tf_op jit(solution)/shard_map/ppermute | solution.py:300
  52.0 4.9 %collective-permute-start.13 = (bf16[2,256,128]{2,1,0:T(8,128)(2,1)S(1)}, bf16[2,256,128]{2,1,0:T(8,128)(2,1)S(1)}, u32[]{:S(2)}, u32[]{:S(2)}) collective-permute-start(bf16[2,256,128]{2,1,0:T(8,128)(2,1)S(1)} %get-tuple-element.74), channel_id=1, source_target_pairs={{0,2},{2,0},{4,6},{6,4},{8,10},{10,8},{12,14},{14,12},{16,18},{18,... | collective-permute-start | bytes 393224 | tf_op jit(solution)/shard_map/ppermute | solution.py:300
  52.0 7.7 %collective-permute-start.14 = (bf16[2,256,128]{2,1,0:T(8,128)(2,1)S(1)}, bf16[2,256,128]{2,1,0:T(8,128)(2,1)S(1)}, u32[]{:S(2)}, u32[]{:S(2)}) collective-permute-start(bf16[2,256,128]{2,1,0:T(8,128)(2,1)S(1)} %get-tuple-element.75), channel_id=1, source_target_pairs={{0,4},{2,6},{4,0},{6,2},{8,12},{10,14},{12,8},{14,10},{16,20},{18,... | collective-permute-start | bytes 393224 | tf_op jit(solution)/shard_map/ppermute | solution.py:300
  55.3 6.8 %collective-permute-start.15 = (bf16[2,256,128]{2,1,0:T(8,128)(2,1)S(1)}, bf16[2,256,128]{2,1,0:T(8,128)(2,1)S(1)}, u32[]{:S(2)}, u32[]{:S(2)}) collective-permute-start(bf16[2,256,128]{2,1,0:T(8,128)(2,1)S(1)} %get-tuple-element.76), channel_id=1, source_target_pairs={{0,6},{2,4},{4,2},{6,0},{8,14},{10,12},{12,10},{14,8},{16,22},{18,... | collective-permute-start | bytes 393224 | tf_op jit(solution)/shard_map/ppermute | solution.py:300
  55.3 6.8 %collective-permute-start.8 = (bf16[2,256,128]{2,1,0:T(8,128)(2,1)S(1)}, bf16[2,256,128]{2,1,0:T(8,128)(2,1)S(1)}, u32[]{:S(2)}, u32[]{:S(2)}) collective-permute-start(bf16[2,256,128]{2,1,0:T(8,128)(2,1)S(1)} %get-tuple-element.62), channel_id=1, source_target_pairs={{0,2},{2,0},{4,6},{6,4},{8,10},{10,8},{12,14},{14,12},{16,18},{18,... | collective-permute-start | bytes 393224 | tf_op jit(solution)/shard_map/ppermute | solution.py:300
  56.8 6.8 %collective-permute-start.16 = (bf16[32,640]{1,0:T(8,128)(2,1)S(1)}, bf16[32,640]{1,0:T(8,128)(2,1)S(1)}, u32[]{:S(2)}, u32[]{:S(2)}) collective-permute-start(bf16[32,640]{1,0:T(8,128)(2,1)S(1)} %reduce-precision_convert_fusion.s0), channel_id=1, source_target_pairs={{0,2},{2,0},{4,6},{6,4},{8,10},{10,8},{12,14},{14,12},{16,18},{18,... | collective-permute-start | bytes 122888 | tf_op jit(solution)/shard_map/ppermute | solution.py:300
  56.9 6.8 %collective-permute-start.17 = (bf16[32,640]{1,0:T(8,128)(2,1)S(1)}, bf16[32,640]{1,0:T(8,128)(2,1)S(1)}, u32[]{:S(2)}, u32[]{:S(2)}) collective-permute-start(bf16[32,640]{1,0:T(8,128)(2,1)S(1)} %reduce-precision_convert_fusion.s0), channel_id=1, source_target_pairs={{0,4},{2,6},{4,0},{6,2},{8,12},{10,14},{12,8},{14,10},{16,20},{18,... | collective-permute-start | bytes 122888 | tf_op jit(solution)/shard_map/ppermute | solution.py:300
  59.7 4.2 %collective-permute-start.18 = (bf16[32,640]{1,0:T(8,128)(2,1)S(1)}, bf16[32,640]{1,0:T(8,128)(2,1)S(1)}, u32[]{:S(2)}, u32[]{:S(2)}) collective-permute-start(bf16[32,640]{1,0:T(8,128)(2,1)S(1)} %reduce-precision_convert_fusion.s0), channel_id=1, source_target_pairs={{0,6},{2,4},{4,2},{6,0},{8,14},{10,12},{12,10},{14,8},{16,22},{18,... | collective-permute-start | bytes 122888 | tf_op jit(solution)/shard_map/ppermute | solution.py:300

commit v4 on v3

--- a/solution.py
+++ b/solution.py
@@ -336,60 +336,71 @@
     rate_row = flat(rate)
     root_row = flat(root)
     scale = 1.0 / math.sqrt(GROUP * seq_total)
-    params = pltpu.CompilerParams(vmem_limit_bytes=8 << 20)
+    params = pltpu.CompilerParams(vmem_limit_bytes=24 << 20)
     smem = pl.BlockSpec(memory_space=pltpu.SMEM)
     whole = pl.BlockSpec(memory_space=pltpu.VMEM)
 
-    def block(shape, axis, offset=0):
-        def at(i):
-            return tuple(i + offset if d == axis else 0 for d in range(len(shape)))
-
-        return pl.BlockSpec(shape, at)
-
-    def specs(offset=0):
-        return dict(
-            group=block((STEP, GROUP, BLK), 0, offset),
-            row=block((1, 8, BLK), 0, offset),
-            packed=block((1, GROUP, BLK), 0, offset),
-            pair=block((2, rows, BLK), 1, offset),
-            states=block((1, SPAN - 1, BLK, BLK), 0, offset),
-            table=block((STEP, BLK, WIDE), 0, offset),
-            lag=block((STEP, WIDE), 0, offset),
-        )
-
-    sp = specs()
+    def view(ref, kind, step):
+        if kind == "all":
+            return ref
+        if kind == "pair":
+            return ref.at[:, pl.ds(pl.multiple_of(step * rows, rows), rows), :]
+        if kind == "one":
+            return ref.at[pl.ds(step, 1)]
+        return ref.at[pl.ds(pl.multiple_of(step * STEP, STEP), STEP)]
+
+    def looped(kernel, kinds, count, name, out_shape, scratch=()):
+        kinds = list(kinds) + [("all", 0)] * len(scratch)
+
+        def whole_kernel(*refs):
+            def turn(step, carry):
+                kernel(*[view(ref, kind, step + at) for ref, (kind, at) in zip(refs, kinds)])
+                return carry
+
+            lax.fori_loop(0, count, turn, 0)
+
+        ins = len(kinds) - len(scratch) - len(out_shape)
+        return pl.pallas_call(
+            whole_kernel,
+            in_specs=[smem if kind == "all" else whole for kind, _ in kinds[:ins]],
+            out_specs=[whole] * len(out_shape),
+            out_shape=list(out_shape),
+            scratch_shapes=list(scratch),
+            compiler_params=params,
+            name=name,
+        )
+
     pieces[2], pieces[3], x_near, y_near, rate_row, root_row = lax.optimization_barrier(
         (pieces[2], pieces[3], x_near, y_near, rate_row, root_row)
     )
     x_far = shift(jnp.stack([pieces[2][0], pieces[3][0]]), 1)
     y_far = shift(jnp.stack([pieces[2][1], pieces[3][1]]), -1)
 
-    table, rate_row = pl.pallas_call(
+    few = ("few", 0)
+    one = ("one", 0)
+    pair = ("pair", 0)
+    table, rate_row = looped(
         table_kernel,
-        grid=(steps,),
-        in_specs=[sp["row"], sp["group"], sp["group"], block((STEP, SPAN * BLK), 0)],
-        out_specs=[sp["table"], sp["row"]],
-        out_shape=[
+        [one, few, few, few, few, one],
+        steps,
+        "tables",
+        [
             jax.ShapeDtypeStruct((local, BLK, WIDE), BF16),
             jax.ShapeDtypeStruct(rate_row.shape, F32),
         ],
-        compiler_params=params,
-        name="tables",
     )(rate_row, rate_wide, gain_wide, med)
 
     store = jax.ShapeDtypeStruct((steps, SPAN - 1, BLK, BLK), BF16)
     small = jax.ShapeDtypeStruct((steps, GROUP, BLK), F32)
     blocks = pltpu.VMEM((2 * SPAN, rows, BLK), BF16)
     halo = (x_near, x_far, y_near, y_far)
-    carried, returned, ends, ahead, behind, mail, cross = pl.pallas_call(
+    carried, returned, ends, ahead, behind, mail, cross = looped(
         state_kernel,
-        grid=(steps,),
-        in_specs=[smem, sp["group"], sp["row"]] + [sp["pair"]] * 8,
-        out_specs=[sp["states"]] * 2 + [sp["packed"]] * 5,
-        out_shape=[store] * 2 + [small] * 5,
-        scratch_shapes=[blocks] * 2,
-        compiler_params=params,
-        name="states",
+        [("all", 0), few, one] + [pair] * 8 + [one] * 7,
+        steps,
+        "states",
+        [store] * 2 + [small] * 5,
+        [blocks] * 2,
     )(q_arr, rate_wide, rate_row, *pieces, *halo)
 
     if units == 4:
@@ -406,19 +417,17 @@
         before = shift(ahead, 2)
         after = shift(behind, -2)
 
-    lag = pl.pallas_call(
+    (lag,) = looped(
         functools.partial(lag_kernel, scale=scale),
-        grid=(steps,),
-        in_specs=[smem, sp["group"], sp["row"], sp["row"], sp["packed"]] + [sp["pair"]] * 6,
-        out_specs=sp["lag"],
-        out_shape=jax.ShapeDtypeStruct((local, WIDE), F32),
-        scratch_shapes=[
+        [("all", 0), few, one, one, one] + [pair] * 6 + [few],
+        steps,
+        "lags",
+        [jax.ShapeDtypeStruct((local, WIDE), F32)],
+        [
             pltpu.VMEM((SPAN, rows, BLK), BF16),
             blocks,
             pltpu.VMEM((STEP, 8, WIDE), F32),
         ],
-        compiler_params=params,
-        name="lags",
     )(q_arr, rate_wide, rate_row, root_row, cross, *pieces, y_near, y_far)
     before, after, lag = lax.optimization_barrier((before, after, lag))
 
@@ -426,20 +435,16 @@
     parts = PARTS
     q_next = q_arr
     for h in range(parts):
-        sh = specs(h * (steps // parts))
-        so = specs()
-        outs = pl.pallas_call(
+        at = h * (steps // parts)
+        outs = looped(
             main_kernel,
-            grid=(steps // parts,),
-            in_specs=[smem, sh["group"], sh["group"], sh["row"], sh["table"]]
-            + [sh["states"]] * 2
-            + [sh["packed"]] * 2
-            + [sh["pair"]] * 8,
-            out_specs=[so["pair"]] * 4,
-            out_shape=[jax.ShapeDtypeStruct((2, sub // parts, BLK), BF16)] * 4,
-            scratch_shapes=[blocks] * 2 + [pltpu.VMEM((SPAN, rows, BLK), F32)] * 2,
-            compiler_params=params,
-            name="convs",
+            [("all", 0)]
+            + [(kind, at) for kind in ["few", "few", "one", "few"] + ["one"] * 4 + ["pair"] * 8]
+            + [pair] * 4,
+            steps // parts,
+            "convs",
+            [jax.ShapeDtypeStruct((2, sub // parts, BLK), BF16)] * 4,
+            [blocks] * 2 + [pltpu.VMEM((SPAN, rows, BLK), F32)] * 2,
         )(
             q_next, rate_wide, gain_wide, rate_row, table, carried, returned, before, after,
             *pieces, *halo,

time: 64.8 us -> 63.7 us (0.983)
  Pallas kernels: 19.7 us -> 18.7 us
    pallas_call x5, Pallas kernels: 17.3 us -> 16.3 us  [the longest x1 5.83 us: body(): looped(functools.partial(lag_kernel, scale=scale), [('all', 0), few, one,...]
where the time goes in v4:
time: 63.7 us; the launch traced here: 63.5 us
  starting transfers between devices  21.6 us (34%)
  waiting for transfers between devices  19.2 us (30%)
  Pallas kernels  18.7 us (29%)
  other arithmetic  2.31 us (4%)
  between operations  0.96 us (2%)
  local copies, waits for them, and re-layouts  0.74 us (1%)
    ppermute x15, waiting for transfers between devices, swap(): return lax.ppermute(value, 'ctx', [(i, i ^ m) for i in range(devices)])  15.1 us
    ppermute x15, starting transfers between devices, swap(): return lax.ppermute(value, 'ctx', [(i, i ^ m) for i in range(devices)])  11.5 us
    ppermute x4, starting transfers between devices, shift(): lax.ppermute(value, 'ctx', [(i, i + by) for i in range(devices) if 0 <= i...  10.1 us
    pallas_call x1, Pallas kernels, body(): looped(functools.partial(lag_kernel, scale=scale), [('all', 0), few, one,...  5.83 us
    pallas_call x2, Pallas kernels, body(): looped(main_kernel, [('all', 0)] + [(kind, at) for kind in ['few', 'few',...  4.11 us
    ppermute x4, waiting for transfers between devices, shift(): lax.ppermute(value, 'ctx', [(i, i + by) for i in range(devices) if 0 <= i...  4.07 us
    pallas_call x1, Pallas kernels, body(): looped(table_kernel, [one, few, few, few, few, one], steps, 'tables', [ja...  3.82 us
    pallas_call x1, Pallas kernels, body(): looped(state_kernel, [('all', 0), few, one] + [pair] * 8 + [one] * 7, ste...  2.49 us
  transfers between devices with their start and end apart: 19, of which 10 were waited for; matrix products, arithmetic and copies ran while one was open for 2% of the time, Pallas kernels for 21%

profile of v4, /device:TPU:0, one launch (start us, length us, event | category | flops | bytes accessed | tf_op | source)
XLA Modules:
  0.0 63.5 jit_solution(11518921774066283189)
XLA Ops:
  0.6 0.0 copy-start
  0.7 1.9 %fusion.5 = (bf16[1,512,128]{2,1,0:T(8,128)(2,1)S(1)}, bf16[1,512,128]{2,1,0:T(8,128)(2,1)S(1)}, bf16[1,512,128]{2,1,0:T(8,128)(2,1)S(1)}, bf16[1,512,128]{2,1,0...) fusion(bf16[2048,128]{1,0:T(8,128)(2,1)} %refs_9_.1, ...), kind=kLoop, calls=%fused_computation.21 | loop fusion | flops 2097152 | bytes 3145744 | tf_op jit(solution)/shard_map/stack | solution.py:312
  2.6 0.5 collective-permute-start.2
  3.2 2.7 %collective-permute-start.1 = (bf16[2,512,128]{2,1,0:T(8,128)(2,1)S(1)}, bf16[2,512,128]{2,1,0:T(8,128)(2,1)S(1)}, u32[]{:S(2)}, u32[]{:S(2)}) collective-permute-start(bf16[2,512,128]{2,1,0:T(8,128)(2,1)S(1)} %pad_maximum_fusion.3), channel_id=1, source_target_pairs={{0,6},{2,4},{4,2},{6,0},{8,14},{10,12},{12,10},{14,8},{16,22},{18,... | collective-permute-start | bytes 786440 | tf_op jit(solution)/shard_map/ppermute | solution.py:300
  5.9 0.1 collective-permute-start
  6.0 0.1 pad_maximum_fusion
  6.1 4.0 %collective-permute-start.3 = (bf16[2,512,128]{2,1,0:T(8,128)(2,1)S(1)}, bf16[2,512,128]{2,1,0:T(8,128)(2,1)S(1)}, u32[]{:S(2)}, u32[]{:S(2)}) collective-permute-start(bf16[2,512,128]{2,1,0:T(8,128)(2,1)S(1)} %get-tuple-element.99), channel_id=1, source_target_pairs={{0,8},{2,10},{4,12},{6,14},{8,16},{10,18},{12,20},{14,22},{16,24},... | collective-permute-start | bytes 786440 | tf_op jit(solution)/shard_map/ppermute | solution.py:304
  10.1 1.3 %collective-permute-start.4 = (bf16[2,512,128]{2,1,0:T(8,128)(2,1)S(1)}, bf16[2,512,128]{2,1,0:T(8,128)(2,1)S(1)}, u32[]{:S(2)}, u32[]{:S(2)}) collective-permute-start(bf16[2,512,128]{2,1,0:T(8,128)(2,1)S(1)} %get-tuple-element.98), channel_id=1, source_target_pairs={{8,0},{10,2},{12,4},{14,6},{16,8},{18,10},{20,12},{22,14},{24,16},... | collective-permute-start | bytes 786440 | tf_op jit(solution)/shard_map/ppermute | solution.py:304
  11.4 0.1 sqrt_bitcast_fusion
  11.5 0.1 copy.14
  11.6 0.1 broadcast_in_dim.28
  11.7 0.1 copy.17
  11.7 0.1 broadcast_in_dim.30
  11.8 0.7 %collective-permute-done.1.refs_6_.refs_8_.refs_12_ = bf16[2,512,128]{2,1,0:T(8,128)(2,1)S(1)} collective-permute-done((bf16[2,512,128]{2,1,0:T(8,128)(2,1)S(1)}, bf16[2,512,128]{2,1,0:T(8,128)(2,1)S(1)}, u32[]{:S(2)}, u32[]{:S(2)}) %collective-permute-start.1) | collective-permute-done | bytes 262176 | tf_op jit(solution)/shard_map/ppermute | solution.py:300
  12.5 5.8 %collective-permute-done.refs_5_.refs_7_.refs_11_ = bf16[2,512,128]{2,1,0:T(8,128)(2,1)S(1)} collective-permute-done((bf16[2,512,128]{2,1,0:T(8,128)(2,1)S(1)}, bf16[2,512,128]{2,1,0:T(8,128)(2,1)S(1)}, u32[]{:S(2)}, u32[]{:S(2)}) %collective-permute-start) | collective-permute-done | bytes 262176 | tf_op jit(solution)/shard_map/ppermute | solution.py:300
  18.3 1.3 %collective-permute-done.4.refs_9_.refs_15_ = bf16[2,512,128]{2,1,0:T(8,128)(2,1)S(1)} collective-permute-done((bf16[2,512,128]{2,1,0:T(8,128)(2,1)S(1)}, bf16[2,512,128]{2,1,0:T(8,128)(2,1)S(1)}, u32[]{:S(2)}, u32[]{:S(2)}) %collective-permute-start.4) | collective-permute-done | bytes 262176 | tf_op jit(solution)/shard_map/ppermute | solution.py:304
  19.7 3.5 %collective-permute-start.5 = (bf16[2,512,128]{2,1,0:T(8,128)(2,1)S(1)}, bf16[2,512,128]{2,1,0:T(8,128)(2,1)S(1)}, u32[]{:S(2)}, u32[]{:S(2)}) collective-permute-start(bf16[2,512,128]{2,1,0:T(8,128)(2,1)S(1)} %pad_maximum_fusion.6), channel_id=1, source_target_pairs={{0,8},{2,10},{4,12},{6,14},{8,16},{10,18},{12,20},{14,22},{16,24},... | collective-permute-start | bytes 786440 | tf_op jit(solution)/shard_map/ppermute | solution.py:304
  23.3 1.3 %collective-permute-start.6 = (bf16[2,512,128]{2,1,0:T(8,128)(2,1)S(1)}, bf16[2,512,128]{2,1,0:T(8,128)(2,1)S(1)}, u32[]{:S(2)}, u32[]{:S(2)}) collective-permute-start(bf16[2,512,128]{2,1,0:T(8,128)(2,1)S(1)} %pad_maximum_fusion.7), channel_id=1, source_target_pairs={{8,0},{10,2},{12,4},{14,6},{16,8},{18,10},{20,12},{22,14},{24,16},... | collective-permute-start | bytes 786440 | tf_op jit(solution)/shard_map/ppermute | solution.py:304
  24.6 0.1 bitcast_multiply_fusion
  24.7 0.1 copy.15
  24.8 0.1 broadcast_in_dim.12.refs_1_
  24.9 0.1 broadcast_in_dim.13.refs_2_
  25.0 3.8 %tables.1 = (bf16[32,128,640]{2,1,0:T(8,128)(2,1)S(1)}, f32[4,8,128]{2,1,0:T(8,128)S(1)}) custom-call(f32[4,8,128]{2,1,0:T(8,128)S(1)} %broadcast_in_dim.29.refs_0_, f32[32,16,128]{2,1,0:T(8,128)S(1)} %broadcast_in_dim.12.refs_1_, f32[32,16,128]{2,1,0:T(8,128)S(1)} %broadcast_in_dim.13.refs_2_, bf16[32,512]{1,0:T(8,128)(2,1)S(1)} %constant_dynamic-slice_fusion.refs_3_), custom_call_target="tpu_custom_call" | custom-call | tf_op jit(solution)/shard_map/tables/pallas_call | solution.py:382
  28.9 2.8 %collective-permute-done.6.refs_10_.refs_16_ = bf16[2,512,128]{2,1,0:T(8,128)(2,1)S(1)} collective-permute-done((bf16[2,512,128]{2,1,0:T(8,128)(2,1)S(1)}, bf16[2,512,128]{2,1,0:T(8,128)(2,1)S(1)}, u32[]{:S(2)}, u32[]{:S(2)}) %collective-permute-start.6) | collective-permute-done | bytes 262176 | tf_op jit(solution)/shard_map/ppermute | solution.py:304
  31.6 2.5 %states.1 = (bf16[4,3,128,128]{3,2,1,0:T(8,128)(2,1)S(1)}, bf16[4,3,128,128]{3,2,1,0:T(8,128)(2,1)S(1)}, f32[4,16,128]{2,1,0:T(8,128)S(1)}, f32[4,16,128]{2,1,0:...) custom-call(s32[1]{0:T(128)} %bitcast.refs_0_.q_ref, ...), custom_call_target="tpu_custom_call" | custom-call | tf_op jit(solution)/shard_map/states/pallas_call | solution.py:397
  34.1 2.4 %collective-permute-start.7 = (f32[4,16,128]{2,1,0:T(8,128)S(1)}, f32[4,16,128]{2,1,0:T(8,128)S(1)}, u32[]{:S(2)}, u32[]{:S(2)}) collective-permute-start(f32[4,16,128]{2,1,0:T(8,128)S(1)} %get-tuple-element.53), channel_id=1, source_target_pairs={{0,16},{2,18},{4,20},{6,22},{8,24},{10,26},{12,28},{14,30},{16,0},... | collective-permute-start | bytes 98312 | tf_op jit(solution)/shard_map/ppermute | solution.py:300
  36.5 5.8 %lags.1.lag_ref = f32[32,640]{1,0:T(8,128)S(1)} custom-call(s32[1]{0:T(128)} %bitcast.refs_0_.q_ref, f32[32,16,128]{2,1,0:T(8,128)S(1)} %broadcast_in_dim.12.refs_1_, f32[4,8,128]{2,1,0:T(8,128)S(1)} %get-tuple-element.45.refs_2_.refs_3_.row_ref, f32[4,8,128]{2,1,0:T(8,128)S(1)} %broadcast_in_dim.31.refs_3_.root_ref, ...), custom_call_target="tpu_custom_call" | custom-call | tf_op jit(solution)/shard_map/lags/pallas_call | solution.py:420
  42.4 2.1 %convs.2 = (bf16[2,256,128]{2,1,0:T(8,128)(2,1)S(1)}, bf16[2,256,128]{2,1,0:T(8,128)(2,1)S(1)}, bf16[2,256,128]{2,1,0:T(8,128)(2,1)S(1)}, bf16[2,256,128]{2,1,0:T(8,128)(2,1)S(1)}) custom-call(s32[1]{0:T(128)} %bitcast.refs_0_.q_ref, f32[32,16,128]{2,1,0:T(8,128)S(1)} %broadcast_in_dim.12.refs_1_, f32[32,16,128]{2,1,0:T(8,128)S(1)} %broadcast_in_dim.13.refs_2_, ...), custom_call_target="tpu_custom_call" | custom-call | tf_op jit(solution)/shard_map/convs/pallas_call | solution.py:439
  44.4 0.0 copy-start.1
  44.4 0.0 copy-start.2
  44.4 0.0 copy-start.3
  44.5 0.2 joins.1
  44.7 0.0 collective-permute-start.11
  44.7 2.1 %convs.3 = (bf16[2,256,128]{2,1,0:T(8,128)(2,1)S(1)}, bf16[2,256,128]{2,1,0:T(8,128)(2,1)S(1)}, bf16[2,256,128]{2,1,0:T(8,128)(2,1)S(1)}, bf16[2,256,128]{2,1,0:T(8,128)(2,1)S(1)}) custom-call(s32[1]{0:T(128)} %bitcast.refs_0_.q_ref, f32[32,16,128]{2,1,0:T(8,128)S(1)} %broadcast_in_dim.12.refs_1_, f32[32,16,128]{2,1,0:T(8,128)S(1)} %broadcast_in_dim.13.refs_2_, ...), custom_call_target="tpu_custom_call" | custom-call | tf_op jit(solution)/shard_map/convs/pallas_call | solution.py:439
  46.8 0.1 collective-permute-start.10
  46.8 2.3 %collective-permute-done.11 = f32[32,640]{1,0:T(8,128)S(1)} collective-permute-done((f32[32,640]{1,0:T(8,128)S(1)}, f32[32,640]{1,0:T(8,128)S(1)}, u32[]{:S(2)}, u32[]{:S(2)}) %collective-permute-start.11) | collective-permute-done | bytes 81952 | tf_op jit(solution)/shard_map/ppermute | solution.py:300
  49.1 0.6 collective-permute-start.12
  49.7 1.5 %collective-permute-start.9 = (bf16[2,256,128]{2,1,0:T(8,128)(2,1)S(1)}, bf16[2,256,128]{2,1,0:T(8,128)(2,1)S(1)}, u32[]{:S(2)}, u32[]{:S(2)}) collective-permute-start(bf16[2,256,128]{2,1,0:T(8,128)(2,1)S(1)} %get-tuple-element.63), channel_id=1, source_target_pairs={{0,4},{2,6},{4,0},{6,2},{8,12},{10,14},{12,8},{14,10},{16,20},{18,... | collective-permute-start | bytes 393224 | tf_op jit(solution)/shard_map/ppermute | solution.py:300
  51.2 0.8 %collective-permute-start.14 = (bf16[2,256,128]{2,1,0:T(8,128)(2,1)S(1)}, bf16[2,256,128]{2,1,0:T(8,128)(2,1)S(1)}, u32[]{:S(2)}, u32[]{:S(2)}) collective-permute-start(bf16[2,256,128]{2,1,0:T(8,128)(2,1)S(1)} %get-tuple-element.75), channel_id=1, source_target_pairs={{0,4},{2,6},{4,0},{6,2},{8,12},{10,14},{12,8},{14,10},{16,20},{18,... | collective-permute-start | bytes 393224 | tf_op jit(solution)/shard_map/ppermute | solution.py:300
  52.1 2.4 %collective-permute-done.12 = bf16[32,640]{1,0:T(8,128)(2,1)S(1)} collective-permute-done((bf16[32,640]{1,0:T(8,128)(2,1)S(1)}, bf16[32,640]{1,0:T(8,128)(2,1)S(1)}, u32[]{:S(2)}, u32[]{:S(2)}) %collective-permute-start.12) | collective-permute-done | bytes 40992 | tf_op jit(solution)/shard_map/ppermute | solution.py:300
  54.4 1.3 %collective-permute-start.8 = (bf16[2,256,128]{2,1,0:T(8,128)(2,1)S(1)}, bf16[2,256,128]{2,1,0:T(8,128)(2,1)S(1)}, u32[]{:S(2)}, u32[]{:S(2)}) collective-permute-start(bf16[2,256,128]{2,1,0:T(8,128)(2,1)S(1)} %get-tuple-element.62), channel_id=1, source_target_pairs={{0,2},{2,0},{4,6},{6,4},{8,10},{10,8},{12,14},{14,12},{16,18},{18,... | collective-permute-start | bytes 393224 | tf_op jit(solution)/shard_map/ppermute | solution.py:300
  55.7 0.3 collective-permute-done.9.refs_2_
  56.0 1.6 %collective-permute-start.17 = (bf16[32,640]{1,0:T(8,128)(2,1)S(1)}, bf16[32,640]{1,0:T(8,128)(2,1)S(1)}, u32[]{:S(2)}, u32[]{:S(2)}) collective-permute-start(bf16[32,640]{1,0:T(8,128)(2,1)S(1)} %reduce-precision_convert_fusion.s0), channel_id=1, source_target_pairs={{0,4},{2,6},{4,0},{6,2},{8,12},{10,14},{12,8},{14,10},{16,20},{18,... | collective-permute-start | bytes 122888 | tf_op jit(solution)/shard_map/ppermute | solution.py:300
  57.6 1.2 %collective-permute-done.14.refs_6_ = bf16[2,256,128]{2,1,0:T(8,128)(2,1)S(1)} collective-permute-done((bf16[2,256,128]{2,1,0:T(8,128)(2,1)S(1)}, bf16[2,256,128]{2,1,0:T(8,128)(2,1)S(1)}, u32[]{:S(2)}, u32[]{:S(2)}) %collective-permute-start.14) | collective-permute-done | bytes 131104 | tf_op jit(solution)/shard_map/ppermute | solution.py:300
  58.8 2.2 %collective-permute-done.15.refs_7_ = bf16[2,256,128]{2,1,0:T(8,128)(2,1)S(1)} collective-permute-done((bf16[2,256,128]{2,1,0:T(8,128)(2,1)S(1)}, bf16[2,256,128]{2,1,0:T(8,128)(2,1)S(1)}, u32[]{:S(2)}, u32[]{:S(2)}) %collective-permute-start.15) | collective-permute-done | bytes 131104 | tf_op jit(solution)/shard_map/ppermute | solution.py:300
  61.0 1.5 %gates.1 = (bf16[2048,128]{1,0:T(8,128)(2,1)}, bf16[2048,128]{1,0:T(8,128)(2,1)}, bf16[2048,128]{1,0:T(8,128)(2,1)}) custom-call(s32[1]{0:T(128)} %bitcast.refs_0_.q_ref, bf16[2,256,128]{2,1,0:T(8,128)(2,1)S(1)} %get-tuple-element.61.refs_0_, bf16[2,256,128]{2,1,0:T(8,128)(2,1)S(1)} %collective-permute-done.8.refs_1_, ...), custom_call_target="tpu_custom_call" | custom-call | tf_op jit(solution)/shard_map/gates/pallas_call | solution.py:476
  62.5 0.2 collective-permute-done.18.s3
  62.8 0.7 %sums.1 = (f32[128,512]{1,0:T(8,128)}, f32[16,128]{1,0:T(8,128)}) custom-call(s32[1]{0:T(128)} %bitcast.refs_0_.q_ref, bf16[32,640]{1,0:T(8,128)(2,1)S(1)} %reduce-precision_convert_fusion.s0, bf16[32,640]{1,0:T(8,128)(2,1)S(1)} %collective-permute-done.16.s1, bf16[32,640]{1,0:T(8,128)(2,1)S(1)} %collective-permute-done.17.s2, ...), custom_call_target="tpu_custom_call" | custom-call | tf_op jit(solution)/shard_map/sums/pallas_call | solution.py:484
  (34 shorter events, 0.3 us)
Async XLA Ops:
  0.6 24.1 %copy-start = (bf16[128,512]{1,0:T(8,128)(2,1)S(1)}, bf16[128,512]{1,0:T(8,128)(2,1)}, u32[]{:S(2)}) copy-start(bf16[128,512]{1,0:T(8,128)(2,1)} %param.11) | copy-start | bytes 393220
  0.6 10.7 %copy-start.4 = (f32[16,128]{1,0:T(8,128)S(1)}, f32[16,128]{1,0:T(8,128)}, u32[]{:S(2)}) copy-start(f32[16,128]{1,0:T(8,128)} %param.13) | copy-start | bytes 24580
  0.7 23.9 %copy-start.5 = (f32[16,128]{1,0:T(8,128)S(1)}, f32[16,128]{1,0:T(8,128)}, u32[]{:S(2)}) copy-start(f32[16,128]{1,0:T(8,128)} %param.12) | copy-start | bytes 24580
  2.6 3.3 %collective-permute-start.2 = (bf16[2,512,128]{2,1,0:T(8,128)(2,1)S(1)}, bf16[2,512,128]{2,1,0:T(8,128)(2,1)S(1)}, u32[]{:S(2)}, u32[]{:S(2)}) collective-permute-start(bf16[2,512,128]{2,1,0:T(8,128)(2,1)S(1)} %pad_maximum_fusion.4), channel_id=1, source_target_pairs={{0,2},{2,0},{4,6},{6,4},{8,10},{10,8},{12,14},{14,12},{16,18},{18,... | collective-permute-start | bytes 786440 | tf_op jit(solution)/shard_map/ppermute | solution.py:300
  3.2 9.3 %collective-permute-start.1 = (bf16[2,512,128]{2,1,0:T(8,128)(2,1)S(1)}, bf16[2,512,128]{2,1,0:T(8,128)(2,1)S(1)}, u32[]{:S(2)}, u32[]{:S(2)}) collective-permute-start(bf16[2,512,128]{2,1,0:T(8,128)(2,1)S(1)} %pad_maximum_fusion.3), channel_id=1, source_target_pairs={{0,6},{2,4},{4,2},{6,0},{8,14},{10,12},{12,10},{14,8},{16,22},{18,... | collective-permute-start | bytes 786440 | tf_op jit(solution)/shard_map/ppermute | solution.py:300
  5.9 12.5 %collective-permute-start = (bf16[2,512,128]{2,1,0:T(8,128)(2,1)S(1)}, bf16[2,512,128]{2,1,0:T(8,128)(2,1)S(1)}, u32[]{:S(2)}, u32[]{:S(2)}) collective-permute-start(bf16[2,512,128]{2,1,0:T(8,128)(2,1)S(1)} %pad_maximum_fusion.2), channel_id=1, source_target_pairs={{0,4},{2,6},{4,0},{6,2},{8,12},{10,14},{12,8},{14,10},{16,20},{18,... | collective-permute-start | bytes 786440 | tf_op jit(solution)/shard_map/ppermute | solution.py:300
  6.1 12.3 %collective-permute-start.3 = (bf16[2,512,128]{2,1,0:T(8,128)(2,1)S(1)}, bf16[2,512,128]{2,1,0:T(8,128)(2,1)S(1)}, u32[]{:S(2)}, u32[]{:S(2)}) collective-permute-start(bf16[2,512,128]{2,1,0:T(8,128)(2,1)S(1)} %get-tuple-element.99), channel_id=1, source_target_pairs={{0,8},{2,10},{4,12},{6,14},{8,16},{10,18},{12,20},{14,22},{16,24},... | collective-permute-start | bytes 786440 | tf_op jit(solution)/shard_map/ppermute | solution.py:304
  10.1 9.6 %collective-permute-start.4 = (bf16[2,512,128]{2,1,0:T(8,128)(2,1)S(1)}, bf16[2,512,128]{2,1,0:T(8,128)(2,1)S(1)}, u32[]{:S(2)}, u32[]{:S(2)}) collective-permute-start(bf16[2,512,128]{2,1,0:T(8,128)(2,1)S(1)} %get-tuple-element.98), channel_id=1, source_target_pairs={{8,0},{10,2},{12,4},{14,6},{16,8},{18,10},{20,12},{22,14},{24,16},... | collective-permute-start | bytes 786440 | tf_op jit(solution)/shard_map/ppermute | solution.py:304
  19.7 9.1 %collective-permute-start.5 = (bf16[2,512,128]{2,1,0:T(8,128)(2,1)S(1)}, bf16[2,512,128]{2,1,0:T(8,128)(2,1)S(1)}, u32[]{:S(2)}, u32[]{:S(2)}) collective-permute-start(bf16[2,512,128]{2,1,0:T(8,128)(2,1)S(1)} %pad_maximum_fusion.6), channel_id=1, source_target_pairs={{0,8},{2,10},{4,12},{6,14},{8,16},{10,18},{12,20},{14,22},{16,24},... | collective-permute-start | bytes 786440 | tf_op jit(solution)/shard_map/ppermute | solution.py:304
  23.3 8.4 %collective-permute-start.6 = (bf16[2,512,128]{2,1,0:T(8,128)(2,1)S(1)}, bf16[2,512,128]{2,1,0:T(8,128)(2,1)S(1)}, u32[]{:S(2)}, u32[]{:S(2)}) collective-permute-start(bf16[2,512,128]{2,1,0:T(8,128)(2,1)S(1)} %pad_maximum_fusion.7), channel_id=1, source_target_pairs={{8,0},{10,2},{12,4},{14,6},{16,8},{18,10},{20,12},{22,14},{24,16},... | collective-permute-start | bytes 786440 | tf_op jit(solution)/shard_map/ppermute | solution.py:304
  34.1 8.2 %collective-permute-start.7 = (f32[4,16,128]{2,1,0:T(8,128)S(1)}, f32[4,16,128]{2,1,0:T(8,128)S(1)}, u32[]{:S(2)}, u32[]{:S(2)}) collective-permute-start(f32[4,16,128]{2,1,0:T(8,128)S(1)} %get-tuple-element.53), channel_id=1, source_target_pairs={{0,16},{2,18},{4,20},{6,22},{8,24},{10,26},{12,28},{14,30},{16,0},... | collective-permute-start | bytes 98312 | tf_op jit(solution)/shard_map/ppermute | solution.py:300
  44.4 16.6 %copy-start.1 = (bf16[2048,128]{1,0:T(8,128)(2,1)S(1)}, bf16[2048,128]{1,0:T(8,128)(2,1)}, u32[]{:S(2)}) copy-start(bf16[2048,128]{1,0:T(8,128)(2,1)} %refs_9_.1) | copy-start | bytes 1572868
  44.4 16.6 %copy-start.2 = (bf16[2048,128]{1,0:T(8,128)(2,1)S(1)}, bf16[2048,128]{1,0:T(8,128)(2,1)}, u32[]{:S(2)}) copy-start(bf16[2048,128]{1,0:T(8,128)(2,1)} %refs_10_.1) | copy-start | bytes 1572868
  44.4 16.6 %copy-start.3 = (bf16[2048,128]{1,0:T(8,128)(2,1)S(1)}, bf16[2048,128]{1,0:T(8,128)(2,1)}, u32[]{:S(2)}) copy-start(bf16[2048,128]{1,0:T(8,128)(2,1)} %refs_8_.1) | copy-start | bytes 1572868
  44.7 4.4 %collective-permute-start.11 = (f32[32,640]{1,0:T(8,128)S(1)}, f32[32,640]{1,0:T(8,128)S(1)}, u32[]{:S(2)}, u32[]{:S(2)}) collective-permute-start(f32[32,640]{1,0:T(8,128)S(1)} %joins.1), channel_id=1, source_target_pairs={{0,8},{2,10},{4,12},{6,14},{8,0},{10,2},{12,4},{14,6},{16,24},{18,... | collective-permute-start | bytes 245768 | tf_op jit(solution)/shard_map/ppermute | solution.py:300
  46.8 7.7 %collective-permute-start.10 = (bf16[2,256,128]{2,1,0:T(8,128)(2,1)S(1)}, bf16[2,256,128]{2,1,0:T(8,128)(2,1)S(1)}, u32[]{:S(2)}, u32[]{:S(2)}) collective-permute-start(bf16[2,256,128]{2,1,0:T(8,128)(2,1)S(1)} %get-tuple-element.64), channel_id=1, source_target_pairs={{0,6},{2,4},{4,2},{6,0},{8,14},{10,12},{12,10},{14,8},{16,22},{18,... | collective-permute-start | bytes 393224 | tf_op jit(solution)/shard_map/ppermute | solution.py:300
  49.1 5.3 %collective-permute-start.12 = (bf16[32,640]{1,0:T(8,128)(2,1)S(1)}, bf16[32,640]{1,0:T(8,128)(2,1)S(1)}, u32[]{:S(2)}, u32[]{:S(2)}) collective-permute-start(bf16[32,640]{1,0:T(8,128)(2,1)S(1)} %reduce-precision_convert_fusion.1), channel_id=1, source_target_pairs={{0,16},{2,18},{4,20},{6,22},{8,24},{10,26},{12,28},{14,30},{16,0},... | collective-permute-start | bytes 122888 | tf_op jit(solution)/shard_map/ppermute | solution.py:300
  49.7 6.3 %collective-permute-start.9 = (bf16[2,256,128]{2,1,0:T(8,128)(2,1)S(1)}, bf16[2,256,128]{2,1,0:T(8,128)(2,1)S(1)}, u32[]{:S(2)}, u32[]{:S(2)}) collective-permute-start(bf16[2,256,128]{2,1,0:T(8,128)(2,1)S(1)} %get-tuple-element.63), channel_id=1, source_target_pairs={{0,4},{2,6},{4,0},{6,2},{8,12},{10,14},{12,8},{14,10},{16,20},{18,... | collective-permute-start | bytes 393224 | tf_op jit(solution)/shard_map/ppermute | solution.py:300
  51.2 4.8 %collective-permute-start.13 = (bf16[2,256,128]{2,1,0:T(8,128)(2,1)S(1)}, bf16[2,256,128]{2,1,0:T(8,128)(2,1)S(1)}, u32[]{:S(2)}, u32[]{:S(2)}) collective-permute-start(bf16[2,256,128]{2,1,0:T(8,128)(2,1)S(1)} %get-tuple-element.74), channel_id=1, source_target_pairs={{0,2},{2,0},{4,6},{6,4},{8,10},{10,8},{12,14},{14,12},{16,18},{18,... | collective-permute-start | bytes 393224 | tf_op jit(solution)/shard_map/ppermute | solution.py:300
  51.2 7.6 %collective-permute-start.14 = (bf16[2,256,128]{2,1,0:T(8,128)(2,1)S(1)}, bf16[2,256,128]{2,1,0:T(8,128)(2,1)S(1)}, u32[]{:S(2)}, u32[]{:S(2)}) collective-permute-start(bf16[2,256,128]{2,1,0:T(8,128)(2,1)S(1)} %get-tuple-element.75), channel_id=1, source_target_pairs={{0,4},{2,6},{4,0},{6,2},{8,12},{10,14},{12,8},{14,10},{16,20},{18,... | collective-permute-start | bytes 393224 | tf_op jit(solution)/shard_map/ppermute | solution.py:300
  54.4 6.6 %collective-permute-start.15 = (bf16[2,256,128]{2,1,0:T(8,128)(2,1)S(1)}, bf16[2,256,128]{2,1,0:T(8,128)(2,1)S(1)}, u32[]{:S(2)}, u32[]{:S(2)}) collective-permute-start(bf16[2,256,128]{2,1,0:T(8,128)(2,1)S(1)} %get-tuple-element.76), channel_id=1, source_target_pairs={{0,6},{2,4},{4,2},{6,0},{8,14},{10,12},{12,10},{14,8},{16,22},{18,... | collective-permute-start | bytes 393224 | tf_op jit(solution)/shard_map/ppermute | solution.py:300
  54.4 6.6 %collective-permute-start.8 = (bf16[2,256,128]{2,1,0:T(8,128)(2,1)S(1)}, bf16[2,256,128]{2,1,0:T(8,128)(2,1)S(1)}, u32[]{:S(2)}, u32[]{:S(2)}) collective-permute-start(bf16[2,256,128]{2,1,0:T(8,128)(2,1)S(1)} %get-tuple-element.62), channel_id=1, source_target_pairs={{0,2},{2,0},{4,6},{6,4},{8,10},{10,8},{12,14},{14,12},{16,18},{18,... | collective-permute-start | bytes 393224 | tf_op jit(solution)/shard_map/ppermute | solution.py:300
  56.0 6.5 %collective-permute-start.16 = (bf16[32,640]{1,0:T(8,128)(2,1)S(1)}, bf16[32,640]{1,0:T(8,128)(2,1)S(1)}, u32[]{:S(2)}, u32[]{:S(2)}) collective-permute-start(bf16[32,640]{1,0:T(8,128)(2,1)S(1)} %reduce-precision_convert_fusion.s0), channel_id=1, source_target_pairs={{0,2},{2,0},{4,6},{6,4},{8,10},{10,8},{12,14},{14,12},{16,18},{18,... | collective-permute-start | bytes 122888 | tf_op jit(solution)/shard_map/ppermute | solution.py:300
  56.0 6.5 %collective-permute-start.17 = (bf16[32,640]{1,0:T(8,128)(2,1)S(1)}, bf16[32,640]{1,0:T(8,128)(2,1)S(1)}, u32[]{:S(2)}, u32[]{:S(2)}) collective-permute-start(bf16[32,640]{1,0:T(8,128)(2,1)S(1)} %reduce-precision_convert_fusion.s0), channel_id=1, source_target_pairs={{0,4},{2,6},{4,0},{6,2},{8,12},{10,14},{12,8},{14,10},{16,20},{18,... | collective-permute-start | bytes 122888 | tf_op jit(solution)/shard_map/ppermute | solution.py:300
  58.8 4.0 %collective-permute-start.18 = (bf16[32,640]{1,0:T(8,128)(2,1)S(1)}, bf16[32,640]{1,0:T(8,128)(2,1)S(1)}, u32[]{:S(2)}, u32[]{:S(2)}) collective-permute-start(bf16[32,640]{1,0:T(8,128)(2,1)S(1)} %reduce-precision_convert_fusion.s0), channel_id=1, source_target_pairs={{0,6},{2,4},{4,2},{6,0},{8,14},{10,12},{12,10},{14,8},{16,22},{18,... | collective-permute-start | bytes 122888 | tf_op jit(solution)/shard_map/ppermute | solution.py:300

commit v5 on v4

--- a/solution.py
+++ b/solution.py
@@ -65,21 +65,21 @@
     return total
 
 
-def gather_blocks(q, pieces, near, far, xs, ys):
+def gather_blocks(q, pieces, near, two, three, xs, ys):
     for m, piece in enumerate(pieces):
         xs[SPAN + (q ^ m)] = piece[0]
         ys[q ^ m] = piece[1]
     for m in range(SPAN):
-        x_part, y_part = near if m < 2 else far
-        xs[q ^ m] = x_part[m % 2]
-        ys[SPAN + (q ^ m)] = y_part[m % 2]
+        x_part, y_part = (near, near, two, three)[m]
+        xs[q ^ m] = x_part[m if m < 2 else 0]
+        ys[SPAN + (q ^ m)] = y_part[m if m < 2 else 0]
 
 
 def state_kernel(
-    q_ref, rate_ref, row_ref, p0, p1, p2, p3, xa, xb, ya, yb,
+    q_ref, rate_ref, row_ref, p0, p1, p2, p3, xa, xb, xc, ya, yb, yc,
     car_ref, ret_ref, end_ref, ahead_ref, behind_ref, mail_ref, cross_ref, xs, ys,
 ):
-    gather_blocks(q_ref[0] & 3, (p0, p1, p2, p3), (xa, ya), (xb, yb), xs, ys)
+    gather_blocks(q_ref[0] & 3, (p0, p1, p2, p3), (xa, ya), (xb, yb), (xc, yc), xs, ys)
     rate = rate_ref[...].reshape(BLK, BLK)
     tok = lanes_of(BLK).astype(F32)
     row = row_ref[0, 0:1, :]
@@ -132,14 +132,14 @@
 
 
 def lag_kernel(
-    q_ref, rate_ref, row_ref, root_ref, cross_ref, p0, p1, p2, p3, ya, yb, lag_ref, xs, ys, sums,
+    q_ref, rate_ref, row_ref, root_ref, cross_ref, p0, p1, p2, p3, ya, yb, yc, lag_ref, xs, ys, sums,
     *, scale,
 ):
     q = q_ref[0] & 3
     for m, piece in enumerate((p0, p1, p2, p3)):
         xs[q ^ m] = piece[0]
         ys[q ^ m] = piece[1]
-        ys[SPAN + (q ^ m)] = (ya if m < 2 else yb)[m % 2]
+        ys[SPAN + (q ^ m)] = (ya, ya, yb, yc)[m][m if m < 2 else 0]
     row_at = lax.broadcasted_iota(jnp.int32, (BLK, BLK), 0)
     causal = lanes_of(BLK) >= row_at
     lane8 = lanes_of(8)
@@ -198,10 +198,10 @@
 
 def main_kernel(
     q_ref, rate_ref, gain_ref, row_ref, table_ref, car_ref, ret_ref, before_ref, after_ref,
-    p0, p1, p2, p3, xa, xb, ya, yb, o0, o1, o2, o3, xs, ys, fs, bs,
+    p0, p1, p2, p3, xa, xb, xc, ya, yb, yc, o0, o1, o2, o3, xs, ys, fs, bs,
 ):
     q = q_ref[0] & 3
-    gather_blocks(q, (p0, p1, p2, p3), (xa, ya), (xb, yb), xs, ys)
+    gather_blocks(q, (p0, p1, p2, p3), (xa, ya), (xb, yb), (xc, yc), xs, ys)
     rate = rate_ref[...].reshape(BLK, BLK)
     gain = gain_ref[...].reshape(BLK, BLK)
     tok = lanes_of(BLK).astype(F32)
@@ -316,7 +316,8 @@
             ]
         )
 
-    pieces = [part(0)] + [swap(part(m), m) for m in range(1, ranks)]
+    mate, late = lax.optimization_barrier((swap(part(1), 1), part(2)))
+    pieces = [part(0), mate, swap(late, 2), swap(part(3), 3)]
 
     x_near = shift(jnp.stack([pieces[0][0], pieces[1][0]]), 1)
     y_near = shift(jnp.stack([pieces[0][1], pieces[1][1]]), -1)
@@ -370,11 +371,13 @@
             name=name,
         )
 
-    pieces[2], pieces[3], x_near, y_near, rate_row, root_row = lax.optimization_barrier(
-        (pieces[2], pieces[3], x_near, y_near, rate_row, root_row)
+    x_three = shift(pieces[3][:1], 1)
+    y_three = shift(pieces[3][1:], -1)
+    pieces[2], x_near, y_near, rate_row, root_row = lax.optimization_barrier(
+        (pieces[2], x_near, y_near, rate_row, root_row)
     )
-    x_far = shift(jnp.stack([pieces[2][0], pieces[3][0]]), 1)
-    y_far = shift(jnp.stack([pieces[2][1], pieces[3][1]]), -1)
+    x_two = shift(pieces[2][:1], 1)
+    y_two = shift(pieces[2][1:], -1)
 
     few = ("few", 0)
     one = ("one", 0)
@@ -393,10 +396,10 @@
     store = jax.ShapeDtypeStruct((steps, SPAN - 1, BLK, BLK), BF16)
     small = jax.ShapeDtypeStruct((steps, GROUP, BLK), F32)
     blocks = pltpu.VMEM((2 * SPAN, rows, BLK), BF16)
-    halo = (x_near, x_far, y_near, y_far)
+    halo = (x_near, x_two, x_three, y_near, y_two, y_three)
     carried, returned, ends, ahead, behind, mail, cross = looped(
         state_kernel,
-        [("all", 0), few, one] + [pair] * 8 + [one] * 7,
+        [("all", 0), few, one] + [pair] * 10 + [one] * 7,
         steps,
         "states",
         [store] * 2 + [small] * 5,
@@ -419,7 +422,7 @@
 
     (lag,) = looped(
         functools.partial(lag_kernel, scale=scale),
-        [("all", 0), few, one, one, one] + [pair] * 6 + [few],
+        [("all", 0), few, one, one, one] + [pair] * 7 + [few],
         steps,
         "lags",
         [jax.ShapeDtypeStruct((local, WIDE), F32)],
@@ -428,7 +431,7 @@
             blocks,
             pltpu.VMEM((STEP, 8, WIDE), F32),
         ],
-    )(q_arr, rate_wide, rate_row, root_row, cross, *pieces, y_near, y_far)
+    )(q_arr, rate_wide, rate_row, root_row, cross, *pieces, y_near, y_two, y_three)
     before, after, lag = lax.optimization_barrier((before, after, lag))
 
     back = []
@@ -439,7 +442,7 @@
         outs = looped(
             main_kernel,
             [("all", 0)]
-            + [(kind, at) for kind in ["few", "few", "one", "few"] + ["one"] * 4 + ["pair"] * 8]
+            + [(kind, at) for kind in ["few", "few", "one", "few"] + ["one"] * 4 + ["pair"] * 10]
             + [pair] * 4,
             steps // parts,
             "convs",
@@ -450,7 +453,6 @@
             *pieces, *halo,
         )
         outs = list(outs)
-        outs[0], q_next = lax.optimization_barrier((outs[0], q_arr))
         back += [outs[0]] + [swap(outs[m], m) for m in range(1, ranks)]
 
     back[0], lag = lax.optimization_barrier((back[0], lag))

time: 63.7 us -> 62.4 us (0.980)
  waiting for transfers between devices: 19.2 us -> 7.61 us
  starting transfers between devices: 21.6 us -> 31.9 us
    ppermute x15, waiting for transfers between devices: 15.1 us -> 5.48 us  [swap(): return lax.ppermute(value, 'ctx', [(i, i ^ m) for i in range(devices)])]
    ppermute x4 -> x6, starting transfers between devices: 10.1 us -> 15.7 us  [shift(): lax.ppermute(value, 'ctx', [(i, i + by) for i in range(devices) if 0 <= i...]
    ppermute x15, starting transfers between devices: 11.5 us -> 16.2 us  [swap(): return lax.ppermute(value, 'ctx', [(i, i ^ m) for i in range(devices)])]
    ppermute x4 -> x6, waiting for transfers between devices: 4.07 us -> 2.13 us  [shift(): lax.ppermute(value, 'ctx', [(i, i + by) for i in range(devices) if 0 <= i...]
  transfers between devices with their start and end apart: 19 -> 21, of which waited for: 10 -> 6; matrix products, arithmetic and copies ran while one was open for 2% -> 2% of each run, Pallas kernels for 21% -> 21%
where the time goes in v5:
time: 62.4 us; the launch traced here: 62.1 us
  starting transfers between devices  31.9 us (51%)
  Pallas kernels  18.7 us (30%)
  waiting for transfers between devices  7.61 us (12%)
  other arithmetic  2.25 us (4%)
  between operations  0.97 us (2%)
  local copies, waits for them, and re-layouts  0.74 us (1%)
    ppermute x15, starting transfers between devices, swap(): return lax.ppermute(value, 'ctx', [(i, i ^ m) for i in range(devices)])  16.2 us
    ppermute x6, starting transfers between devices, shift(): lax.ppermute(value, 'ctx', [(i, i + by) for i in range(devices) if 0 <= i...  15.7 us
    pallas_call x1, Pallas kernels, body(): looped(functools.partial(lag_kernel, scale=scale), [('all', 0), few, one,...  5.83 us
    ppermute x15, waiting for transfers between devices, swap(): return lax.ppermute(value, 'ctx', [(i, i ^ m) for i in range(devices)])  5.48 us
    pallas_call x2, Pallas kernels, body(): looped(main_kernel, [('all', 0)] + [(kind, at) for kind in ['few', 'few',...  4.11 us
    pallas_call x1, Pallas kernels, body(): looped(table_kernel, [one, few, few, few, few, one], steps, 'tables', [ja...  3.82 us
    pallas_call x1, Pallas kernels, body(): looped(state_kernel, [('all', 0), few, one] + [pair] * 10 + [one] * 7, st...  2.47 us
    ppermute x6, waiting for transfers between devices, shift(): lax.ppermute(value, 'ctx', [(i, i + by) for i in range(devices) if 0 <= i...  2.13 us
  transfers between devices with their start and end apart: 21, of which 6 were waited for; matrix products, arithmetic and copies ran while one was open for 2% of the time, Pallas kernels for 21%

profile of v5, /device:TPU:0, one launch (start us, length us, event | category | flops | bytes accessed | tf_op | source)
XLA Modules:
  0.0 62.1 jit_solution(17150704664810170240)
XLA Ops:
  0.6 0.0 copy-start
  0.7 1.9 %fusion.6 = (bf16[1,512,128]{2,1,0:T(8,128)(2,1)S(1)}, bf16[1,512,128]{2,1,0:T(8,128)(2,1)S(1)}, bf16[1,512,128]{2,1,0:T(8,128)(2,1)S(1)}, bf16[1,512,128]{2,1,0...) fusion(bf16[2048,128]{1,0:T(8,128)(2,1)} %refs_9_.1, ...), kind=kLoop, calls=%fused_computation.20 | loop fusion | flops 2097152 | bytes 3145744 | tf_op jit(solution)/shard_map/stack | solution.py:312
  2.6 0.5 collective-permute-start
  3.2 2.7 %collective-permute-start.4 = (bf16[2,512,128]{2,1,0:T(8,128)(2,1)S(1)}, bf16[2,512,128]{2,1,0:T(8,128)(2,1)S(1)}, u32[]{:S(2)}, u32[]{:S(2)}) collective-permute-start(bf16[2,512,128]{2,1,0:T(8,128)(2,1)S(1)} %pad_maximum_fusion.5), channel_id=1, source_target_pairs={{0,6},{2,4},{4,2},{6,0},{8,14},{10,12},{12,10},{14,8},{16,22},{18,... | collective-permute-start | bytes 786440 | tf_op jit(solution)/shard_map/ppermute | solution.py:300
  5.9 0.1 pad_maximum_fusion
  6.0 3.5 %collective-permute-start.2 = (bf16[2,512,128]{2,1,0:T(8,128)(2,1)S(1)}, bf16[2,512,128]{2,1,0:T(8,128)(2,1)S(1)}, u32[]{:S(2)}, u32[]{:S(2)}) collective-permute-start(bf16[2,512,128]{2,1,0:T(8,128)(2,1)S(1)} %get-tuple-element.95), channel_id=1, source_target_pairs={{0,8},{2,10},{4,12},{6,14},{8,16},{10,18},{12,20},{14,22},{16,24},... | collective-permute-start | bytes 786440 | tf_op jit(solution)/shard_map/ppermute | solution.py:304
  9.5 1.3 %collective-permute-start.3 = (bf16[2,512,128]{2,1,0:T(8,128)(2,1)S(1)}, bf16[2,512,128]{2,1,0:T(8,128)(2,1)S(1)}, u32[]{:S(2)}, u32[]{:S(2)}) collective-permute-start(bf16[2,512,128]{2,1,0:T(8,128)(2,1)S(1)} %get-tuple-element.94), channel_id=1, source_target_pairs={{8,0},{10,2},{12,4},{14,6},{16,8},{18,10},{20,12},{22,14},{24,16},... | collective-permute-start | bytes 786440 | tf_op jit(solution)/shard_map/ppermute | solution.py:304
  10.8 1.3 %collective-permute-start.1 = (bf16[2,512,128]{2,1,0:T(8,128)(2,1)S(1)}, bf16[2,512,128]{2,1,0:T(8,128)(2,1)S(1)}, u32[]{:S(2)}, u32[]{:S(2)}) collective-permute-start(bf16[2,512,128]{2,1,0:T(8,128)(2,1)S(1)} %pad_maximum_fusion.3), channel_id=1, source_target_pairs={{0,4},{2,6},{4,0},{6,2},{8,12},{10,14},{12,8},{14,10},{16,20},{18,... | collective-permute-start | bytes 786440 | tf_op jit(solution)/shard_map/ppermute | solution.py:300
  12.1 0.1 sqrt_bitcast_fusion
  12.2 0.1 copy.14
  12.3 0.1 broadcast_in_dim.28
  12.4 0.1 copy.17
  12.5 0.1 broadcast_in_dim.30
  12.6 0.0 collective-permute-done.4.refs_6_.refs_8_.refs_12_
  12.6 4.6 %collective-permute-start.6 = (bf16[1,512,128]{2,1,0:T(8,128)(2,1)S(1)}, bf16[1,512,128]{2,1,0:T(8,128)(2,1)S(1)}, u32[]{:S(2)}, u32[]{:S(2)}) collective-permute-start(bf16[1,512,128]{2,1,0:T(8,128)(2,1)S(1)} %get-tuple-element.88), channel_id=1, source_target_pairs={{0,8},{2,10},{4,12},{6,14},{8,16},{10,18},{12,20},{14,22},{16,24},... | collective-permute-start | bytes 393224 | tf_op jit(solution)/shard_map/ppermute | solution.py:304
  17.1 1.3 %collective-permute-start.8 = (bf16[1,512,128]{2,1,0:T(8,128)(2,1)S(1)}, bf16[1,512,128]{2,1,0:T(8,128)(2,1)S(1)}, u32[]{:S(2)}, u32[]{:S(2)}) collective-permute-start(bf16[1,512,128]{2,1,0:T(8,128)(2,1)S(1)} %get-tuple-element.87), channel_id=1, source_target_pairs={{8,0},{10,2},{12,4},{14,6},{16,8},{18,10},{20,12},{22,14},{24,16},... | collective-permute-start | bytes 393224 | tf_op jit(solution)/shard_map/ppermute | solution.py:304
  18.5 0.9 %collective-permute-done.3.refs_10_.refs_9_.refs_16_ = bf16[2,512,128]{2,1,0:T(8,128)(2,1)S(1)} collective-permute-done((bf16[2,512,128]{2,1,0:T(8,128)(2,1)S(1)}, bf16[2,512,128]{2,1,0:T(8,128)(2,1)S(1)}, u32[]{:S(2)}, u32[]{:S(2)}) %collective-permute-start.3) | collective-permute-done | bytes 262176 | tf_op jit(solution)/shard_map/ppermute | solution.py:304
  19.4 3.7 %collective-permute-start.5 = (bf16[1,512,128]{2,1,0:T(8,128)(2,1)S(1)}, bf16[1,512,128]{2,1,0:T(8,128)(2,1)S(1)}, u32[]{:S(2)}, u32[]{:S(2)}) collective-permute-start(bf16[1,512,128]{2,1,0:T(8,128)(2,1)S(1)} %get-tuple-element.90), channel_id=1, source_target_pairs={{0,8},{2,10},{4,12},{6,14},{8,16},{10,18},{12,20},{14,22},{16,24},... | collective-permute-start | bytes 393224 | tf_op jit(solution)/shard_map/ppermute | solution.py:304
  23.1 1.3 %collective-permute-start.7 = (bf16[1,512,128]{2,1,0:T(8,128)(2,1)S(1)}, bf16[1,512,128]{2,1,0:T(8,128)(2,1)S(1)}, u32[]{:S(2)}, u32[]{:S(2)}) collective-permute-start(bf16[1,512,128]{2,1,0:T(8,128)(2,1)S(1)} %get-tuple-element.89), channel_id=1, source_target_pairs={{8,0},{10,2},{12,4},{14,6},{16,8},{18,10},{20,12},{22,14},{24,16},... | collective-permute-start | bytes 393224 | tf_op jit(solution)/shard_map/ppermute | solution.py:304
  24.4 0.1 bitcast_multiply_fusion
  24.5 0.1 copy.15
  24.6 0.1 broadcast_in_dim.12.refs_1_
  24.7 0.1 broadcast_in_dim.13.refs_2_
  24.9 3.8 %tables.1 = (bf16[32,128,640]{2,1,0:T(8,128)(2,1)S(1)}, f32[4,8,128]{2,1,0:T(8,128)S(1)}) custom-call(f32[4,8,128]{2,1,0:T(8,128)S(1)} %broadcast_in_dim.29.refs_0_, f32[32,16,128]{2,1,0:T(8,128)S(1)} %broadcast_in_dim.12.refs_1_, f32[32,16,128]{2,1,0:T(8,128)S(1)} %broadcast_in_dim.13.refs_2_, bf16[32,512]{1,0:T(8,128)(2,1)S(1)} %constant_dynamic-slice_fusion.refs_3_), custom_call_target="tpu_custom_call" | custom-call | tf_op jit(solution)/shard_map/tables/pallas_call | solution.py:385
  28.7 1.2 %collective-permute-done.7.refs_11_.refs_10_.refs_17_ = bf16[1,512,128]{2,1,0:T(8,128)(2,1)S(1)} collective-permute-done((bf16[1,512,128]{2,1,0:T(8,128)(2,1)S(1)}, bf16[1,512,128]{2,1,0:T(8,128)(2,1)S(1)}, u32[]{:S(2)}, u32[]{:S(2)}) %collective-permute-start.7) | collective-permute-done | bytes 131104 | tf_op jit(solution)/shard_map/ppermute | solution.py:304
  30.0 2.5 %states.1 = (bf16[4,3,128,128]{3,2,1,0:T(8,128)(2,1)S(1)}, bf16[4,3,128,128]{3,2,1,0:T(8,128)(2,1)S(1)}, f32[4,16,128]{2,1,0:T(8,128)S(1)}, f32[4,16,128]{2,1,0:...) custom-call(s32[1]{0:T(128)} %bitcast.refs_0_.q_ref, ...), custom_call_target="tpu_custom_call" | custom-call | tf_op jit(solution)/shard_map/states/pallas_call | solution.py:400
  32.4 2.6 %collective-permute-start.9 = (f32[4,16,128]{2,1,0:T(8,128)S(1)}, f32[4,16,128]{2,1,0:T(8,128)S(1)}, u32[]{:S(2)}, u32[]{:S(2)}) collective-permute-start(f32[4,16,128]{2,1,0:T(8,128)S(1)} %get-tuple-element.52), channel_id=1, source_target_pairs={{0,16},{2,18},{4,20},{6,22},{8,24},{10,26},{12,28},{14,30},{16,0},... | collective-permute-start | bytes 98312 | tf_op jit(solution)/shard_map/ppermute | solution.py:300
  35.0 5.8 %lags.1.lag_ref = f32[32,640]{1,0:T(8,128)S(1)} custom-call(s32[1]{0:T(128)} %bitcast.refs_0_.q_ref, f32[32,16,128]{2,1,0:T(8,128)S(1)} %broadcast_in_dim.12.refs_1_, f32[4,8,128]{2,1,0:T(8,128)S(1)} %get-tuple-element.45.refs_2_.refs_3_.row_ref, f32[4,8,128]{2,1,0:T(8,128)S(1)} %broadcast_in_dim.31.refs_3_.root_ref, ...), custom_call_target="tpu_custom_call" | custom-call | tf_op jit(solution)/shard_map/lags/pallas_call | solution.py:423
  40.9 2.1 %convs.2 = (bf16[2,256,128]{2,1,0:T(8,128)(2,1)S(1)}, bf16[2,256,128]{2,1,0:T(8,128)(2,1)S(1)}, bf16[2,256,128]{2,1,0:T(8,128)(2,1)S(1)}, bf16[2,256,128]{2,1,0:T(8,128)(2,1)S(1)}) custom-call(s32[1]{0:T(128)} %bitcast.refs_0_.q_ref, f32[32,16,128]{2,1,0:T(8,128)S(1)} %broadcast_in_dim.12.refs_1_, f32[32,16,128]{2,1,0:T(8,128)S(1)} %broadcast_in_dim.13.refs_2_, ...), custom_call_target="tpu_custom_call" | custom-call | tf_op jit(solution)/shard_map/convs/pallas_call | solution.py:442
  42.9 0.0 copy-start.1
  43.0 0.0 copy-start.2
  43.0 0.0 copy-start.3
  43.0 0.2 joins.1
  43.2 1.5 %collective-permute-start.13 = (f32[32,640]{1,0:T(8,128)S(1)}, f32[32,640]{1,0:T(8,128)S(1)}, u32[]{:S(2)}, u32[]{:S(2)}) collective-permute-start(f32[32,640]{1,0:T(8,128)S(1)} %joins.1), channel_id=1, source_target_pairs={{0,8},{2,10},{4,12},{6,14},{8,0},{10,2},{12,4},{14,6},{16,24},{18,... | collective-permute-start | bytes 245768 | tf_op jit(solution)/shard_map/ppermute | solution.py:300
  44.7 1.4 %collective-permute-start.11 = (bf16[2,256,128]{2,1,0:T(8,128)(2,1)S(1)}, bf16[2,256,128]{2,1,0:T(8,128)(2,1)S(1)}, u32[]{:S(2)}, u32[]{:S(2)}) collective-permute-start(bf16[2,256,128]{2,1,0:T(8,128)(2,1)S(1)} %get-tuple-element.61), channel_id=1, source_target_pairs={{0,4},{2,6},{4,0},{6,2},{8,12},{10,14},{12,8},{14,10},{16,20},{18,... | collective-permute-start | bytes 393224 | tf_op jit(solution)/shard_map/ppermute | solution.py:300
  46.1 2.0 %convs.3 = (bf16[2,256,128]{2,1,0:T(8,128)(2,1)S(1)}, bf16[2,256,128]{2,1,0:T(8,128)(2,1)S(1)}, bf16[2,256,128]{2,1,0:T(8,128)(2,1)S(1)}, bf16[2,256,128]{2,1,0:T(8,128)(2,1)S(1)}) custom-call(s32[1]{0:T(128)} %bitcast.refs_0_.q_ref, f32[32,16,128]{2,1,0:T(8,128)S(1)} %broadcast_in_dim.12.refs_1_, f32[32,16,128]{2,1,0:T(8,128)S(1)} %broadcast_in_dim.13.refs_2_, ...), custom_call_target="tpu_custom_call" | custom-call | tf_op jit(solution)/shard_map/convs/pallas_call | solution.py:442
  48.1 0.6 collective-permute-start.14
  48.7 0.9 %collective-permute-start.15 = (bf16[2,256,128]{2,1,0:T(8,128)(2,1)S(1)}, bf16[2,256,128]{2,1,0:T(8,128)(2,1)S(1)}, u32[]{:S(2)}, u32[]{:S(2)}) collective-permute-start(bf16[2,256,128]{2,1,0:T(8,128)(2,1)S(1)} %get-tuple-element.70), channel_id=1, source_target_pairs={{0,2},{2,0},{4,6},{6,4},{8,10},{10,8},{12,14},{14,12},{16,18},{18,... | collective-permute-start | bytes 393224 | tf_op jit(solution)/shard_map/ppermute | solution.py:300
  49.6 1.2 %collective-permute-start.16 = (bf16[2,256,128]{2,1,0:T(8,128)(2,1)S(1)}, bf16[2,256,128]{2,1,0:T(8,128)(2,1)S(1)}, u32[]{:S(2)}, u32[]{:S(2)}) collective-permute-start(bf16[2,256,128]{2,1,0:T(8,128)(2,1)S(1)} %get-tuple-element.71), channel_id=1, source_target_pairs={{0,4},{2,6},{4,0},{6,2},{8,12},{10,14},{12,8},{14,10},{16,20},{18,... | collective-permute-start | bytes 393224 | tf_op jit(solution)/shard_map/ppermute | solution.py:300
  50.8 2.3 %collective-permute-done.14 = bf16[32,640]{1,0:T(8,128)(2,1)S(1)} collective-permute-done((bf16[32,640]{1,0:T(8,128)(2,1)S(1)}, bf16[32,640]{1,0:T(8,128)(2,1)S(1)}, u32[]{:S(2)}, u32[]{:S(2)}) %collective-permute-start.14) | collective-permute-done | bytes 40992 | tf_op jit(solution)/shard_map/ppermute | solution.py:300
  53.1 1.1 %collective-permute-start.10 = (bf16[2,256,128]{2,1,0:T(8,128)(2,1)S(1)}, bf16[2,256,128]{2,1,0:T(8,128)(2,1)S(1)}, u32[]{:S(2)}, u32[]{:S(2)}) collective-permute-start(bf16[2,256,128]{2,1,0:T(8,128)(2,1)S(1)} %get-tuple-element.60), channel_id=1, source_target_pairs={{0,2},{2,0},{4,6},{6,4},{8,10},{10,8},{12,14},{14,12},{16,18},{18,... | collective-permute-start | bytes 393224 | tf_op jit(solution)/shard_map/ppermute | solution.py:300
  54.2 0.2 collective-permute-done.12.refs_3_
  54.4 1.0 %collective-permute-start.19 = (bf16[32,640]{1,0:T(8,128)(2,1)S(1)}, bf16[32,640]{1,0:T(8,128)(2,1)S(1)}, u32[]{:S(2)}, u32[]{:S(2)}) collective-permute-start(bf16[32,640]{1,0:T(8,128)(2,1)S(1)} %reduce-precision_convert_fusion.s0), channel_id=1, source_target_pairs={{0,4},{2,6},{4,0},{6,2},{8,12},{10,14},{12,8},{14,10},{16,20},{18,... | collective-permute-start | bytes 122888 | tf_op jit(solution)/shard_map/ppermute | solution.py:300
  55.4 0.6 collective-permute-done.16.refs_6_
  56.0 1.5 %collective-permute-start.20 = (bf16[32,640]{1,0:T(8,128)(2,1)S(1)}, bf16[32,640]{1,0:T(8,128)(2,1)S(1)}, u32[]{:S(2)}, u32[]{:S(2)}) collective-permute-start(bf16[32,640]{1,0:T(8,128)(2,1)S(1)} %reduce-precision_convert_fusion.s0), channel_id=1, source_target_pairs={{0,6},{2,4},{4,2},{6,0},{8,14},{10,12},{12,10},{14,8},{16,22},{18,... | collective-permute-start | bytes 122888 | tf_op jit(solution)/shard_map/ppermute | solution.py:300
  57.5 2.4 %collective-permute-done.17.refs_7_ = bf16[2,256,128]{2,1,0:T(8,128)(2,1)S(1)} collective-permute-done((bf16[2,256,128]{2,1,0:T(8,128)(2,1)S(1)}, bf16[2,256,128]{2,1,0:T(8,128)(2,1)S(1)}, u32[]{:S(2)}, u32[]{:S(2)}) %collective-permute-start.17) | collective-permute-done | bytes 131104 | tf_op jit(solution)/shard_map/ppermute | solution.py:300
  59.9 1.5 %gates.1 = (bf16[2048,128]{1,0:T(8,128)(2,1)}, bf16[2048,128]{1,0:T(8,128)(2,1)}, bf16[2048,128]{1,0:T(8,128)(2,1)}) custom-call(s32[1]{0:T(128)} %bitcast.refs_0_.q_ref, bf16[2,256,128]{2,1,0:T(8,128)(2,1)S(1)} %get-tuple-element.59.refs_0_, bf16[2,256,128]{2,1,0:T(8,128)(2,1)S(1)} %collective-permute-done.10.refs_1_, ...), custom_call_target="tpu_custom_call" | custom-call | tf_op jit(solution)/shard_map/gates/pallas_call | solution.py:478
  61.4 0.7 %sums.1 = (f32[128,512]{1,0:T(8,128)}, f32[16,128]{1,0:T(8,128)}) custom-call(s32[1]{0:T(128)} %bitcast.refs_0_.q_ref, bf16[32,640]{1,0:T(8,128)(2,1)S(1)} %reduce-precision_convert_fusion.s0, bf16[32,640]{1,0:T(8,128)(2,1)S(1)} %collective-permute-done.18.s1, bf16[32,640]{1,0:T(8,128)(2,1)S(1)} %collective-permute-done.19.s2, ...), custom_call_target="tpu_custom_call" | custom-call | tf_op jit(solution)/shard_map/sums/pallas_call | solution.py:486
  (36 shorter events, 0.2 us)
Async XLA Ops:
  0.6 24.0 %copy-start = (bf16[128,512]{1,0:T(8,128)(2,1)S(1)}, bf16[128,512]{1,0:T(8,128)(2,1)}, u32[]{:S(2)}) copy-start(bf16[128,512]{1,0:T(8,128)(2,1)} %param.11) | copy-start | bytes 393220
  0.6 11.5 %copy-start.4 = (f32[16,128]{1,0:T(8,128)S(1)}, f32[16,128]{1,0:T(8,128)}, u32[]{:S(2)}) copy-start(f32[16,128]{1,0:T(8,128)} %param.13) | copy-start | bytes 24580
  0.7 23.8 %copy-start.5 = (f32[16,128]{1,0:T(8,128)S(1)}, f32[16,128]{1,0:T(8,128)}, u32[]{:S(2)}) copy-start(f32[16,128]{1,0:T(8,128)} %param.12) | copy-start | bytes 24580
  2.6 3.2 %collective-permute-start = (bf16[2,512,128]{2,1,0:T(8,128)(2,1)S(1)}, bf16[2,512,128]{2,1,0:T(8,128)(2,1)S(1)}, u32[]{:S(2)}, u32[]{:S(2)}) collective-permute-start(bf16[2,512,128]{2,1,0:T(8,128)(2,1)S(1)} %pad_maximum_fusion.2), channel_id=1, source_target_pairs={{0,2},{2,0},{4,6},{6,4},{8,10},{10,8},{12,14},{14,12},{16,18},{18,... | collective-permute-start | bytes 786440 | tf_op jit(solution)/shard_map/ppermute | solution.py:300
  3.2 9.4 %collective-permute-start.4 = (bf16[2,512,128]{2,1,0:T(8,128)(2,1)S(1)}, bf16[2,512,128]{2,1,0:T(8,128)(2,1)S(1)}, u32[]{:S(2)}, u32[]{:S(2)}) collective-permute-start(bf16[2,512,128]{2,1,0:T(8,128)(2,1)S(1)} %pad_maximum_fusion.5), channel_id=1, source_target_pairs={{0,6},{2,4},{4,2},{6,0},{8,14},{10,12},{12,10},{14,8},{16,22},{18,... | collective-permute-start | bytes 786440 | tf_op jit(solution)/shard_map/ppermute | solution.py:300
  6.0 12.5 %collective-permute-start.2 = (bf16[2,512,128]{2,1,0:T(8,128)(2,1)S(1)}, bf16[2,512,128]{2,1,0:T(8,128)(2,1)S(1)}, u32[]{:S(2)}, u32[]{:S(2)}) collective-permute-start(bf16[2,512,128]{2,1,0:T(8,128)(2,1)S(1)} %get-tuple-element.95), channel_id=1, source_target_pairs={{0,8},{2,10},{4,12},{6,14},{8,16},{10,18},{12,20},{14,22},{16,24},... | collective-permute-start | bytes 786440 | tf_op jit(solution)/shard_map/ppermute | solution.py:304
  9.5 9.8 %collective-permute-start.3 = (bf16[2,512,128]{2,1,0:T(8,128)(2,1)S(1)}, bf16[2,512,128]{2,1,0:T(8,128)(2,1)S(1)}, u32[]{:S(2)}, u32[]{:S(2)}) collective-permute-start(bf16[2,512,128]{2,1,0:T(8,128)(2,1)S(1)} %get-tuple-element.94), channel_id=1, source_target_pairs={{8,0},{10,2},{12,4},{14,6},{16,8},{18,10},{20,12},{22,14},{24,16},... | collective-permute-start | bytes 786440 | tf_op jit(solution)/shard_map/ppermute | solution.py:304
  10.8 8.5 %collective-permute-start.1 = (bf16[2,512,128]{2,1,0:T(8,128)(2,1)S(1)}, bf16[2,512,128]{2,1,0:T(8,128)(2,1)S(1)}, u32[]{:S(2)}, u32[]{:S(2)}) collective-permute-start(bf16[2,512,128]{2,1,0:T(8,128)(2,1)S(1)} %pad_maximum_fusion.3), channel_id=1, source_target_pairs={{0,4},{2,6},{4,0},{6,2},{8,12},{10,14},{12,8},{14,10},{16,20},{18,... | collective-permute-start | bytes 786440 | tf_op jit(solution)/shard_map/ppermute | solution.py:300
  12.6 16.1 %collective-permute-start.6 = (bf16[1,512,128]{2,1,0:T(8,128)(2,1)S(1)}, bf16[1,512,128]{2,1,0:T(8,128)(2,1)S(1)}, u32[]{:S(2)}, u32[]{:S(2)}) collective-permute-start(bf16[1,512,128]{2,1,0:T(8,128)(2,1)S(1)} %get-tuple-element.88), channel_id=1, source_target_pairs={{0,8},{2,10},{4,12},{6,14},{8,16},{10,18},{12,20},{14,22},{16,24},... | collective-permute-start | bytes 393224 | tf_op jit(solution)/shard_map/ppermute | solution.py:304
  17.1 11.6 %collective-permute-start.8 = (bf16[1,512,128]{2,1,0:T(8,128)(2,1)S(1)}, bf16[1,512,128]{2,1,0:T(8,128)(2,1)S(1)}, u32[]{:S(2)}, u32[]{:S(2)}) collective-permute-start(bf16[1,512,128]{2,1,0:T(8,128)(2,1)S(1)} %get-tuple-element.87), channel_id=1, source_target_pairs={{8,0},{10,2},{12,4},{14,6},{16,8},{18,10},{20,12},{22,14},{24,16},... | collective-permute-start | bytes 393224 | tf_op jit(solution)/shard_map/ppermute | solution.py:304
  19.4 9.4 %collective-permute-start.5 = (bf16[1,512,128]{2,1,0:T(8,128)(2,1)S(1)}, bf16[1,512,128]{2,1,0:T(8,128)(2,1)S(1)}, u32[]{:S(2)}, u32[]{:S(2)}) collective-permute-start(bf16[1,512,128]{2,1,0:T(8,128)(2,1)S(1)} %get-tuple-element.90), channel_id=1, source_target_pairs={{0,8},{2,10},{4,12},{6,14},{8,16},{10,18},{12,20},{14,22},{16,24},... | collective-permute-start | bytes 393224 | tf_op jit(solution)/shard_map/ppermute | solution.py:304
  23.1 6.9 %collective-permute-start.7 = (bf16[1,512,128]{2,1,0:T(8,128)(2,1)S(1)}, bf16[1,512,128]{2,1,0:T(8,128)(2,1)S(1)}, u32[]{:S(2)}, u32[]{:S(2)}) collective-permute-start(bf16[1,512,128]{2,1,0:T(8,128)(2,1)S(1)} %get-tuple-element.89), channel_id=1, source_target_pairs={{8,0},{10,2},{12,4},{14,6},{16,8},{18,10},{20,12},{22,14},{24,16},... | collective-permute-start | bytes 393224 | tf_op jit(solution)/shard_map/ppermute | solution.py:304
  32.4 8.4 %collective-permute-start.9 = (f32[4,16,128]{2,1,0:T(8,128)S(1)}, f32[4,16,128]{2,1,0:T(8,128)S(1)}, u32[]{:S(2)}, u32[]{:S(2)}) collective-permute-start(f32[4,16,128]{2,1,0:T(8,128)S(1)} %get-tuple-element.52), channel_id=1, source_target_pairs={{0,16},{2,18},{4,20},{6,22},{8,24},{10,26},{12,28},{14,30},{16,0},... | collective-permute-start | bytes 98312 | tf_op jit(solution)/shard_map/ppermute | solution.py:300
  42.9 16.9 %copy-start.1 = (bf16[2048,128]{1,0:T(8,128)(2,1)S(1)}, bf16[2048,128]{1,0:T(8,128)(2,1)}, u32[]{:S(2)}) copy-start(bf16[2048,128]{1,0:T(8,128)(2,1)} %refs_9_.1) | copy-start | bytes 1572868
  43.0 16.9 %copy-start.2 = (bf16[2048,128]{1,0:T(8,128)(2,1)S(1)}, bf16[2048,128]{1,0:T(8,128)(2,1)}, u32[]{:S(2)}) copy-start(bf16[2048,128]{1,0:T(8,128)(2,1)} %refs_10_.1) | copy-start | bytes 1572868
  43.0 16.9 %copy-start.3 = (bf16[2048,128]{1,0:T(8,128)(2,1)S(1)}, bf16[2048,128]{1,0:T(8,128)(2,1)}, u32[]{:S(2)}) copy-start(bf16[2048,128]{1,0:T(8,128)(2,1)} %refs_8_.1) | copy-start | bytes 1572868
  43.2 4.9 %collective-permute-start.13 = (f32[32,640]{1,0:T(8,128)S(1)}, f32[32,640]{1,0:T(8,128)S(1)}, u32[]{:S(2)}, u32[]{:S(2)}) collective-permute-start(f32[32,640]{1,0:T(8,128)S(1)} %joins.1), channel_id=1, source_target_pairs={{0,8},{2,10},{4,12},{6,14},{8,0},{10,2},{12,4},{14,6},{16,24},{18,... | collective-permute-start | bytes 245768 | tf_op jit(solution)/shard_map/ppermute | solution.py:300
  44.7 8.4 %collective-permute-start.11 = (bf16[2,256,128]{2,1,0:T(8,128)(2,1)S(1)}, bf16[2,256,128]{2,1,0:T(8,128)(2,1)S(1)}, u32[]{:S(2)}, u32[]{:S(2)}) collective-permute-start(bf16[2,256,128]{2,1,0:T(8,128)(2,1)S(1)} %get-tuple-element.61), channel_id=1, source_target_pairs={{0,4},{2,6},{4,0},{6,2},{8,12},{10,14},{12,8},{14,10},{16,20},{18,... | collective-permute-start | bytes 393224 | tf_op jit(solution)/shard_map/ppermute | solution.py:300
  48.1 5.0 %collective-permute-start.14 = (bf16[32,640]{1,0:T(8,128)(2,1)S(1)}, bf16[32,640]{1,0:T(8,128)(2,1)S(1)}, u32[]{:S(2)}, u32[]{:S(2)}) collective-permute-start(bf16[32,640]{1,0:T(8,128)(2,1)S(1)} %reduce-precision_convert_fusion.1), channel_id=1, source_target_pairs={{0,16},{2,18},{4,20},{6,22},{8,24},{10,26},{12,28},{14,30},{16,0},... | collective-permute-start | bytes 122888 | tf_op jit(solution)/shard_map/ppermute | solution.py:300
  48.7 5.7 %collective-permute-start.12 = (bf16[2,256,128]{2,1,0:T(8,128)(2,1)S(1)}, bf16[2,256,128]{2,1,0:T(8,128)(2,1)S(1)}, u32[]{:S(2)}, u32[]{:S(2)}) collective-permute-start(bf16[2,256,128]{2,1,0:T(8,128)(2,1)S(1)} %get-tuple-element.62), channel_id=1, source_target_pairs={{0,6},{2,4},{4,2},{6,0},{8,14},{10,12},{12,10},{14,8},{16,22},{18,... | collective-permute-start | bytes 393224 | tf_op jit(solution)/shard_map/ppermute | solution.py:300
  48.7 5.8 %collective-permute-start.15 = (bf16[2,256,128]{2,1,0:T(8,128)(2,1)S(1)}, bf16[2,256,128]{2,1,0:T(8,128)(2,1)S(1)}, u32[]{:S(2)}, u32[]{:S(2)}) collective-permute-start(bf16[2,256,128]{2,1,0:T(8,128)(2,1)S(1)} %get-tuple-element.70), channel_id=1, source_target_pairs={{0,2},{2,0},{4,6},{6,4},{8,10},{10,8},{12,14},{14,12},{16,18},{18,... | collective-permute-start | bytes 393224 | tf_op jit(solution)/shard_map/ppermute | solution.py:300
  49.6 6.4 %collective-permute-start.16 = (bf16[2,256,128]{2,1,0:T(8,128)(2,1)S(1)}, bf16[2,256,128]{2,1,0:T(8,128)(2,1)S(1)}, u32[]{:S(2)}, u32[]{:S(2)}) collective-permute-start(bf16[2,256,128]{2,1,0:T(8,128)(2,1)S(1)} %get-tuple-element.71), channel_id=1, source_target_pairs={{0,4},{2,6},{4,0},{6,2},{8,12},{10,14},{12,8},{14,10},{16,20},{18,... | collective-permute-start | bytes 393224 | tf_op jit(solution)/shard_map/ppermute | solution.py:300
  53.1 6.8 %collective-permute-start.17 = (bf16[2,256,128]{2,1,0:T(8,128)(2,1)S(1)}, bf16[2,256,128]{2,1,0:T(8,128)(2,1)S(1)}, u32[]{:S(2)}, u32[]{:S(2)}) collective-permute-start(bf16[2,256,128]{2,1,0:T(8,128)(2,1)S(1)} %get-tuple-element.72), channel_id=1, source_target_pairs={{0,6},{2,4},{4,2},{6,0},{8,14},{10,12},{12,10},{14,8},{16,22},{18,... | collective-permute-start | bytes 393224 | tf_op jit(solution)/shard_map/ppermute | solution.py:300
  53.1 6.8 %collective-permute-start.10 = (bf16[2,256,128]{2,1,0:T(8,128)(2,1)S(1)}, bf16[2,256,128]{2,1,0:T(8,128)(2,1)S(1)}, u32[]{:S(2)}, u32[]{:S(2)}) collective-permute-start(bf16[2,256,128]{2,1,0:T(8,128)(2,1)S(1)} %get-tuple-element.60), channel_id=1, source_target_pairs={{0,2},{2,0},{4,6},{6,4},{8,10},{10,8},{12,14},{14,12},{16,18},{18,... | collective-permute-start | bytes 393224 | tf_op jit(solution)/shard_map/ppermute | solution.py:300
  54.4 7.0 %collective-permute-start.18 = (bf16[32,640]{1,0:T(8,128)(2,1)S(1)}, bf16[32,640]{1,0:T(8,128)(2,1)S(1)}, u32[]{:S(2)}, u32[]{:S(2)}) collective-permute-start(bf16[32,640]{1,0:T(8,128)(2,1)S(1)} %reduce-precision_convert_fusion.s0), channel_id=1, source_target_pairs={{0,2},{2,0},{4,6},{6,4},{8,10},{10,8},{12,14},{14,12},{16,18},{18,... | collective-permute-start | bytes 122888 | tf_op jit(solution)/shard_map/ppermute | solution.py:300
  54.4 7.0 %collective-permute-start.19 = (bf16[32,640]{1,0:T(8,128)(2,1)S(1)}, bf16[32,640]{1,0:T(8,128)(2,1)S(1)}, u32[]{:S(2)}, u32[]{:S(2)}) collective-permute-start(bf16[32,640]{1,0:T(8,128)(2,1)S(1)} %reduce-precision_convert_fusion.s0), channel_id=1, source_target_pairs={{0,4},{2,6},{4,0},{6,2},{8,12},{10,14},{12,8},{14,10},{16,20},{18,... | collective-permute-start | bytes 122888 | tf_op jit(solution)/shard_map/ppermute | solution.py:300
  56.0 5.4 %collective-permute-start.20 = (bf16[32,640]{1,0:T(8,128)(2,1)S(1)}, bf16[32,640]{1,0:T(8,128)(2,1)S(1)}, u32[]{:S(2)}, u32[]{:S(2)}) collective-permute-start(bf16[32,640]{1,0:T(8,128)(2,1)S(1)} %reduce-precision_convert_fusion.s0), channel_id=1, source_target_pairs={{0,6},{2,4},{4,2},{6,0},{8,14},{10,12},{12,10},{14,8},{16,22},{18,... | collective-permute-start | bytes 122888 | tf_op jit(solution)/shard_map/ppermute | solution.py:300

commit v6 on v5

--- a/solution.py
+++ b/solution.py
@@ -150,10 +150,14 @@
             [jnp.concatenate(y[o : o + SPAN], axis=0) for o in range(SPAN + 1)], axis=1
         )
         own_x = jnp.concatenate([xs[j, rows, :] for j in range(SPAN)], axis=0)
-        pairs = mm(own_x, wide_y, TN)
+        moved = roll_left(wide_y, 64)
+        last = jnp.where(lanes_of(SPAN * GROUP) < 64, moved[:, SPAN * BLK :], 0.0).astype(BF16)
+        moved = jnp.concatenate((moved[:, : SPAN * BLK], last), axis=1)
+        tall = jnp.concatenate((own_x[:, :64], pltpu.roll(own_x, 64, 1)[:, :64]), axis=0)
+        pairs = mm(tall, jnp.concatenate((wide_y, moved), axis=0), TN)
         tiles = [pairs[:, o * BLK : (o + 1) * BLK] for o in range(SPAN + 1)]
-        tiles[0] = jnp.where(causal, tiles[0], 0.0)
-        count = BLK // 8
+        tiles[0] = jnp.where(causal[:64], tiles[0], 0.0)
+        count = 8
         parts = [[tile[8 * i : 8 * (i + 1)] for i in range(count)] for tile in tiles]
         while count > 1:
             count //= 2

time: 62.4 us -> 62.1 us (level)
  no operation moved by 1% of the time
where the time goes in v6:
time: 62.1 us; the launch traced here: 61.9 us
  starting transfers between devices  31.9 us (51%)
  Pallas kernels  18.4 us (30%)
  waiting for transfers between devices  7.63 us (12%)
  other arithmetic  2.25 us (4%)
  between operations  0.97 us (2%)
  local copies, waits for them, and re-layouts  0.74 us (1%)
    ppermute x15, starting transfers between devices, swap(): return lax.ppermute(value, 'ctx', [(i, i ^ m) for i in range(devices)])  16.2 us
    ppermute x6, starting transfers between devices, shift(): lax.ppermute(value, 'ctx', [(i, i + by) for i in range(devices) if 0 <= i...  15.7 us
    pallas_call x1, Pallas kernels, body(): looped(functools.partial(lag_kernel, scale=scale), [('all', 0), few, one,...  5.57 us
    ppermute x15, waiting for transfers between devices, swap(): return lax.ppermute(value, 'ctx', [(i, i ^ m) for i in range(devices)])  5.5 us
    pallas_call x2, Pallas kernels, body(): looped(main_kernel, [('all', 0)] + [(kind, at) for kind in ['few', 'few',...  4.1 us
    pallas_call x1, Pallas kernels, body(): looped(table_kernel, [one, few, few, few, few, one], steps, 'tables', [ja...  3.82 us
    pallas_call x1, Pallas kernels, body(): looped(state_kernel, [('all', 0), few, one] + [pair] * 10 + [one] * 7, st...  2.47 us
    ppermute x6, waiting for transfers between devices, shift(): lax.ppermute(value, 'ctx', [(i, i + by) for i in range(devices) if 0 <= i...  2.13 us
  transfers between devices with their start and end apart: 21, of which 6 were waited for; matrix products, arithmetic and copies ran while one was open for 2% of the time, Pallas kernels for 21%

profile of v6, /device:TPU:0, one launch (start us, length us, event | category | flops | bytes accessed | tf_op | source)
XLA Modules:
  0.0 61.9 jit_solution(9930541064651225963)
XLA Ops:
  0.6 0.0 copy-start
  0.7 1.9 %fusion.6 = (bf16[1,512,128]{2,1,0:T(8,128)(2,1)S(1)}, bf16[1,512,128]{2,1,0:T(8,128)(2,1)S(1)}, bf16[1,512,128]{2,1,0:T(8,128)(2,1)S(1)}, bf16[1,512,128]{2,1,0...) fusion(bf16[2048,128]{1,0:T(8,128)(2,1)} %refs_9_.1, ...), kind=kLoop, calls=%fused_computation.20 | loop fusion | flops 2097152 | bytes 3145744 | tf_op jit(solution)/shard_map/stack | solution.py:316
  2.6 0.5 collective-permute-start
  3.2 2.7 %collective-permute-start.4 = (bf16[2,512,128]{2,1,0:T(8,128)(2,1)S(1)}, bf16[2,512,128]{2,1,0:T(8,128)(2,1)S(1)}, u32[]{:S(2)}, u32[]{:S(2)}) collective-permute-start(bf16[2,512,128]{2,1,0:T(8,128)(2,1)S(1)} %pad_maximum_fusion.5), channel_id=1, source_target_pairs={{0,6},{2,4},{4,2},{6,0},{8,14},{10,12},{12,10},{14,8},{16,22},{18,... | collective-permute-start | bytes 786440 | tf_op jit(solution)/shard_map/ppermute | solution.py:304
  5.9 0.1 pad_maximum_fusion
  6.0 3.5 %collective-permute-start.2 = (bf16[2,512,128]{2,1,0:T(8,128)(2,1)S(1)}, bf16[2,512,128]{2,1,0:T(8,128)(2,1)S(1)}, u32[]{:S(2)}, u32[]{:S(2)}) collective-permute-start(bf16[2,512,128]{2,1,0:T(8,128)(2,1)S(1)} %get-tuple-element.95), channel_id=1, source_target_pairs={{0,8},{2,10},{4,12},{6,14},{8,16},{10,18},{12,20},{14,22},{16,24},... | collective-permute-start | bytes 786440 | tf_op jit(solution)/shard_map/ppermute | solution.py:308
  9.5 1.3 %collective-permute-start.3 = (bf16[2,512,128]{2,1,0:T(8,128)(2,1)S(1)}, bf16[2,512,128]{2,1,0:T(8,128)(2,1)S(1)}, u32[]{:S(2)}, u32[]{:S(2)}) collective-permute-start(bf16[2,512,128]{2,1,0:T(8,128)(2,1)S(1)} %get-tuple-element.94), channel_id=1, source_target_pairs={{8,0},{10,2},{12,4},{14,6},{16,8},{18,10},{20,12},{22,14},{24,16},... | collective-permute-start | bytes 786440 | tf_op jit(solution)/shard_map/ppermute | solution.py:308
  10.8 1.3 %collective-permute-start.1 = (bf16[2,512,128]{2,1,0:T(8,128)(2,1)S(1)}, bf16[2,512,128]{2,1,0:T(8,128)(2,1)S(1)}, u32[]{:S(2)}, u32[]{:S(2)}) collective-permute-start(bf16[2,512,128]{2,1,0:T(8,128)(2,1)S(1)} %pad_maximum_fusion.3), channel_id=1, source_target_pairs={{0,4},{2,6},{4,0},{6,2},{8,12},{10,14},{12,8},{14,10},{16,20},{18,... | collective-permute-start | bytes 786440 | tf_op jit(solution)/shard_map/ppermute | solution.py:304
  12.1 0.1 sqrt_bitcast_fusion
  12.2 0.1 copy.14
  12.3 0.1 broadcast_in_dim.28
  12.4 0.1 copy.17
  12.5 0.1 broadcast_in_dim.30
  12.6 0.0 collective-permute-done.4.refs_6_.refs_8_.refs_12_
  12.6 4.6 %collective-permute-start.6 = (bf16[1,512,128]{2,1,0:T(8,128)(2,1)S(1)}, bf16[1,512,128]{2,1,0:T(8,128)(2,1)S(1)}, u32[]{:S(2)}, u32[]{:S(2)}) collective-permute-start(bf16[1,512,128]{2,1,0:T(8,128)(2,1)S(1)} %get-tuple-element.88), channel_id=1, source_target_pairs={{0,8},{2,10},{4,12},{6,14},{8,16},{10,18},{12,20},{14,22},{16,24},... | collective-permute-start | bytes 393224 | tf_op jit(solution)/shard_map/ppermute | solution.py:308
  17.1 1.3 %collective-permute-start.8 = (bf16[1,512,128]{2,1,0:T(8,128)(2,1)S(1)}, bf16[1,512,128]{2,1,0:T(8,128)(2,1)S(1)}, u32[]{:S(2)}, u32[]{:S(2)}) collective-permute-start(bf16[1,512,128]{2,1,0:T(8,128)(2,1)S(1)} %get-tuple-element.87), channel_id=1, source_target_pairs={{8,0},{10,2},{12,4},{14,6},{16,8},{18,10},{20,12},{22,14},{24,16},... | collective-permute-start | bytes 393224 | tf_op jit(solution)/shard_map/ppermute | solution.py:308
  18.5 0.9 %collective-permute-done.3.refs_10_.refs_9_.refs_16_ = bf16[2,512,128]{2,1,0:T(8,128)(2,1)S(1)} collective-permute-done((bf16[2,512,128]{2,1,0:T(8,128)(2,1)S(1)}, bf16[2,512,128]{2,1,0:T(8,128)(2,1)S(1)}, u32[]{:S(2)}, u32[]{:S(2)}) %collective-permute-start.3) | collective-permute-done | bytes 262176 | tf_op jit(solution)/shard_map/ppermute | solution.py:308
  19.4 3.7 %collective-permute-start.5 = (bf16[1,512,128]{2,1,0:T(8,128)(2,1)S(1)}, bf16[1,512,128]{2,1,0:T(8,128)(2,1)S(1)}, u32[]{:S(2)}, u32[]{:S(2)}) collective-permute-start(bf16[1,512,128]{2,1,0:T(8,128)(2,1)S(1)} %get-tuple-element.90), channel_id=1, source_target_pairs={{0,8},{2,10},{4,12},{6,14},{8,16},{10,18},{12,20},{14,22},{16,24},... | collective-permute-start | bytes 393224 | tf_op jit(solution)/shard_map/ppermute | solution.py:308
  23.1 1.3 %collective-permute-start.7 = (bf16[1,512,128]{2,1,0:T(8,128)(2,1)S(1)}, bf16[1,512,128]{2,1,0:T(8,128)(2,1)S(1)}, u32[]{:S(2)}, u32[]{:S(2)}) collective-permute-start(bf16[1,512,128]{2,1,0:T(8,128)(2,1)S(1)} %get-tuple-element.89), channel_id=1, source_target_pairs={{8,0},{10,2},{12,4},{14,6},{16,8},{18,10},{20,12},{22,14},{24,16},... | collective-permute-start | bytes 393224 | tf_op jit(solution)/shard_map/ppermute | solution.py:308
  24.4 0.1 bitcast_multiply_fusion
  24.5 0.1 copy.15
  24.6 0.1 broadcast_in_dim.12.refs_1_
  24.7 0.1 broadcast_in_dim.13.refs_2_
  24.9 3.8 %tables.1 = (bf16[32,128,640]{2,1,0:T(8,128)(2,1)S(1)}, f32[4,8,128]{2,1,0:T(8,128)S(1)}) custom-call(f32[4,8,128]{2,1,0:T(8,128)S(1)} %broadcast_in_dim.29.refs_0_, f32[32,16,128]{2,1,0:T(8,128)S(1)} %broadcast_in_dim.12.refs_1_, f32[32,16,128]{2,1,0:T(8,128)S(1)} %broadcast_in_dim.13.refs_2_, bf16[32,512]{1,0:T(8,128)(2,1)S(1)} %constant_dynamic-slice_fusion.refs_3_), custom_call_target="tpu_custom_call" | custom-call | tf_op jit(solution)/shard_map/tables/pallas_call | solution.py:389
  28.7 1.2 %collective-permute-done.7.refs_11_.refs_10_.refs_17_ = bf16[1,512,128]{2,1,0:T(8,128)(2,1)S(1)} collective-permute-done((bf16[1,512,128]{2,1,0:T(8,128)(2,1)S(1)}, bf16[1,512,128]{2,1,0:T(8,128)(2,1)S(1)}, u32[]{:S(2)}, u32[]{:S(2)}) %collective-permute-start.7) | collective-permute-done | bytes 131104 | tf_op jit(solution)/shard_map/ppermute | solution.py:308
  30.0 2.5 %states.1 = (bf16[4,3,128,128]{3,2,1,0:T(8,128)(2,1)S(1)}, bf16[4,3,128,128]{3,2,1,0:T(8,128)(2,1)S(1)}, f32[4,16,128]{2,1,0:T(8,128)S(1)}, f32[4,16,128]{2,1,0:...) custom-call(s32[1]{0:T(128)} %bitcast.refs_0_.q_ref, ...), custom_call_target="tpu_custom_call" | custom-call | tf_op jit(solution)/shard_map/states/pallas_call | solution.py:404
  32.4 2.6 %collective-permute-start.9 = (f32[4,16,128]{2,1,0:T(8,128)S(1)}, f32[4,16,128]{2,1,0:T(8,128)S(1)}, u32[]{:S(2)}, u32[]{:S(2)}) collective-permute-start(f32[4,16,128]{2,1,0:T(8,128)S(1)} %get-tuple-element.52), channel_id=1, source_target_pairs={{0,16},{2,18},{4,20},{6,22},{8,24},{10,26},{12,28},{14,30},{16,0},... | collective-permute-start | bytes 98312 | tf_op jit(solution)/shard_map/ppermute | solution.py:304
  35.0 5.6 %lags.1.lag_ref = f32[32,640]{1,0:T(8,128)S(1)} custom-call(s32[1]{0:T(128)} %bitcast.refs_0_.q_ref, f32[32,16,128]{2,1,0:T(8,128)S(1)} %broadcast_in_dim.12.refs_1_, f32[4,8,128]{2,1,0:T(8,128)S(1)} %get-tuple-element.45.refs_2_.refs_3_.row_ref, f32[4,8,128]{2,1,0:T(8,128)S(1)} %broadcast_in_dim.31.refs_3_.root_ref, ...), custom_call_target="tpu_custom_call" | custom-call | tf_op jit(solution)/shard_map/lags/pallas_call | solution.py:427
  40.6 2.1 %convs.2 = (bf16[2,256,128]{2,1,0:T(8,128)(2,1)S(1)}, bf16[2,256,128]{2,1,0:T(8,128)(2,1)S(1)}, bf16[2,256,128]{2,1,0:T(8,128)(2,1)S(1)}, bf16[2,256,128]{2,1,0:T(8,128)(2,1)S(1)}) custom-call(s32[1]{0:T(128)} %bitcast.refs_0_.q_ref, f32[32,16,128]{2,1,0:T(8,128)S(1)} %broadcast_in_dim.12.refs_1_, f32[32,16,128]{2,1,0:T(8,128)S(1)} %broadcast_in_dim.13.refs_2_, ...), custom_call_target="tpu_custom_call" | custom-call | tf_op jit(solution)/shard_map/convs/pallas_call | solution.py:446
  42.7 0.0 copy-start.1
  42.7 0.0 copy-start.2
  42.7 0.0 copy-start.3
  42.7 0.2 joins.1
  43.0 1.5 %collective-permute-start.13 = (f32[32,640]{1,0:T(8,128)S(1)}, f32[32,640]{1,0:T(8,128)S(1)}, u32[]{:S(2)}, u32[]{:S(2)}) collective-permute-start(f32[32,640]{1,0:T(8,128)S(1)} %joins.1), channel_id=1, source_target_pairs={{0,8},{2,10},{4,12},{6,14},{8,0},{10,2},{12,4},{14,6},{16,24},{18,... | collective-permute-start | bytes 245768 | tf_op jit(solution)/shard_map/ppermute | solution.py:304
  44.4 1.4 %collective-permute-start.11 = (bf16[2,256,128]{2,1,0:T(8,128)(2,1)S(1)}, bf16[2,256,128]{2,1,0:T(8,128)(2,1)S(1)}, u32[]{:S(2)}, u32[]{:S(2)}) collective-permute-start(bf16[2,256,128]{2,1,0:T(8,128)(2,1)S(1)} %get-tuple-element.61), channel_id=1, source_target_pairs={{0,4},{2,6},{4,0},{6,2},{8,12},{10,14},{12,8},{14,10},{16,20},{18,... | collective-permute-start | bytes 393224 | tf_op jit(solution)/shard_map/ppermute | solution.py:304
  45.8 2.0 %convs.3 = (bf16[2,256,128]{2,1,0:T(8,128)(2,1)S(1)}, bf16[2,256,128]{2,1,0:T(8,128)(2,1)S(1)}, bf16[2,256,128]{2,1,0:T(8,128)(2,1)S(1)}, bf16[2,256,128]{2,1,0:T(8,128)(2,1)S(1)}) custom-call(s32[1]{0:T(128)} %bitcast.refs_0_.q_ref, f32[32,16,128]{2,1,0:T(8,128)S(1)} %broadcast_in_dim.12.refs_1_, f32[32,16,128]{2,1,0:T(8,128)S(1)} %broadcast_in_dim.13.refs_2_, ...), custom_call_target="tpu_custom_call" | custom-call | tf_op jit(solution)/shard_map/convs/pallas_call | solution.py:446
  47.9 0.6 collective-permute-start.14
  48.4 0.9 %collective-permute-start.15 = (bf16[2,256,128]{2,1,0:T(8,128)(2,1)S(1)}, bf16[2,256,128]{2,1,0:T(8,128)(2,1)S(1)}, u32[]{:S(2)}, u32[]{:S(2)}) collective-permute-start(bf16[2,256,128]{2,1,0:T(8,128)(2,1)S(1)} %get-tuple-element.70), channel_id=1, source_target_pairs={{0,2},{2,0},{4,6},{6,4},{8,10},{10,8},{12,14},{14,12},{16,18},{18,... | collective-permute-start | bytes 393224 | tf_op jit(solution)/shard_map/ppermute | solution.py:304
  49.3 1.2 %collective-permute-start.16 = (bf16[2,256,128]{2,1,0:T(8,128)(2,1)S(1)}, bf16[2,256,128]{2,1,0:T(8,128)(2,1)S(1)}, u32[]{:S(2)}, u32[]{:S(2)}) collective-permute-start(bf16[2,256,128]{2,1,0:T(8,128)(2,1)S(1)} %get-tuple-element.71), channel_id=1, source_target_pairs={{0,4},{2,6},{4,0},{6,2},{8,12},{10,14},{12,8},{14,10},{16,20},{18,... | collective-permute-start | bytes 393224 | tf_op jit(solution)/shard_map/ppermute | solution.py:304
  50.6 2.3 %collective-permute-done.14 = bf16[32,640]{1,0:T(8,128)(2,1)S(1)} collective-permute-done((bf16[32,640]{1,0:T(8,128)(2,1)S(1)}, bf16[32,640]{1,0:T(8,128)(2,1)S(1)}, u32[]{:S(2)}, u32[]{:S(2)}) %collective-permute-start.14) | collective-permute-done | bytes 40992 | tf_op jit(solution)/shard_map/ppermute | solution.py:304
  52.8 1.1 %collective-permute-start.10 = (bf16[2,256,128]{2,1,0:T(8,128)(2,1)S(1)}, bf16[2,256,128]{2,1,0:T(8,128)(2,1)S(1)}, u32[]{:S(2)}, u32[]{:S(2)}) collective-permute-start(bf16[2,256,128]{2,1,0:T(8,128)(2,1)S(1)} %get-tuple-element.60), channel_id=1, source_target_pairs={{0,2},{2,0},{4,6},{6,4},{8,10},{10,8},{12,14},{14,12},{16,18},{18,... | collective-permute-start | bytes 393224 | tf_op jit(solution)/shard_map/ppermute | solution.py:304
  54.0 0.2 collective-permute-done.12.refs_3_
  54.2 1.0 %collective-permute-start.19 = (bf16[32,640]{1,0:T(8,128)(2,1)S(1)}, bf16[32,640]{1,0:T(8,128)(2,1)S(1)}, u32[]{:S(2)}, u32[]{:S(2)}) collective-permute-start(bf16[32,640]{1,0:T(8,128)(2,1)S(1)} %reduce-precision_convert_fusion.s0), channel_id=1, source_target_pairs={{0,4},{2,6},{4,0},{6,2},{8,12},{10,14},{12,8},{14,10},{16,20},{18,... | collective-permute-start | bytes 122888 | tf_op jit(solution)/shard_map/ppermute | solution.py:304
  55.2 0.6 collective-permute-done.16.refs_6_
  55.8 1.5 %collective-permute-start.20 = (bf16[32,640]{1,0:T(8,128)(2,1)S(1)}, bf16[32,640]{1,0:T(8,128)(2,1)S(1)}, u32[]{:S(2)}, u32[]{:S(2)}) collective-permute-start(bf16[32,640]{1,0:T(8,128)(2,1)S(1)} %reduce-precision_convert_fusion.s0), channel_id=1, source_target_pairs={{0,6},{2,4},{4,2},{6,0},{8,14},{10,12},{12,10},{14,8},{16,22},{18,... | collective-permute-start | bytes 122888 | tf_op jit(solution)/shard_map/ppermute | solution.py:304
  57.2 2.4 %collective-permute-done.17.refs_7_ = bf16[2,256,128]{2,1,0:T(8,128)(2,1)S(1)} collective-permute-done((bf16[2,256,128]{2,1,0:T(8,128)(2,1)S(1)}, bf16[2,256,128]{2,1,0:T(8,128)(2,1)S(1)}, u32[]{:S(2)}, u32[]{:S(2)}) %collective-permute-start.17) | collective-permute-done | bytes 131104 | tf_op jit(solution)/shard_map/ppermute | solution.py:304
  59.6 1.5 %gates.1 = (bf16[2048,128]{1,0:T(8,128)(2,1)}, bf16[2048,128]{1,0:T(8,128)(2,1)}, bf16[2048,128]{1,0:T(8,128)(2,1)}) custom-call(s32[1]{0:T(128)} %bitcast.refs_0_.q_ref, bf16[2,256,128]{2,1,0:T(8,128)(2,1)S(1)} %get-tuple-element.59.refs_0_, bf16[2,256,128]{2,1,0:T(8,128)(2,1)S(1)} %collective-permute-done.10.refs_1_, ...), custom_call_target="tpu_custom_call" | custom-call | tf_op jit(solution)/shard_map/gates/pallas_call | solution.py:482
  61.1 0.7 %sums.1 = (f32[128,512]{1,0:T(8,128)}, f32[16,128]{1,0:T(8,128)}) custom-call(s32[1]{0:T(128)} %bitcast.refs_0_.q_ref, bf16[32,640]{1,0:T(8,128)(2,1)S(1)} %reduce-precision_convert_fusion.s0, bf16[32,640]{1,0:T(8,128)(2,1)S(1)} %collective-permute-done.18.s1, bf16[32,640]{1,0:T(8,128)(2,1)S(1)} %collective-permute-done.19.s2, ...), custom_call_target="tpu_custom_call" | custom-call | tf_op jit(solution)/shard_map/sums/pallas_call | solution.py:490
  (36 shorter events, 0.2 us)
Async XLA Ops:
  0.6 24.0 %copy-start = (bf16[128,512]{1,0:T(8,128)(2,1)S(1)}, bf16[128,512]{1,0:T(8,128)(2,1)}, u32[]{:S(2)}) copy-start(bf16[128,512]{1,0:T(8,128)(2,1)} %param.11) | copy-start | bytes 393220
  0.6 11.5 %copy-start.4 = (f32[16,128]{1,0:T(8,128)S(1)}, f32[16,128]{1,0:T(8,128)}, u32[]{:S(2)}) copy-start(f32[16,128]{1,0:T(8,128)} %param.13) | copy-start | bytes 24580
  0.7 23.8 %copy-start.5 = (f32[16,128]{1,0:T(8,128)S(1)}, f32[16,128]{1,0:T(8,128)}, u32[]{:S(2)}) copy-start(f32[16,128]{1,0:T(8,128)} %param.12) | copy-start | bytes 24580
  2.6 3.2 %collective-permute-start = (bf16[2,512,128]{2,1,0:T(8,128)(2,1)S(1)}, bf16[2,512,128]{2,1,0:T(8,128)(2,1)S(1)}, u32[]{:S(2)}, u32[]{:S(2)}) collective-permute-start(bf16[2,512,128]{2,1,0:T(8,128)(2,1)S(1)} %pad_maximum_fusion.2), channel_id=1, source_target_pairs={{0,2},{2,0},{4,6},{6,4},{8,10},{10,8},{12,14},{14,12},{16,18},{18,... | collective-permute-start | bytes 786440 | tf_op jit(solution)/shard_map/ppermute | solution.py:304
  3.2 9.4 %collective-permute-start.4 = (bf16[2,512,128]{2,1,0:T(8,128)(2,1)S(1)}, bf16[2,512,128]{2,1,0:T(8,128)(2,1)S(1)}, u32[]{:S(2)}, u32[]{:S(2)}) collective-permute-start(bf16[2,512,128]{2,1,0:T(8,128)(2,1)S(1)} %pad_maximum_fusion.5), channel_id=1, source_target_pairs={{0,6},{2,4},{4,2},{6,0},{8,14},{10,12},{12,10},{14,8},{16,22},{18,... | collective-permute-start | bytes 786440 | tf_op jit(solution)/shard_map/ppermute | solution.py:304
  6.0 12.5 %collective-permute-start.2 = (bf16[2,512,128]{2,1,0:T(8,128)(2,1)S(1)}, bf16[2,512,128]{2,1,0:T(8,128)(2,1)S(1)}, u32[]{:S(2)}, u32[]{:S(2)}) collective-permute-start(bf16[2,512,128]{2,1,0:T(8,128)(2,1)S(1)} %get-tuple-element.95), channel_id=1, source_target_pairs={{0,8},{2,10},{4,12},{6,14},{8,16},{10,18},{12,20},{14,22},{16,24},... | collective-permute-start | bytes 786440 | tf_op jit(solution)/shard_map/ppermute | solution.py:308
  9.5 9.8 %collective-permute-start.3 = (bf16[2,512,128]{2,1,0:T(8,128)(2,1)S(1)}, bf16[2,512,128]{2,1,0:T(8,128)(2,1)S(1)}, u32[]{:S(2)}, u32[]{:S(2)}) collective-permute-start(bf16[2,512,128]{2,1,0:T(8,128)(2,1)S(1)} %get-tuple-element.94), channel_id=1, source_target_pairs={{8,0},{10,2},{12,4},{14,6},{16,8},{18,10},{20,12},{22,14},{24,16},... | collective-permute-start | bytes 786440 | tf_op jit(solution)/shard_map/ppermute | solution.py:308
  10.8 8.5 %collective-permute-start.1 = (bf16[2,512,128]{2,1,0:T(8,128)(2,1)S(1)}, bf16[2,512,128]{2,1,0:T(8,128)(2,1)S(1)}, u32[]{:S(2)}, u32[]{:S(2)}) collective-permute-start(bf16[2,512,128]{2,1,0:T(8,128)(2,1)S(1)} %pad_maximum_fusion.3), channel_id=1, source_target_pairs={{0,4},{2,6},{4,0},{6,2},{8,12},{10,14},{12,8},{14,10},{16,20},{18,... | collective-permute-start | bytes 786440 | tf_op jit(solution)/shard_map/ppermute | solution.py:304
  12.6 16.1 %collective-permute-start.6 = (bf16[1,512,128]{2,1,0:T(8,128)(2,1)S(1)}, bf16[1,512,128]{2,1,0:T(8,128)(2,1)S(1)}, u32[]{:S(2)}, u32[]{:S(2)}) collective-permute-start(bf16[1,512,128]{2,1,0:T(8,128)(2,1)S(1)} %get-tuple-element.88), channel_id=1, source_target_pairs={{0,8},{2,10},{4,12},{6,14},{8,16},{10,18},{12,20},{14,22},{16,24},... | collective-permute-start | bytes 393224 | tf_op jit(solution)/shard_map/ppermute | solution.py:308
  17.1 11.6 %collective-permute-start.8 = (bf16[1,512,128]{2,1,0:T(8,128)(2,1)S(1)}, bf16[1,512,128]{2,1,0:T(8,128)(2,1)S(1)}, u32[]{:S(2)}, u32[]{:S(2)}) collective-permute-start(bf16[1,512,128]{2,1,0:T(8,128)(2,1)S(1)} %get-tuple-element.87), channel_id=1, source_target_pairs={{8,0},{10,2},{12,4},{14,6},{16,8},{18,10},{20,12},{22,14},{24,16},... | collective-permute-start | bytes 393224 | tf_op jit(solution)/shard_map/ppermute | solution.py:308
  19.4 9.4 %collective-permute-start.5 = (bf16[1,512,128]{2,1,0:T(8,128)(2,1)S(1)}, bf16[1,512,128]{2,1,0:T(8,128)(2,1)S(1)}, u32[]{:S(2)}, u32[]{:S(2)}) collective-permute-start(bf16[1,512,128]{2,1,0:T(8,128)(2,1)S(1)} %get-tuple-element.90), channel_id=1, source_target_pairs={{0,8},{2,10},{4,12},{6,14},{8,16},{10,18},{12,20},{14,22},{16,24},... | collective-permute-start | bytes 393224 | tf_op jit(solution)/shard_map/ppermute | solution.py:308
  23.1 6.9 %collective-permute-start.7 = (bf16[1,512,128]{2,1,0:T(8,128)(2,1)S(1)}, bf16[1,512,128]{2,1,0:T(8,128)(2,1)S(1)}, u32[]{:S(2)}, u32[]{:S(2)}) collective-permute-start(bf16[1,512,128]{2,1,0:T(8,128)(2,1)S(1)} %get-tuple-element.89), channel_id=1, source_target_pairs={{8,0},{10,2},{12,4},{14,6},{16,8},{18,10},{20,12},{22,14},{24,16},... | collective-permute-start | bytes 393224 | tf_op jit(solution)/shard_map/ppermute | solution.py:308
  32.4 8.2 %collective-permute-start.9 = (f32[4,16,128]{2,1,0:T(8,128)S(1)}, f32[4,16,128]{2,1,0:T(8,128)S(1)}, u32[]{:S(2)}, u32[]{:S(2)}) collective-permute-start(f32[4,16,128]{2,1,0:T(8,128)S(1)} %get-tuple-element.52), channel_id=1, source_target_pairs={{0,16},{2,18},{4,20},{6,22},{8,24},{10,26},{12,28},{14,30},{16,0},... | collective-permute-start | bytes 98312 | tf_op jit(solution)/shard_map/ppermute | solution.py:304
  42.7 16.9 %copy-start.1 = (bf16[2048,128]{1,0:T(8,128)(2,1)S(1)}, bf16[2048,128]{1,0:T(8,128)(2,1)}, u32[]{:S(2)}) copy-start(bf16[2048,128]{1,0:T(8,128)(2,1)} %refs_9_.1) | copy-start | bytes 1572868
  42.7 16.9 %copy-start.2 = (bf16[2048,128]{1,0:T(8,128)(2,1)S(1)}, bf16[2048,128]{1,0:T(8,128)(2,1)}, u32[]{:S(2)}) copy-start(bf16[2048,128]{1,0:T(8,128)(2,1)} %refs_10_.1) | copy-start | bytes 1572868
  42.7 16.9 %copy-start.3 = (bf16[2048,128]{1,0:T(8,128)(2,1)S(1)}, bf16[2048,128]{1,0:T(8,128)(2,1)}, u32[]{:S(2)}) copy-start(bf16[2048,128]{1,0:T(8,128)(2,1)} %refs_8_.1) | copy-start | bytes 1572868
  43.0 4.9 %collective-permute-start.13 = (f32[32,640]{1,0:T(8,128)S(1)}, f32[32,640]{1,0:T(8,128)S(1)}, u32[]{:S(2)}, u32[]{:S(2)}) collective-permute-start(f32[32,640]{1,0:T(8,128)S(1)} %joins.1), channel_id=1, source_target_pairs={{0,8},{2,10},{4,12},{6,14},{8,0},{10,2},{12,4},{14,6},{16,24},{18,... | collective-permute-start | bytes 245768 | tf_op jit(solution)/shard_map/ppermute | solution.py:304
  44.4 8.4 %collective-permute-start.11 = (bf16[2,256,128]{2,1,0:T(8,128)(2,1)S(1)}, bf16[2,256,128]{2,1,0:T(8,128)(2,1)S(1)}, u32[]{:S(2)}, u32[]{:S(2)}) collective-permute-start(bf16[2,256,128]{2,1,0:T(8,128)(2,1)S(1)} %get-tuple-element.61), channel_id=1, source_target_pairs={{0,4},{2,6},{4,0},{6,2},{8,12},{10,14},{12,8},{14,10},{16,20},{18,... | collective-permute-start | bytes 393224 | tf_op jit(solution)/shard_map/ppermute | solution.py:304
  47.9 5.0 %collective-permute-start.14 = (bf16[32,640]{1,0:T(8,128)(2,1)S(1)}, bf16[32,640]{1,0:T(8,128)(2,1)S(1)}, u32[]{:S(2)}, u32[]{:S(2)}) collective-permute-start(bf16[32,640]{1,0:T(8,128)(2,1)S(1)} %reduce-precision_convert_fusion.1), channel_id=1, source_target_pairs={{0,16},{2,18},{4,20},{6,22},{8,24},{10,26},{12,28},{14,30},{16,0},... | collective-permute-start | bytes 122888 | tf_op jit(solution)/shard_map/ppermute | solution.py:304
  48.4 5.7 %collective-permute-start.12 = (bf16[2,256,128]{2,1,0:T(8,128)(2,1)S(1)}, bf16[2,256,128]{2,1,0:T(8,128)(2,1)S(1)}, u32[]{:S(2)}, u32[]{:S(2)}) collective-permute-start(bf16[2,256,128]{2,1,0:T(8,128)(2,1)S(1)} %get-tuple-element.62), channel_id=1, source_target_pairs={{0,6},{2,4},{4,2},{6,0},{8,14},{10,12},{12,10},{14,8},{16,22},{18,... | collective-permute-start | bytes 393224 | tf_op jit(solution)/shard_map/ppermute | solution.py:304
  48.4 5.7 %collective-permute-start.15 = (bf16[2,256,128]{2,1,0:T(8,128)(2,1)S(1)}, bf16[2,256,128]{2,1,0:T(8,128)(2,1)S(1)}, u32[]{:S(2)}, u32[]{:S(2)}) collective-permute-start(bf16[2,256,128]{2,1,0:T(8,128)(2,1)S(1)} %get-tuple-element.70), channel_id=1, source_target_pairs={{0,2},{2,0},{4,6},{6,4},{8,10},{10,8},{12,14},{14,12},{16,18},{18,... | collective-permute-start | bytes 393224 | tf_op jit(solution)/shard_map/ppermute | solution.py:304
  49.3 6.4 %collective-permute-start.16 = (bf16[2,256,128]{2,1,0:T(8,128)(2,1)S(1)}, bf16[2,256,128]{2,1,0:T(8,128)(2,1)S(1)}, u32[]{:S(2)}, u32[]{:S(2)}) collective-permute-start(bf16[2,256,128]{2,1,0:T(8,128)(2,1)S(1)} %get-tuple-element.71), channel_id=1, source_target_pairs={{0,4},{2,6},{4,0},{6,2},{8,12},{10,14},{12,8},{14,10},{16,20},{18,... | collective-permute-start | bytes 393224 | tf_op jit(solution)/shard_map/ppermute | solution.py:304
  52.8 6.8 %collective-permute-start.17 = (bf16[2,256,128]{2,1,0:T(8,128)(2,1)S(1)}, bf16[2,256,128]{2,1,0:T(8,128)(2,1)S(1)}, u32[]{:S(2)}, u32[]{:S(2)}) collective-permute-start(bf16[2,256,128]{2,1,0:T(8,128)(2,1)S(1)} %get-tuple-element.72), channel_id=1, source_target_pairs={{0,6},{2,4},{4,2},{6,0},{8,14},{10,12},{12,10},{14,8},{16,22},{18,... | collective-permute-start | bytes 393224 | tf_op jit(solution)/shard_map/ppermute | solution.py:304
  52.8 6.8 %collective-permute-start.10 = (bf16[2,256,128]{2,1,0:T(8,128)(2,1)S(1)}, bf16[2,256,128]{2,1,0:T(8,128)(2,1)S(1)}, u32[]{:S(2)}, u32[]{:S(2)}) collective-permute-start(bf16[2,256,128]{2,1,0:T(8,128)(2,1)S(1)} %get-tuple-element.60), channel_id=1, source_target_pairs={{0,2},{2,0},{4,6},{6,4},{8,10},{10,8},{12,14},{14,12},{16,18},{18,... | collective-permute-start | bytes 393224 | tf_op jit(solution)/shard_map/ppermute | solution.py:304
  54.2 7.0 %collective-permute-start.18 = (bf16[32,640]{1,0:T(8,128)(2,1)S(1)}, bf16[32,640]{1,0:T(8,128)(2,1)S(1)}, u32[]{:S(2)}, u32[]{:S(2)}) collective-permute-start(bf16[32,640]{1,0:T(8,128)(2,1)S(1)} %reduce-precision_convert_fusion.s0), channel_id=1, source_target_pairs={{0,2},{2,0},{4,6},{6,4},{8,10},{10,8},{12,14},{14,12},{16,18},{18,... | collective-permute-start | bytes 122888 | tf_op jit(solution)/shard_map/ppermute | solution.py:304
  54.2 7.0 %collective-permute-start.19 = (bf16[32,640]{1,0:T(8,128)(2,1)S(1)}, bf16[32,640]{1,0:T(8,128)(2,1)S(1)}, u32[]{:S(2)}, u32[]{:S(2)}) collective-permute-start(bf16[32,640]{1,0:T(8,128)(2,1)S(1)} %reduce-precision_convert_fusion.s0), channel_id=1, source_target_pairs={{0,4},{2,6},{4,0},{6,2},{8,12},{10,14},{12,8},{14,10},{16,20},{18,... | collective-permute-start | bytes 122888 | tf_op jit(solution)/shard_map/ppermute | solution.py:304
  55.8 5.4 %collective-permute-start.20 = (bf16[32,640]{1,0:T(8,128)(2,1)S(1)}, bf16[32,640]{1,0:T(8,128)(2,1)S(1)}, u32[]{:S(2)}, u32[]{:S(2)}) collective-permute-start(bf16[32,640]{1,0:T(8,128)(2,1)S(1)} %reduce-precision_convert_fusion.s0), channel_id=1, source_target_pairs={{0,6},{2,4},{4,2},{6,0},{8,14},{10,12},{12,10},{14,8},{16,22},{18,... | collective-permute-start | bytes 122888 | tf_op jit(solution)/shard_map/ppermute | solution.py:304
